TPU v7x, 32 devices: a whole 2x2x4 slice. The times are simulated.
32 devices in a mesh: tile: 8 (over y, x, core), member: 4 (over z).
Axes of the slice: x: 2, y: 2, z: 4, core: 2. Of those that a mesh axis runs over, the one named last changes fastest.
Arguments:
- hx: bfloat16 [512, 32768], P('member', 'tile'), may hold values from -6 to 6
- obs_value: bfloat16 [32768], P('tile'), may hold values from -8 to 8
- obs_rinv: bfloat16 [32768], P('tile'), may hold values from 0.29882812 to 4
- obs_index: int32 [32, 1024], P('tile'), may hold values from 512 to 5631, as said below
- loc_weight: float32 [32, 1024], P(('tile', 'member')), may hold values from 0.05 to 1
- state: bfloat16 [512, 131072], P('member', 'tile'), may hold values from -6 to 6
Outputs:
- analysis: bfloat16 [512, 131072], P('member', 'tile')
Inputs may be any that keep to these rules, and one draw needn't show every extreme that they name: `obs_index`: row p lists 1024 distinct positions in the pool of tile p // 4: positions 0 .. 1023 are the last 1024 observations of the tile before it, the next 4096 the tile's own, the last 1024 the first observations of the tile after it; the tiles form a closed band. All positions of a row lie within 2048 consecutive positions.
All inputs are finite; a program needn't handle non-finite values.
Results may differ from a plain program's by a relative error of at most 0.012.
The roundings to bfloat16 on the way count: a program that leaves them out, or rounds other values in their place, can miss the bound.
Values may be sent and summed in bfloat16 or wider, within the bound.
No kernel may reach another device: no remote copies, remote signals or barrier semaphores. Data moves between devices by JAX's collectives and lax.ppermute only.
A program may use at most 64 MiB of HBM per device.

v0:
```python
import functools

import jax
import jax.numpy as jnp
from jax import lax
from jax.experimental import pallas as pl
from jax.experimental.pallas import tpu as pltpu
from jax.sharding import PartitionSpec as P


LOC = 1024
NS_ITERS = 3
LANES = 128
WINDOW = 2 * LOC
CHUNKS = 2
BLOCK = 512


def partners(count, step):
    return [(i, i ^ step) for i in range(count)]


def swap(block, step):
    return lax.ppermute(block, "member", partners(lax.axis_size("member"), step))


def cut_kernel(first, pos_ref, state_ref, out_ref, sem):
    width = out_ref.shape[1]
    start = pl.multiple_of(first(pos_ref[0]) * width, LANES)
    copy = pltpu.make_async_copy(state_ref.at[:, pl.ds(start, width)], out_ref, sem)
    copy.start()
    copy.wait()


def cut(position, state, step, chunk, count):
    rows, total = state.shape
    width = total // (count * CHUNKS)
    return pl.pallas_call(
        functools.partial(cut_kernel, lambda pos: (pos ^ step) * CHUNKS + chunk),
        in_specs=[
            pl.BlockSpec(memory_space=pltpu.SMEM),
            pl.BlockSpec(memory_space=pl.ANY),
        ],
        out_specs=pl.BlockSpec(memory_space=pltpu.VMEM),
        scratch_shapes=[pltpu.SemaphoreType.DMA],
        out_shape=jax.ShapeDtypeStruct((rows, width), state.dtype),
        cost_estimate=pl.CostEstimate(
            flops=0, transcendentals=0, bytes_accessed=2 * rows * width
        ),
    )(position, state)


def pick_kernel(pos_ref, start_ref, index_ref, own_ref, low_ref, high_ref, out_ref, pair_ref, pool):
    step = pl.program_id(0)
    own = own_ref.shape[1]
    span = WINDOW + LANES

    @pl.when(step == 0)
    def _():
        pool[:, :LOC] = low_ref[...]
        pool[:, LOC : LOC + own] = own_ref[...]
        pool[:, LOC + own :] = high_ref[...]

    start = pl.multiple_of(start_ref[pos_ref[0] ^ step], LANES)
    relative = index_ref[0] - start
    window = pool[:, pl.ds(start, span)]
    half = LOC // 4
    for part in range(4):
        where = relative[:, part * half : (part + 1) * half]
        hot = lax.broadcasted_iota(jnp.int32, (span, half), 0) == where
        hot = jnp.where(hot, 1.0, 0.0).astype(jnp.bfloat16)
        picked = jnp.dot(window, hot, preferred_element_type=jnp.float32)
        picked = picked.astype(jnp.bfloat16)
        out_ref[0, :, part * half : (part + 1) * half] = picked[: out_ref.shape[1]]

        @pl.when(step == 0)
        def _():
            pair_ref[:, part * half : (part + 1) * half] = picked[out_ref.shape[1] :]


def pick(position, starts, index, own, low, high, members):
    count = index.shape[0]
    rows, width = own.shape
    whole = lambda shape: pl.BlockSpec(shape, lambda i, pos, start: (0,) * len(shape))
    return pl.pallas_call(
        pick_kernel,
        grid_spec=pltpu.PrefetchScalarGridSpec(
            num_scalar_prefetch=2,
            grid=(count,),
            in_specs=[
                pl.BlockSpec((1, 1, LOC), lambda i, pos, start: (pos[0] ^ i, 0, 0)),
                whole(own.shape),
                whole(low.shape),
                whole(high.shape),
            ],
            out_specs=[
                pl.BlockSpec((1, members, LOC), lambda i, pos, start: (i, 0, 0)),
                whole((rows - members, LOC)),
            ],
            scratch_shapes=[pltpu.VMEM((rows, width + 2 * LOC), jnp.bfloat16)],
        ),
        compiler_params=pltpu.CompilerParams(vmem_limit_bytes=20 << 20),
        out_shape=[
            jax.ShapeDtypeStruct((count, members, LOC), jnp.bfloat16),
            jax.ShapeDtypeStruct((rows - members, LOC), jnp.bfloat16),
        ],
        cost_estimate=pl.CostEstimate(
            flops=2 * count * rows * (WINDOW + LANES) * LOC,
            transcendentals=0,
            bytes_accessed=2 * rows * width + 2 * count * rows * LOC,
        ),
    )(position, starts, index.reshape(count, 1, LOC), own, low, high)


def update_kernel(count, aliased, pos_ref, transform_ref, *refs):
    blocks = refs[:count]
    outs = refs[count + aliased : 2 * count + aliased]
    pert = refs[-1]
    rows = blocks[0].shape[0]
    values = [block[...].astype(jnp.float32) for block in blocks]
    total = jnp.sum(values[0], axis=0, keepdims=True)
    for value in values[1:]:
        total += jnp.sum(value, axis=0, keepdims=True)
    mean = total / (count * rows)
    for k, value in enumerate(values):
        pert[k * rows : (k + 1) * rows, :] = (value - mean).astype(jnp.bfloat16)
    combined = jnp.dot(transform_ref[...], pert[...], preferred_element_type=jnp.float32)
    result = (mean + combined).astype(jnp.bfloat16)
    for k in range(count):
        outs[k][...] = result[k * rows : (k + 1) * rows]


def update_state(position, transform, state, received, chunk, buffer):
    rows, total = state.shape
    count = len(received) + 1
    members = transform.shape[0]
    width = received[0].shape[1]
    block = min(BLOCK, width)
    per = width // block
    own = pl.BlockSpec((rows, block), lambda i, pos: (0, (pos[0] * CHUNKS + chunk) * per + i))
    plain = pl.BlockSpec((rows, block), lambda i, pos: (0, i))
    aliased = 0 if buffer is None else 1
    extra = [] if buffer is None else [pl.BlockSpec(memory_space=pl.ANY)]
    return pl.pallas_call(
        functools.partial(update_kernel, count, aliased),
        grid_spec=pltpu.PrefetchScalarGridSpec(
            num_scalar_prefetch=1,
            grid=(per,),
            in_specs=[pl.BlockSpec((members, members), lambda i, pos: (0, 0)), own]
            + [plain] * (count - 1)
            + extra,
            out_specs=[own] + [plain] * (count - 1),
            scratch_shapes=[pltpu.VMEM((members, block), jnp.bfloat16)],
        ),
        out_shape=[jax.ShapeDtypeStruct((rows, total), state.dtype)]
        + [jax.ShapeDtypeStruct((rows, width), state.dtype)] * (count - 1),
        input_output_aliases={} if buffer is None else {2 + count: 0},
        compiler_params=pltpu.CompilerParams(vmem_limit_bytes=16 << 20),
        cost_estimate=pl.CostEstimate(
            flops=2 * members * members * width,
            transcendentals=0,
            bytes_accessed=4 * members * width + 2 * members * members,
        ),
    )(position, transform, state, *received, *([] if buffer is None else [buffer]))


def place_kernel(first, pos_ref, piece_ref, buffer_ref, out_ref, sem):
    width = piece_ref.shape[1]
    start = pl.multiple_of(first(pos_ref[0]) * width, LANES)
    copy = pltpu.make_async_copy(piece_ref, out_ref.at[:, pl.ds(start, width)], sem)
    copy.start()
    copy.wait()


def place(position, buffer, piece, step, chunk):
    rows, width = piece.shape
    return pl.pallas_call(
        functools.partial(place_kernel, lambda pos: (pos ^ step) * CHUNKS + chunk),
        in_specs=[
            pl.BlockSpec(memory_space=pltpu.SMEM),
            pl.BlockSpec(memory_space=pl.ANY),
            pl.BlockSpec(memory_space=pl.ANY),
        ],
        out_specs=pl.BlockSpec(memory_space=pl.ANY),
        scratch_shapes=[pltpu.SemaphoreType.DMA],
        compiler_params=pltpu.CompilerParams(vmem_limit_bytes=1 << 20),
        out_shape=jax.ShapeDtypeStruct(buffer.shape, buffer.dtype),
        input_output_aliases={2: 0},
        cost_estimate=pl.CostEstimate(
            flops=0, transcendentals=0, bytes_accessed=2 * rows * width
        ),
    )(position, piece, buffer)


def product(left, right, dims):
    return lax.dot_general(left, right, (dims, ((), ())), preferred_element_type=jnp.float32)


def analysis(obs_block, obs_pair, loc_row):
    members = obs_block.shape[0]
    block_f = obs_block.astype(jnp.float32)
    obs_mean = jnp.mean(block_f, axis=0)
    obs_root = jnp.sqrt(obs_pair[1].astype(jnp.float32) * loc_row)
    scaled = ((block_f - obs_mean) * obs_root).astype(jnp.bfloat16)
    innovation = (obs_pair[0].astype(jnp.float32) - obs_mean) * obs_root
    gram_matrix = product(scaled, scaled, ((1,), (1,)))
    identity = jnp.eye(members, dtype=jnp.float32)
    system = gram_matrix + (members - 1.0) * identity
    projection = jnp.dot(scaled.astype(jnp.float32), innovation, precision=lax.Precision.HIGHEST)
    norm_a = jnp.sqrt(jnp.sum(system * system))
    upper_iter = system / norm_a
    lower_iter = identity
    for sweep in range(NS_ITERS):
        upper_b = upper_iter.astype(jnp.bfloat16)
        lower_b = lower_iter.astype(jnp.bfloat16)
        half_step = (1.5 * identity - 0.5 * product(lower_b, upper_b, ((1,), (0,)))).astype(
            jnp.bfloat16
        )
        if sweep + 1 < NS_ITERS:
            upper_iter = product(upper_b, half_step, ((1,), (0,)))
        lower_iter = product(half_step, lower_b, ((1,), (0,)))
    invroot = lower_iter / jnp.sqrt(norm_a)
    inner_w = jnp.dot(invroot, projection, precision=lax.Precision.HIGHEST)
    mean_w = jnp.dot(invroot, inner_w, precision=lax.Precision.HIGHEST)
    transform = jnp.sqrt(members - 1.0) * invroot + mean_w[:, None]
    return transform.astype(jnp.bfloat16).T


def shift_tiles(block, step):
    count = lax.axis_size("tile")
    return lax.ppermute(block, "tile", [(i, (i + step) % count) for i in range(count)])


def send_order(count):
    return [count - 1, *range(1, count - 1)]


def on_device(hx, obs_value, obs_rinv, obs_index, loc_weight, state):
    rows = hx.shape[0]
    count = lax.axis_size("member")
    position = lax.axis_index("member").astype(jnp.int32).reshape(1)
    steps = send_order(count)

    def send_chunk(chunk):
        return {step: swap(cut(position, state, step, chunk, count), step) for step in steps}

    arrived = [send_chunk(0)]

    pad = jnp.zeros((14, hx.shape[1]), hx.dtype)
    stacked = jnp.concatenate([hx, obs_value[None], obs_rinv[None], pad], axis=0)
    low = shift_tiles(stacked[:, -LOC:], 1)
    high = shift_tiles(stacked[:, :LOC], -1)
    limit = hx.shape[1] - WINDOW + 2 * LOC - LANES
    starts = jnp.minimum(jnp.min(obs_index, axis=1) // LANES * LANES, limit)
    picked, obs_pair = pick(position, starts, obs_index, stacked, low, high, rows)
    others = {step: swap(picked[step], step) for step in steps}
    obs_block = jnp.concatenate([picked[0]] + [others[s] for s in range(1, count)], axis=0)

    for chunk in range(1, CHUNKS):
        arrived.append(send_chunk(chunk))

    transform = analysis(obs_block, obs_pair, loc_weight[0])

    buffer, returned = None, []
    for chunk in range(CHUNKS):
        received = [arrived[chunk][step] for step in range(1, count)]
        buffer, *others = update_state(position, transform, state, received, chunk, buffer)
        returned.append({step: swap(others[step - 1], step) for step in steps})
    for chunk in range(CHUNKS):
        for step in steps:
            buffer = place(position, buffer, returned[chunk][step], step, chunk)
    return buffer


def solution(mesh):
    in_specs = (
        P("member", "tile"),
        P("tile"),
        P("tile"),
        P("tile", None),
        P(("tile", "member"), None),
        P("member", "tile"),
    )
    out_specs = P("member", "tile")
    return jax.shard_map(
        on_device, mesh=mesh, in_specs=in_specs, out_specs=out_specs, check_vma=False
    )
```

profile of v0, /device:TPU:0, one launch (start us, length us, event | category | flops | bytes accessed | tf_op | source)
XLA Modules:
  0.0 220.8 jit_solution(3099121129909774328)
XLA Ops:
  0.0 0.7 broadcast_in_dim.12
  0.7 0.7 broadcast_in_dim.13
  1.4 0.1 pad.7.clone
  1.5 1.5 maximum_maximum_fusion.own_ref
  3.1 3.4 %collective-permute-start.1 = (bf16[144,1024]{1,0:T(8,128)(2,1)S(1)}, bf16[144,1024]{1,0:T(8,128)(2,1)S(1)}, u32[]{:S(2)}, u32[]{:S(2)}) collective-permute-start(bf16[144,1024]{1,0:T(8,128)(2,1)S(1)} %get-tuple-element.25), channel_id=1, source_target_pairs={{0,28},{4,0},{8,4},{12,8},{16,12},{20,16},{24,20},{28,24},{1,29},{... | collective-permute-start | bytes 884744 | tf_op jit(solution)/shard_map/ppermute | solution.py:231
  6.5 1.9 shard_map.65
  8.4 1.6 collective-permute-start.5
  10.0 1.9 shard_map.66
  11.9 2.7 %collective-permute-start.6 = (bf16[128,2048]{1,0:T(8,128)(2,1)}, bf16[128,2048]{1,0:T(8,128)(2,1)S(1)}, u32[]{:S(2)}, u32[]{:S(2)}) collective-permute-start(bf16[128,2048]{1,0:T(8,128)(2,1)} %shard_map.66), channel_id=1, source_target_pairs={{0,2},{1,3},{2,0},{3,1},{4,6},{5,7},{6,4},{7,5},{8,10},{9,11},{10,... | collective-permute-start | bytes 1572872 | tf_op jit(solution)/shard_map/ppermute | solution.py:24
  14.5 1.8 shard_map.70
  16.4 1.9 shard_map.69
  18.2 1.9 shard_map.68
  20.1 0.0 copy-start.10
  20.1 1.9 shard_map.67
  22.0 0.1 reduce_min.9
  22.2 0.0 collective-permute-done.low_ref
  22.2 8.6 %shard_map.64 = (bf16[4,128,1024]{2,1,0:T(8,128)(2,1)S(1)}, bf16[16,1024]{1,0:T(8,128)(2,1)S(1)}) custom-call(s32[1]{0:T(128)} %bitcast.pos_ref, s32[4]{0:T(128)S(1)} %multiply_minimum_fusion.start_ref, s32[4,1,1024]{2,1,0:T(1,128)S(1)} %reshape.16.index_ref, bf16[144,4096]{1,0:T(8,128)(2,1)S(1)} %maximum_maximum_fusion.own_ref, ...), custom_call_target="tpu_custom_call" | custom-call | flops 2566914048 | bytes 2359296 | tf_op jit(solution)/shard_map/pallas_call | solution.py:85
  30.8 0.0 copy-start.11
  30.8 0.0 copy-start.2
  30.8 0.1 slice_bitcast_fusion.3
  30.9 0.3 collective-permute-start.4
  31.2 1.7 collective-permute-start.3
  32.9 2.5 %collective-permute-start.2 = (bf16[128,1024]{1,0:T(8,128)(2,1)S(1)}, bf16[128,1024]{1,0:T(8,128)(2,1)S(1)}, u32[]{:S(2)}, u32[]{:S(2)}) collective-permute-start(bf16[128,1024]{1,0:T(8,128)(2,1)S(1)} %get-tuple-element.30), channel_id=1, source_target_pairs={{0,1},{1,0},{2,3},{3,2},{4,5},{5,4},{6,7},{7,6},{8,9},{9,8},{10,11... | collective-permute-start | bytes 786440 | tf_op jit(solution)/shard_map/ppermute | solution.py:24
  35.4 6.9 %collective-permute-done.4 = bf16[128,1024]{1,0:T(8,128)(2,1)S(1)} collective-permute-done((bf16[128,1024]{1,0:T(8,128)(2,1)S(1)}, bf16[128,1024]{1,0:T(8,128)(2,1)S(1)}, u32[]{:S(2)}, u32[]{:S(2)}) %collective-permute-start.4) | collective-permute-done | bytes 262176 | tf_op jit(solution)/shard_map/ppermute | solution.py:24
  42.3 14.3 %collective-permute-start.8 = (bf16[128,2048]{1,0:T(8,128)(2,1)}, bf16[128,2048]{1,0:T(8,128)(2,1)S(1)}, u32[]{:S(2)}, u32[]{:S(2)}) collective-permute-start(bf16[128,2048]{1,0:T(8,128)(2,1)} %shard_map.68), channel_id=1, source_target_pairs={{0,1},{1,0},{2,3},{3,2},{4,5},{5,4},{6,7},{7,6},{8,9},{9,8},{10,11... | collective-permute-start | bytes 1572872 | tf_op jit(solution)/shard_map/ppermute | solution.py:24
  56.5 3.7 %collective-permute-done.3 = bf16[128,1024]{1,0:T(8,128)(2,1)S(1)} collective-permute-done((bf16[128,1024]{1,0:T(8,128)(2,1)S(1)}, bf16[128,1024]{1,0:T(8,128)(2,1)S(1)}, u32[]{:S(2)}, u32[]{:S(2)}) %collective-permute-start.3) | collective-permute-done | bytes 262176 | tf_op jit(solution)/shard_map/ppermute | solution.py:24
  60.3 0.0 collective-permute-done.2
  60.3 2.5 %collective-permute-start.10 = (bf16[128,2048]{1,0:T(8,128)(2,1)S(1)}, bf16[128,2048]{1,0:T(8,128)(2,1)S(1)}, u32[]{:S(2)}, u32[]{:S(2)}) collective-permute-start(bf16[128,2048]{1,0:T(8,128)(2,1)S(1)} %copy-done.2), channel_id=1, source_target_pairs={{0,3},{1,2},{2,1},{3,0},{4,7},{5,6},{6,5},{7,4},{8,11},{9,10},{10,... | collective-permute-start | bytes 1572872 | tf_op jit(solution)/shard_map/ppermute | solution.py:24
  62.8 0.2 convert_reduce_fusion
  63.0 2.4 %multiply_reduce_fusion = (f32[]{:T(128)}, f32[512,512]{1,0:T(8,128)}) fusion(f32[1024]{0:T(1024)S(1)} %bitcast.38, f32[1024]{0:T(1024)S(1)} %get-tuple-element.32, bf16[128,1024]{1,0:T(8,128)(2,1)S(1)} %collective-permute-done.4, bf16[128,1024]{1,0:T(8,128)(2,1)S(1)} %collective-permute-done.3, bf16[128,1024]{1,0:T(8,128)(2,1)S(1)} %collective-permute-done.2, ...), kind=kOutput, calls=%fused_computation.25 | convolution fusion | flops 543948800 | bytes 2105348 | tf_op jit(solution)/shard_map/dot_general | solution.py:196
  66.2 0.0 copy-start.13
  66.2 1.8 fusion.2
  68.0 0.4 convolution_convert_fusion.2
  68.5 0.4 convolution_convert_fusion.3
  68.9 0.4 fusion.3
  69.4 0.8 copy-done.3
  70.2 1.2 convolution_convert_fusion.1
  71.4 2.9 %fusion.4 = bf16[512,512]{1,0:T(8,128)(2,1)} fusion(bf16[512,512]{1,0:T(8,128)(2,1)} %convolution_convert_fusion.1, bf16[512,512]{1,0:T(8,128)(2,1)} %copy-done.12, bf16[512,512]{1,0:T(8,128)(2,1)} %copy-done.3), kind=kOutput, calls=%fused_computation.18 | convolution fusion | flops 538443776 | bytes 2097152 | tf_op jit(solution)/shard_map/dot_general | solution.py:196
  74.3 1.8 convolution_divide_fusion
  76.1 0.0 copy-start
  76.1 0.9 convolution_bitcast_fusion.1
  77.1 0.7 convolution_bitcast_fusion
  77.7 0.7 fusion.9
  78.4 0.0 collective-permute-done.8.refs_1_
  78.4 0.1 copy-done.1
  78.4 1.4 collective-permute-start.7
  79.8 0.1 fusion.7.transform_ref
  79.9 29.8 %collective-permute-done.9.refs_2_ = bf16[128,2048]{1,0:T(8,128)(2,1)S(1)} collective-permute-done((bf16[128,2048]{1,0:T(8,128)(2,1)}, bf16[128,2048]{1,0:T(8,128)(2,1)S(1)}, u32[]{:S(2)}, u32[]{:S(2)}) %collective-permute-start.9) | collective-permute-done | bytes 524320 | tf_op jit(solution)/shard_map/ppermute | solution.py:24
  109.7 0.0 collective-permute-done.10.refs_3_
  109.7 3.2 %shard_map.71 = (bf16[128,16384]{1,0:T(8,128)(2,1)}, bf16[128,2048]{1,0:T(8,128)(2,1)S(1)}, bf16[128,2048]{1,0:T(8,128)(2,1)S(1)}, bf16[128,2048]{1,0:T(8,128)(2,1)S(1)}) custom-call(s32[1]{0:T(128)} %bitcast.pos_ref, bf16[512,512]{1,0:T(8,128)(2,1)S(1)} %fusion.7.transform_ref, bf16[128,16384]{1,0:T(8,128)(2,1)S(1)} %copy-done, ...), custom_call_target="tpu_custom_call" | custom-call | flops 1073741824 | bytes 4718592 | tf_op jit(solution)/shard_map/pallas_call | solution.py:144
  112.9 1.9 collective-permute-start.16
  114.8 22.6 %collective-permute-start.14 = (bf16[128,2048]{1,0:T(8,128)(2,1)S(1)}, bf16[128,2048]{1,0:T(8,128)(2,1)S(1)}, u32[]{:S(2)}, u32[]{:S(2)}) collective-permute-start(bf16[128,2048]{1,0:T(8,128)(2,1)S(1)} %get-tuple-element.21), channel_id=1, source_target_pairs={{0,2},{1,3},{2,0},{3,1},{4,6},{5,7},{6,4},{7,5},{8,10},{9,11},{10,... | collective-permute-start | bytes 1572872 | tf_op jit(solution)/shard_map/ppermute | solution.py:24
  137.4 3.2 %shard_map.72 = (bf16[128,16384]{1,0:T(8,128)(2,1)}, bf16[128,2048]{1,0:T(8,128)(2,1)S(1)}, bf16[128,2048]{1,0:T(8,128)(2,1)S(1)}, bf16[128,2048]{1,0:T(8,128)(2,1)S(1)}) custom-call(s32[1]{0:T(128)} %bitcast.pos_ref, bf16[512,512]{1,0:T(8,128)(2,1)S(1)} %fusion.7.transform_ref, bf16[128,16384]{1,0:T(8,128)(2,1)S(1)} %copy-done, ...), custom_call_target="tpu_custom_call", output_to_operand_aliasing={{0}: (6, {})} | custom-call | flops 1073741824 | bytes 4718592 | tf_op jit(solution)/shard_map/pallas_call | solution.py:144
  140.6 1.9 collective-permute-start.13
  142.5 18.3 %collective-permute-start.12 = (bf16[128,2048]{1,0:T(8,128)(2,1)S(1)}, bf16[128,2048]{1,0:T(8,128)(2,1)S(1)}, u32[]{:S(2)}, u32[]{:S(2)}) collective-permute-start(bf16[128,2048]{1,0:T(8,128)(2,1)S(1)} %get-tuple-element.19), channel_id=1, source_target_pairs={{0,1},{1,0},{2,3},{3,2},{4,5},{5,4},{6,7},{7,6},{8,9},{9,8},{10,11... | collective-permute-start | bytes 1572872 | tf_op jit(solution)/shard_map/ppermute | solution.py:24
  160.8 17.6 %collective-permute-start.11 = (bf16[128,2048]{1,0:T(8,128)(2,1)S(1)}, bf16[128,2048]{1,0:T(8,128)(2,1)S(1)}, u32[]{:S(2)}, u32[]{:S(2)}) collective-permute-start(bf16[128,2048]{1,0:T(8,128)(2,1)S(1)} %get-tuple-element.18), channel_id=1, source_target_pairs={{0,2},{1,3},{2,0},{3,1},{4,6},{5,7},{6,4},{7,5},{8,10},{9,11},{10,... | collective-permute-start | bytes 1572872 | tf_op jit(solution)/shard_map/ppermute | solution.py:24
  178.4 0.8 shard_map.73.buffer_ref
  179.2 0.8 shard_map.74.buffer_ref
  180.0 19.6 %collective-permute-done.14.piece_ref = bf16[128,2048]{1,0:T(8,128)(2,1)S(1)} collective-permute-done((bf16[128,2048]{1,0:T(8,128)(2,1)S(1)}, bf16[128,2048]{1,0:T(8,128)(2,1)S(1)}, u32[]{:S(2)}, u32[]{:S(2)}) %collective-permute-start.14) | collective-permute-done | bytes 524320 | tf_op jit(solution)/shard_map/ppermute | solution.py:24
  199.6 0.8 shard_map.75.buffer_ref
  200.4 0.8 shard_map.76.buffer_ref
  201.2 0.8 shard_map.77.buffer_ref
  202.1 17.9 %collective-permute-done.11.piece_ref = bf16[128,2048]{1,0:T(8,128)(2,1)S(1)} collective-permute-done((bf16[128,2048]{1,0:T(8,128)(2,1)S(1)}, bf16[128,2048]{1,0:T(8,128)(2,1)S(1)}, u32[]{:S(2)}, u32[]{:S(2)}) %collective-permute-start.11) | collective-permute-done | bytes 524320 | tf_op jit(solution)/shard_map/ppermute | solution.py:24
  220.0 0.8 shard_map.78
  (39 shorter events, 0.2 us)
Async XLA Ops:
  3.1 19.1 %collective-permute-start.1 = (bf16[144,1024]{1,0:T(8,128)(2,1)S(1)}, bf16[144,1024]{1,0:T(8,128)(2,1)S(1)}, u32[]{:S(2)}, u32[]{:S(2)}) collective-permute-start(bf16[144,1024]{1,0:T(8,128)(2,1)S(1)} %get-tuple-element.25), channel_id=1, source_target_pairs={{0,28},{4,0},{8,4},{12,8},{16,12},{20,16},{24,20},{28,24},{1,29},{... | collective-permute-start | bytes 884744 | tf_op jit(solution)/shard_map/ppermute | solution.py:231
  6.5 15.7 %collective-permute-start = (bf16[144,1024]{1,0:T(8,128)(2,1)S(1)}, bf16[144,1024]{1,0:T(8,128)(2,1)S(1)}, u32[]{:S(2)}, u32[]{:S(2)}) collective-permute-start(bf16[144,1024]{1,0:T(8,128)(2,1)S(1)} %get-tuple-element.26), channel_id=1, source_target_pairs={{0,4},{4,8},{8,12},{12,16},{16,20},{20,24},{24,28},{28,0},{1,5},{5... | collective-permute-start | bytes 884744 | tf_op jit(solution)/shard_map/ppermute | solution.py:231
  8.4 129.0 %collective-permute-start.5 = (bf16[128,2048]{1,0:T(8,128)(2,1)}, bf16[128,2048]{1,0:T(8,128)(2,1)S(1)}, u32[]{:S(2)}, u32[]{:S(2)}) collective-permute-start(bf16[128,2048]{1,0:T(8,128)(2,1)} %shard_map.65), channel_id=1, source_target_pairs={{0,1},{1,0},{2,3},{3,2},{4,5},{5,4},{6,7},{7,6},{8,9},{9,8},{10,11... | collective-permute-start | bytes 1572872 | tf_op jit(solution)/shard_map/ppermute | solution.py:24
  11.9 125.5 %collective-permute-start.6 = (bf16[128,2048]{1,0:T(8,128)(2,1)}, bf16[128,2048]{1,0:T(8,128)(2,1)S(1)}, u32[]{:S(2)}, u32[]{:S(2)}) collective-permute-start(bf16[128,2048]{1,0:T(8,128)(2,1)} %shard_map.66), channel_id=1, source_target_pairs={{0,2},{1,3},{2,0},{3,1},{4,6},{5,7},{6,4},{7,5},{8,10},{9,11},{10,... | collective-permute-start | bytes 1572872 | tf_op jit(solution)/shard_map/ppermute | solution.py:24
  20.1 1.9 copy-start.10
  30.8 4.6 %copy-start.11 = (f32[1,1024]{1,0:T(1,128)S(1)}, f32[1,1024]{1,0:T(1,128)}, u32[]{:S(2)}) copy-start(f32[1,1024]{1,0:T(1,128)} %param.10) | copy-start | bytes 12292
  30.8 29.5 %copy-start.2 = (bf16[128,2048]{1,0:T(8,128)(2,1)S(1)}, bf16[128,2048]{1,0:T(8,128)(2,1)}, u32[]{:S(2)}) copy-start(bf16[128,2048]{1,0:T(8,128)(2,1)} %shard_map.70) | copy-start | bytes 1572868
  30.9 11.4 %collective-permute-start.4 = (bf16[128,1024]{1,0:T(8,128)(2,1)S(1)}, bf16[128,1024]{1,0:T(8,128)(2,1)S(1)}, u32[]{:S(2)}, u32[]{:S(2)}) collective-permute-start(bf16[128,1024]{1,0:T(8,128)(2,1)S(1)} %get-tuple-element.28), channel_id=1, source_target_pairs={{0,3},{1,2},{2,1},{3,0},{4,7},{5,6},{6,5},{7,4},{8,11},{9,10},{10,... | collective-permute-start | bytes 786440 | tf_op jit(solution)/shard_map/ppermute | solution.py:24
  31.2 29.1 %collective-permute-start.3 = (bf16[128,1024]{1,0:T(8,128)(2,1)S(1)}, bf16[128,1024]{1,0:T(8,128)(2,1)S(1)}, u32[]{:S(2)}, u32[]{:S(2)}) collective-permute-start(bf16[128,1024]{1,0:T(8,128)(2,1)S(1)} %get-tuple-element.29), channel_id=1, source_target_pairs={{0,2},{1,3},{2,0},{3,1},{4,6},{5,7},{6,4},{7,5},{8,10},{9,11},{10,... | collective-permute-start | bytes 786440 | tf_op jit(solution)/shard_map/ppermute | solution.py:24
  32.9 27.4 %collective-permute-start.2 = (bf16[128,1024]{1,0:T(8,128)(2,1)S(1)}, bf16[128,1024]{1,0:T(8,128)(2,1)S(1)}, u32[]{:S(2)}, u32[]{:S(2)}) collective-permute-start(bf16[128,1024]{1,0:T(8,128)(2,1)S(1)} %get-tuple-element.30), channel_id=1, source_target_pairs={{0,1},{1,0},{2,3},{3,2},{4,5},{5,4},{6,7},{7,6},{8,9},{9,8},{10,11... | collective-permute-start | bytes 786440 | tf_op jit(solution)/shard_map/ppermute | solution.py:24
  42.3 23.2 %copy-start.4 = (bf16[128,1024]{1,0:T(8,128)(2,1)}, bf16[128,1024]{1,0:T(8,128)(2,1)S(1)}, u32[]{:S(2)}) copy-start(bf16[128,1024]{1,0:T(8,128)(2,1)S(1)} %collective-permute-done.4) | copy-start | bytes 786436
  42.3 36.1 %collective-permute-start.8 = (bf16[128,2048]{1,0:T(8,128)(2,1)}, bf16[128,2048]{1,0:T(8,128)(2,1)S(1)}, u32[]{:S(2)}, u32[]{:S(2)}) collective-permute-start(bf16[128,2048]{1,0:T(8,128)(2,1)} %shard_map.68), channel_id=1, source_target_pairs={{0,1},{1,0},{2,3},{3,2},{4,5},{5,4},{6,7},{7,6},{8,9},{9,8},{10,11... | collective-permute-start | bytes 1572872 | tf_op jit(solution)/shard_map/ppermute | solution.py:24
  60.3 5.2 %copy-start.6 = (bf16[128,1024]{1,0:T(8,128)(2,1)}, bf16[128,1024]{1,0:T(8,128)(2,1)S(1)}, u32[]{:S(2)}) copy-start(bf16[128,1024]{1,0:T(8,128)(2,1)S(1)} %collective-permute-done.3) | copy-start | bytes 786436
  60.3 49.4 %collective-permute-start.9 = (bf16[128,2048]{1,0:T(8,128)(2,1)}, bf16[128,2048]{1,0:T(8,128)(2,1)S(1)}, u32[]{:S(2)}, u32[]{:S(2)}) collective-permute-start(bf16[128,2048]{1,0:T(8,128)(2,1)} %shard_map.69), channel_id=1, source_target_pairs={{0,2},{1,3},{2,0},{3,1},{4,6},{5,7},{6,4},{7,5},{8,10},{9,11},{10,... | collective-permute-start | bytes 1572872 | tf_op jit(solution)/shard_map/ppermute | solution.py:24
  60.3 5.2 %copy-start.8 = (bf16[128,1024]{1,0:T(8,128)(2,1)}, bf16[128,1024]{1,0:T(8,128)(2,1)S(1)}, u32[]{:S(2)}) copy-start(bf16[128,1024]{1,0:T(8,128)(2,1)S(1)} %collective-permute-done.2) | copy-start | bytes 786436
  60.3 49.4 %collective-permute-start.10 = (bf16[128,2048]{1,0:T(8,128)(2,1)S(1)}, bf16[128,2048]{1,0:T(8,128)(2,1)S(1)}, u32[]{:S(2)}, u32[]{:S(2)}) collective-permute-start(bf16[128,2048]{1,0:T(8,128)(2,1)S(1)} %copy-done.2), channel_id=1, source_target_pairs={{0,3},{1,2},{2,1},{3,0},{4,7},{5,6},{6,5},{7,4},{8,11},{9,10},{10,... | collective-permute-start | bytes 1572872 | tf_op jit(solution)/shard_map/ppermute | solution.py:24
  66.2 1.8 copy-start.13
  68.5 0.9 copy-start.12
  69.4 0.8 copy-start.3
  74.3 1.8 copy-start.5
  74.3 1.8 copy-start.7
  74.3 1.8 copy-start.9
  76.1 33.6 %copy-start = (bf16[128,16384]{1,0:T(8,128)(2,1)S(1)}, bf16[128,16384]{1,0:T(8,128)(2,1)}, u32[]{:S(2)}) copy-start(bf16[128,16384]{1,0:T(8,128)(2,1)} %refs_0_.3) | copy-start | bytes 12582916
  77.0 1.4 copy-start.1
  78.4 59.0 %collective-permute-start.7 = (bf16[128,2048]{1,0:T(8,128)(2,1)S(1)}, bf16[128,2048]{1,0:T(8,128)(2,1)S(1)}, u32[]{:S(2)}, u32[]{:S(2)}) collective-permute-start(bf16[128,2048]{1,0:T(8,128)(2,1)S(1)} %copy-done.1), channel_id=1, source_target_pairs={{0,3},{1,2},{2,1},{3,0},{4,7},{5,6},{6,5},{7,4},{8,11},{9,10},{10,... | collective-permute-start | bytes 1572872 | tf_op jit(solution)/shard_map/ppermute | solution.py:24
  112.9 47.9 %collective-permute-start.16 = (bf16[128,2048]{1,0:T(8,128)(2,1)S(1)}, bf16[128,2048]{1,0:T(8,128)(2,1)S(1)}, u32[]{:S(2)}, u32[]{:S(2)}) collective-permute-start(bf16[128,2048]{1,0:T(8,128)(2,1)S(1)} %get-tuple-element.23), channel_id=1, source_target_pairs={{0,3},{1,2},{2,1},{3,0},{4,7},{5,6},{6,5},{7,4},{8,11},{9,10},{10,... | collective-permute-start | bytes 1572872 | tf_op jit(solution)/shard_map/ppermute | solution.py:24
  114.8 84.8 %collective-permute-start.14 = (bf16[128,2048]{1,0:T(8,128)(2,1)S(1)}, bf16[128,2048]{1,0:T(8,128)(2,1)S(1)}, u32[]{:S(2)}, u32[]{:S(2)}) collective-permute-start(bf16[128,2048]{1,0:T(8,128)(2,1)S(1)} %get-tuple-element.21), channel_id=1, source_target_pairs={{0,2},{1,3},{2,0},{3,1},{4,6},{5,7},{6,4},{7,5},{8,10},{9,11},{10,... | collective-permute-start | bytes 1572872 | tf_op jit(solution)/shard_map/ppermute | solution.py:24
  137.4 41.8 %collective-permute-start.15 = (bf16[128,2048]{1,0:T(8,128)(2,1)S(1)}, bf16[128,2048]{1,0:T(8,128)(2,1)S(1)}, u32[]{:S(2)}, u32[]{:S(2)}) collective-permute-start(bf16[128,2048]{1,0:T(8,128)(2,1)S(1)} %get-tuple-element.22), channel_id=1, source_target_pairs={{0,1},{1,0},{2,3},{3,2},{4,5},{5,4},{6,7},{7,6},{8,9},{9,8},{10,11... | collective-permute-start | bytes 1572872 | tf_op jit(solution)/shard_map/ppermute | solution.py:24
  140.6 59.8 %collective-permute-start.13 = (bf16[128,2048]{1,0:T(8,128)(2,1)S(1)}, bf16[128,2048]{1,0:T(8,128)(2,1)S(1)}, u32[]{:S(2)}, u32[]{:S(2)}) collective-permute-start(bf16[128,2048]{1,0:T(8,128)(2,1)S(1)} %get-tuple-element.20), channel_id=1, source_target_pairs={{0,3},{1,2},{2,1},{3,0},{4,7},{5,6},{6,5},{7,4},{8,11},{9,10},{10,... | collective-permute-start | bytes 1572872 | tf_op jit(solution)/shard_map/ppermute | solution.py:24
  142.5 58.7 %collective-permute-start.12 = (bf16[128,2048]{1,0:T(8,128)(2,1)S(1)}, bf16[128,2048]{1,0:T(8,128)(2,1)S(1)}, u32[]{:S(2)}, u32[]{:S(2)}) collective-permute-start(bf16[128,2048]{1,0:T(8,128)(2,1)S(1)} %get-tuple-element.19), channel_id=1, source_target_pairs={{0,1},{1,0},{2,3},{3,2},{4,5},{5,4},{6,7},{7,6},{8,9},{9,8},{10,11... | collective-permute-start | bytes 1572872 | tf_op jit(solution)/shard_map/ppermute | solution.py:24
  160.8 59.2 %collective-permute-start.11 = (bf16[128,2048]{1,0:T(8,128)(2,1)S(1)}, bf16[128,2048]{1,0:T(8,128)(2,1)S(1)}, u32[]{:S(2)}, u32[]{:S(2)}) collective-permute-start(bf16[128,2048]{1,0:T(8,128)(2,1)S(1)} %get-tuple-element.18), channel_id=1, source_target_pairs={{0,2},{1,3},{2,0},{3,1},{4,6},{5,7},{6,4},{7,5},{8,10},{9,11},{10,... | collective-permute-start | bytes 1572872 | tf_op jit(solution)/shard_map/ppermute | solution.py:24
where the time goes:
time: 221 us
  starting transfers between devices  92.6 us (42%)
  waiting for transfers between devices  77.9 us (35%)
  Pallas kernels  30.9 us (14%)
  matrix products  13.6 us (6%)
  local copies, waits for them, and re-layouts  2.53 us (1%)
    ppermute x15, starting transfers between devices, swap(): lax.ppermute(block, 'member', partners(lax.axis_size('member'), step))  89.2 us
    ppermute x15, waiting for transfers between devices, swap(): lax.ppermute(block, 'member', partners(lax.axis_size('member'), step))  77.9 us
    dot_general x8, matrix products, product(): lax.dot_general(left, right, (dims, ((), ())), preferred_element_type=jnp...  11.4 us
    pallas_call x6, Pallas kernels, cut(): pl.pallas_call(functools.partial(cut_kernel, lambda pos: (pos ^ step) * C...  11.1 us
    pallas_call x1, Pallas kernels, pick(): pl.pallas_call(pick_kernel, grid_spec=pltpu.PrefetchScalarGridSpec(num_sc...  8.61 us
    pallas_call x2, Pallas kernels, update_state(): pl.pallas_call(functools.partial(update_kernel, count, aliased), grid_spe...  6.37 us
    pallas_call x6, Pallas kernels, place(): pl.pallas_call(functools.partial(place_kernel, lambda pos: (pos ^ step) *...  4.82 us
  transfers between devices with their start and end apart: 17, of which 5 were waited for; matrix products, arithmetic and copies ran while one was open for 6% of the time, Pallas kernels for 14%

commit v1 on v0

--- a/solution.py
+++ b/solution.py
@@ -24,25 +24,44 @@
     return lax.ppermute(block, "member", partners(lax.axis_size("member"), step))
 
 
-def cut_kernel(first, pos_ref, state_ref, out_ref, sem):
-    width = out_ref.shape[1]
+def cut_kernel(first, bands, pos_ref, state_ref, out_ref, held, in_sem, out_sem):
+    rows, width = out_ref.shape
     start = pl.multiple_of(first(pos_ref[0]) * width, LANES)
-    copy = pltpu.make_async_copy(state_ref.at[:, pl.ds(start, width)], out_ref, sem)
-    copy.start()
-    copy.wait()
+    band = rows // bands
+    reads, writes = [], []
+    for k in range(bands):
+        part = pl.ds(k * band, band)
+        reads.append(
+            pltpu.make_async_copy(
+                state_ref.at[part, pl.ds(start, width)], held.at[part], in_sem.at[k]
+            )
+        )
+        writes.append(pltpu.make_async_copy(held.at[part], out_ref.at[part], out_sem.at[k]))
+    for copy in reads:
+        copy.start()
+    for read, write in zip(reads, writes):
+        read.wait()
+        write.start()
+    for copy in writes:
+        copy.wait()
 
 
 def cut(position, state, step, chunk, count):
     rows, total = state.shape
     width = total // (count * CHUNKS)
+    bands = max(rows // 32, 1)
     return pl.pallas_call(
-        functools.partial(cut_kernel, lambda pos: (pos ^ step) * CHUNKS + chunk),
+        functools.partial(cut_kernel, lambda pos: (pos ^ step) * CHUNKS + chunk, bands),
         in_specs=[
             pl.BlockSpec(memory_space=pltpu.SMEM),
             pl.BlockSpec(memory_space=pl.ANY),
         ],
-        out_specs=pl.BlockSpec(memory_space=pltpu.VMEM),
-        scratch_shapes=[pltpu.SemaphoreType.DMA],
+        out_specs=pl.BlockSpec(memory_space=pl.ANY),
+        scratch_shapes=[
+            pltpu.VMEM((rows, width), state.dtype),
+            pltpu.SemaphoreType.DMA((bands,)),
+            pltpu.SemaphoreType.DMA((bands,)),
+        ],
         out_shape=jax.ShapeDtypeStruct((rows, width), state.dtype),
         cost_estimate=pl.CostEstimate(
             flops=0, transcendentals=0, bytes_accessed=2 * rows * width
@@ -241,10 +260,11 @@
     position = lax.axis_index("member").astype(jnp.int32).reshape(1)
     steps = send_order(count)
 
-    def send_chunk(chunk):
-        return {step: swap(cut(position, state, step, chunk, count), step) for step in steps}
-
-    arrived = [send_chunk(0)]
+    def send_chunk(chunk, order):
+        return {step: swap(cut(position, state, step, chunk, count), step) for step in order}
+
+    arrived = [send_chunk(0, steps[:1])]
+    arrived[0] |= send_chunk(0, steps[1:])
 
     pad = jnp.zeros((14, hx.shape[1]), hx.dtype)
     stacked = jnp.concatenate([hx, obs_value[None], obs_rinv[None], pad], axis=0)
@@ -257,7 +277,7 @@
     obs_block = jnp.concatenate([picked[0]] + [others[s] for s in range(1, count)], axis=0)
 
     for chunk in range(1, CHUNKS):
-        arrived.append(send_chunk(chunk))
+        arrived.append(send_chunk(chunk, steps))
 
     transform = analysis(obs_block, obs_pair, loc_weight[0])
 

time: 221 us -> 221 us (level)
  no operation moved by 1% of the time
where the time goes in v1:
time: 221 us
  starting transfers between devices  92.4 us (42%)
  waiting for transfers between devices  78.3 us (35%)
  Pallas kernels  30.7 us (14%)
  matrix products  13.6 us (6%)
  local copies, waits for them, and re-layouts  2.53 us (1%)
    ppermute x15, starting transfers between devices, swap(): lax.ppermute(block, 'member', partners(lax.axis_size('member'), step))  89 us
    ppermute x15, waiting for transfers between devices, swap(): lax.ppermute(block, 'member', partners(lax.axis_size('member'), step))  78.3 us
    dot_general x8, matrix products, product(): lax.dot_general(left, right, (dims, ((), ())), preferred_element_type=jnp...  11.4 us
    pallas_call x6, Pallas kernels, cut(): pl.pallas_call(functools.partial(cut_kernel, lambda pos: (pos ^ step) * C...  10.9 us
    pallas_call x1, Pallas kernels, pick(): pl.pallas_call(pick_kernel, grid_spec=pltpu.PrefetchScalarGridSpec(num_sc...  8.61 us
    pallas_call x2, Pallas kernels, update_state(): pl.pallas_call(functools.partial(update_kernel, count, aliased), grid_spe...  6.36 us
    pallas_call x6, Pallas kernels, place(): pl.pallas_call(functools.partial(place_kernel, lambda pos: (pos ^ step) *...  4.82 us
  transfers between devices with their start and end apart: 17, of which 5 were waited for; matrix products, arithmetic and copies ran while one was open for 6% of the time, Pallas kernels for 14%

profile of v1, /device:TPU:0, one launch (start us, length us, event | category | flops | bytes accessed | tf_op | source)
XLA Modules:
  0.0 220.7 jit_solution(2350835941268340812)
XLA Ops:
  0.0 0.7 broadcast_in_dim.12
  0.7 0.7 broadcast_in_dim.13
  1.4 0.1 pad.7.clone
  1.5 1.5 maximum_maximum_fusion.own_ref
  3.1 3.4 %collective-permute-start.1 = (bf16[144,1024]{1,0:T(8,128)(2,1)S(1)}, bf16[144,1024]{1,0:T(8,128)(2,1)S(1)}, u32[]{:S(2)}, u32[]{:S(2)}) collective-permute-start(bf16[144,1024]{1,0:T(8,128)(2,1)S(1)} %get-tuple-element.25), channel_id=1, source_target_pairs={{0,28},{4,0},{8,4},{12,8},{16,12},{20,16},{24,20},{28,24},{1,29},{... | collective-permute-start | bytes 884744 | tf_op jit(solution)/shard_map/ppermute | solution.py:250
  6.5 1.8 shard_map.65
  8.3 1.6 collective-permute-start.5
  10.0 1.8 shard_map.66
  11.8 2.7 %collective-permute-start.6 = (bf16[128,2048]{1,0:T(8,128)(2,1)}, bf16[128,2048]{1,0:T(8,128)(2,1)S(1)}, u32[]{:S(2)}, u32[]{:S(2)}) collective-permute-start(bf16[128,2048]{1,0:T(8,128)(2,1)} %shard_map.66), channel_id=1, source_target_pairs={{0,2},{1,3},{2,0},{3,1},{4,6},{5,7},{6,4},{7,5},{8,10},{9,11},{10,... | collective-permute-start | bytes 1572872 | tf_op jit(solution)/shard_map/ppermute | solution.py:24
  14.4 1.8 shard_map.70
  16.3 1.8 shard_map.69
  18.1 1.8 shard_map.68
  19.9 0.0 copy-start.10
  19.9 1.8 shard_map.67
  21.8 0.1 reduce_min.9
  21.9 0.0 collective-permute-done.low_ref
  22.0 8.6 %shard_map.64 = (bf16[4,128,1024]{2,1,0:T(8,128)(2,1)S(1)}, bf16[16,1024]{1,0:T(8,128)(2,1)S(1)}) custom-call(s32[1]{0:T(128)} %bitcast.pos_ref, s32[4]{0:T(128)S(1)} %multiply_minimum_fusion.start_ref, s32[4,1,1024]{2,1,0:T(1,128)S(1)} %reshape.16.index_ref, bf16[144,4096]{1,0:T(8,128)(2,1)S(1)} %maximum_maximum_fusion.own_ref, ...), custom_call_target="tpu_custom_call" | custom-call | flops 2566914048 | bytes 2359296 | tf_op jit(solution)/shard_map/pallas_call | solution.py:104
  30.6 0.0 copy-start.11
  30.6 0.0 copy-start.2
  30.6 0.1 slice_bitcast_fusion.3
  30.7 0.3 collective-permute-start.4
  31.0 1.7 collective-permute-start.3
  32.7 2.5 %collective-permute-start.2 = (bf16[128,1024]{1,0:T(8,128)(2,1)S(1)}, bf16[128,1024]{1,0:T(8,128)(2,1)S(1)}, u32[]{:S(2)}, u32[]{:S(2)}) collective-permute-start(bf16[128,1024]{1,0:T(8,128)(2,1)S(1)} %get-tuple-element.30), channel_id=1, source_target_pairs={{0,1},{1,0},{2,3},{3,2},{4,5},{5,4},{6,7},{7,6},{8,9},{9,8},{10,11... | collective-permute-start | bytes 786440 | tf_op jit(solution)/shard_map/ppermute | solution.py:24
  35.2 7.2 %collective-permute-done.4 = bf16[128,1024]{1,0:T(8,128)(2,1)S(1)} collective-permute-done((bf16[128,1024]{1,0:T(8,128)(2,1)S(1)}, bf16[128,1024]{1,0:T(8,128)(2,1)S(1)}, u32[]{:S(2)}, u32[]{:S(2)}) %collective-permute-start.4) | collective-permute-done | bytes 262176 | tf_op jit(solution)/shard_map/ppermute | solution.py:24
  42.4 14.1 %collective-permute-start.8 = (bf16[128,2048]{1,0:T(8,128)(2,1)}, bf16[128,2048]{1,0:T(8,128)(2,1)S(1)}, u32[]{:S(2)}, u32[]{:S(2)}) collective-permute-start(bf16[128,2048]{1,0:T(8,128)(2,1)} %shard_map.68), channel_id=1, source_target_pairs={{0,1},{1,0},{2,3},{3,2},{4,5},{5,4},{6,7},{7,6},{8,9},{9,8},{10,11... | collective-permute-start | bytes 1572872 | tf_op jit(solution)/shard_map/ppermute | solution.py:24
  56.5 3.7 %collective-permute-done.3 = bf16[128,1024]{1,0:T(8,128)(2,1)S(1)} collective-permute-done((bf16[128,1024]{1,0:T(8,128)(2,1)S(1)}, bf16[128,1024]{1,0:T(8,128)(2,1)S(1)}, u32[]{:S(2)}, u32[]{:S(2)}) %collective-permute-start.3) | collective-permute-done | bytes 262176 | tf_op jit(solution)/shard_map/ppermute | solution.py:24
  60.2 2.5 %collective-permute-start.10 = (bf16[128,2048]{1,0:T(8,128)(2,1)S(1)}, bf16[128,2048]{1,0:T(8,128)(2,1)S(1)}, u32[]{:S(2)}, u32[]{:S(2)}) collective-permute-start(bf16[128,2048]{1,0:T(8,128)(2,1)S(1)} %copy-done.2), channel_id=1, source_target_pairs={{0,3},{1,2},{2,1},{3,0},{4,7},{5,6},{6,5},{7,4},{8,11},{9,10},{10,... | collective-permute-start | bytes 1572872 | tf_op jit(solution)/shard_map/ppermute | solution.py:24
  62.8 0.2 convert_reduce_fusion
  63.0 2.4 %multiply_reduce_fusion = (f32[]{:T(128)}, f32[512,512]{1,0:T(8,128)}) fusion(f32[1024]{0:T(1024)S(1)} %bitcast.38, f32[1024]{0:T(1024)S(1)} %get-tuple-element.32, bf16[128,1024]{1,0:T(8,128)(2,1)S(1)} %collective-permute-done.4, bf16[128,1024]{1,0:T(8,128)(2,1)S(1)} %collective-permute-done.3, bf16[128,1024]{1,0:T(8,128)(2,1)S(1)} %collective-permute-done.2, ...), kind=kOutput, calls=%fused_computation.25 | convolution fusion | flops 543948800 | bytes 2105348 | tf_op jit(solution)/shard_map/dot_general | solution.py:215
  66.1 0.0 copy-start.13
  66.2 1.8 fusion.2
  67.9 0.4 convolution_convert_fusion.2
  68.4 0.4 convolution_convert_fusion.3
  68.8 0.4 fusion.3
  69.3 0.8 copy-done.3
  70.1 1.2 convolution_convert_fusion.1
  71.3 2.9 %fusion.4 = bf16[512,512]{1,0:T(8,128)(2,1)} fusion(bf16[512,512]{1,0:T(8,128)(2,1)} %convolution_convert_fusion.1, bf16[512,512]{1,0:T(8,128)(2,1)} %copy-done.12, bf16[512,512]{1,0:T(8,128)(2,1)} %copy-done.3), kind=kOutput, calls=%fused_computation.18 | convolution fusion | flops 538443776 | bytes 2097152 | tf_op jit(solution)/shard_map/dot_general | solution.py:215
  74.2 1.8 convolution_divide_fusion
  76.0 0.0 copy-start
  76.0 0.9 convolution_bitcast_fusion.1
  77.0 0.7 convolution_bitcast_fusion
  77.6 0.7 fusion.9
  78.3 0.1 copy-done.1
  78.3 1.4 collective-permute-start.7
  79.7 0.1 fusion.7.transform_ref
  79.9 29.8 %collective-permute-done.9.refs_2_ = bf16[128,2048]{1,0:T(8,128)(2,1)S(1)} collective-permute-done((bf16[128,2048]{1,0:T(8,128)(2,1)}, bf16[128,2048]{1,0:T(8,128)(2,1)S(1)}, u32[]{:S(2)}, u32[]{:S(2)}) %collective-permute-start.9) | collective-permute-done | bytes 524320 | tf_op jit(solution)/shard_map/ppermute | solution.py:24
  109.6 3.2 %shard_map.71 = (bf16[128,16384]{1,0:T(8,128)(2,1)}, bf16[128,2048]{1,0:T(8,128)(2,1)S(1)}, bf16[128,2048]{1,0:T(8,128)(2,1)S(1)}, bf16[128,2048]{1,0:T(8,128)(2,1)S(1)}) custom-call(s32[1]{0:T(128)} %bitcast.pos_ref, bf16[512,512]{1,0:T(8,128)(2,1)S(1)} %fusion.7.transform_ref, bf16[128,16384]{1,0:T(8,128)(2,1)S(1)} %copy-done, ...), custom_call_target="tpu_custom_call" | custom-call | flops 1073741824 | bytes 4718592 | tf_op jit(solution)/shard_map/pallas_call | solution.py:163
  112.8 1.9 collective-permute-start.16
  114.7 22.6 %collective-permute-start.14 = (bf16[128,2048]{1,0:T(8,128)(2,1)S(1)}, bf16[128,2048]{1,0:T(8,128)(2,1)S(1)}, u32[]{:S(2)}, u32[]{:S(2)}) collective-permute-start(bf16[128,2048]{1,0:T(8,128)(2,1)S(1)} %get-tuple-element.21), channel_id=1, source_target_pairs={{0,2},{1,3},{2,0},{3,1},{4,6},{5,7},{6,4},{7,5},{8,10},{9,11},{10,... | collective-permute-start | bytes 1572872 | tf_op jit(solution)/shard_map/ppermute | solution.py:24
  137.3 0.0 collective-permute-done.7.refs_3_
  137.3 3.2 %shard_map.72 = (bf16[128,16384]{1,0:T(8,128)(2,1)}, bf16[128,2048]{1,0:T(8,128)(2,1)S(1)}, bf16[128,2048]{1,0:T(8,128)(2,1)S(1)}, bf16[128,2048]{1,0:T(8,128)(2,1)S(1)}) custom-call(s32[1]{0:T(128)} %bitcast.pos_ref, bf16[512,512]{1,0:T(8,128)(2,1)S(1)} %fusion.7.transform_ref, bf16[128,16384]{1,0:T(8,128)(2,1)S(1)} %copy-done, ...), custom_call_target="tpu_custom_call", output_to_operand_aliasing={{0}: (6, {})} | custom-call | flops 1073741824 | bytes 4718592 | tf_op jit(solution)/shard_map/pallas_call | solution.py:163
  140.5 1.9 collective-permute-start.13
  142.4 18.3 %collective-permute-start.12 = (bf16[128,2048]{1,0:T(8,128)(2,1)S(1)}, bf16[128,2048]{1,0:T(8,128)(2,1)S(1)}, u32[]{:S(2)}, u32[]{:S(2)}) collective-permute-start(bf16[128,2048]{1,0:T(8,128)(2,1)S(1)} %get-tuple-element.19), channel_id=1, source_target_pairs={{0,1},{1,0},{2,3},{3,2},{4,5},{5,4},{6,7},{7,6},{8,9},{9,8},{10,11... | collective-permute-start | bytes 1572872 | tf_op jit(solution)/shard_map/ppermute | solution.py:24
  160.7 0.0 collective-permute-done.16.piece_ref
  160.7 17.6 %collective-permute-start.11 = (bf16[128,2048]{1,0:T(8,128)(2,1)S(1)}, bf16[128,2048]{1,0:T(8,128)(2,1)S(1)}, u32[]{:S(2)}, u32[]{:S(2)}) collective-permute-start(bf16[128,2048]{1,0:T(8,128)(2,1)S(1)} %get-tuple-element.18), channel_id=1, source_target_pairs={{0,2},{1,3},{2,0},{3,1},{4,6},{5,7},{6,4},{7,5},{8,10},{9,11},{10,... | collective-permute-start | bytes 1572872 | tf_op jit(solution)/shard_map/ppermute | solution.py:24
  178.3 0.8 shard_map.73.buffer_ref
  179.1 0.0 collective-permute-done.15.piece_ref
  179.1 0.8 shard_map.74.buffer_ref
  179.9 19.6 %collective-permute-done.14.piece_ref = bf16[128,2048]{1,0:T(8,128)(2,1)S(1)} collective-permute-done((bf16[128,2048]{1,0:T(8,128)(2,1)S(1)}, bf16[128,2048]{1,0:T(8,128)(2,1)S(1)}, u32[]{:S(2)}, u32[]{:S(2)}) %collective-permute-start.14) | collective-permute-done | bytes 524320 | tf_op jit(solution)/shard_map/ppermute | solution.py:24
  199.5 0.8 shard_map.75.buffer_ref
  200.3 0.8 shard_map.76.buffer_ref
  201.2 0.8 shard_map.77.buffer_ref
  202.0 17.9 %collective-permute-done.11.piece_ref = bf16[128,2048]{1,0:T(8,128)(2,1)S(1)} collective-permute-done((bf16[128,2048]{1,0:T(8,128)(2,1)S(1)}, bf16[128,2048]{1,0:T(8,128)(2,1)S(1)}, u32[]{:S(2)}, u32[]{:S(2)}) %collective-permute-start.11) | collective-permute-done | bytes 524320 | tf_op jit(solution)/shard_map/ppermute | solution.py:24
  219.9 0.8 shard_map.78
  (39 shorter events, 0.2 us)
Async XLA Ops:
  3.1 18.9 %collective-permute-start.1 = (bf16[144,1024]{1,0:T(8,128)(2,1)S(1)}, bf16[144,1024]{1,0:T(8,128)(2,1)S(1)}, u32[]{:S(2)}, u32[]{:S(2)}) collective-permute-start(bf16[144,1024]{1,0:T(8,128)(2,1)S(1)} %get-tuple-element.25), channel_id=1, source_target_pairs={{0,28},{4,0},{8,4},{12,8},{16,12},{20,16},{24,20},{28,24},{1,29},{... | collective-permute-start | bytes 884744 | tf_op jit(solution)/shard_map/ppermute | solution.py:250
  6.5 15.5 %collective-permute-start = (bf16[144,1024]{1,0:T(8,128)(2,1)S(1)}, bf16[144,1024]{1,0:T(8,128)(2,1)S(1)}, u32[]{:S(2)}, u32[]{:S(2)}) collective-permute-start(bf16[144,1024]{1,0:T(8,128)(2,1)S(1)} %get-tuple-element.26), channel_id=1, source_target_pairs={{0,4},{4,8},{8,12},{12,16},{16,20},{20,24},{24,28},{28,0},{1,5},{5... | collective-permute-start | bytes 884744 | tf_op jit(solution)/shard_map/ppermute | solution.py:250
  8.3 129.0 %collective-permute-start.5 = (bf16[128,2048]{1,0:T(8,128)(2,1)}, bf16[128,2048]{1,0:T(8,128)(2,1)S(1)}, u32[]{:S(2)}, u32[]{:S(2)}) collective-permute-start(bf16[128,2048]{1,0:T(8,128)(2,1)} %shard_map.65), channel_id=1, source_target_pairs={{0,1},{1,0},{2,3},{3,2},{4,5},{5,4},{6,7},{7,6},{8,9},{9,8},{10,11... | collective-permute-start | bytes 1572872 | tf_op jit(solution)/shard_map/ppermute | solution.py:24
  11.8 125.5 %collective-permute-start.6 = (bf16[128,2048]{1,0:T(8,128)(2,1)}, bf16[128,2048]{1,0:T(8,128)(2,1)S(1)}, u32[]{:S(2)}, u32[]{:S(2)}) collective-permute-start(bf16[128,2048]{1,0:T(8,128)(2,1)} %shard_map.66), channel_id=1, source_target_pairs={{0,2},{1,3},{2,0},{3,1},{4,6},{5,7},{6,4},{7,5},{8,10},{9,11},{10,... | collective-permute-start | bytes 1572872 | tf_op jit(solution)/shard_map/ppermute | solution.py:24
  19.9 1.8 copy-start.10
  30.6 4.6 %copy-start.11 = (f32[1,1024]{1,0:T(1,128)S(1)}, f32[1,1024]{1,0:T(1,128)}, u32[]{:S(2)}) copy-start(f32[1,1024]{1,0:T(1,128)} %param.10) | copy-start | bytes 12292
  30.6 29.6 %copy-start.2 = (bf16[128,2048]{1,0:T(8,128)(2,1)S(1)}, bf16[128,2048]{1,0:T(8,128)(2,1)}, u32[]{:S(2)}) copy-start(bf16[128,2048]{1,0:T(8,128)(2,1)} %shard_map.70) | copy-start | bytes 1572868
  30.7 11.7 %collective-permute-start.4 = (bf16[128,1024]{1,0:T(8,128)(2,1)S(1)}, bf16[128,1024]{1,0:T(8,128)(2,1)S(1)}, u32[]{:S(2)}, u32[]{:S(2)}) collective-permute-start(bf16[128,1024]{1,0:T(8,128)(2,1)S(1)} %get-tuple-element.28), channel_id=1, source_target_pairs={{0,3},{1,2},{2,1},{3,0},{4,7},{5,6},{6,5},{7,4},{8,11},{9,10},{10,... | collective-permute-start | bytes 786440 | tf_op jit(solution)/shard_map/ppermute | solution.py:24
  31.0 29.2 %collective-permute-start.3 = (bf16[128,1024]{1,0:T(8,128)(2,1)S(1)}, bf16[128,1024]{1,0:T(8,128)(2,1)S(1)}, u32[]{:S(2)}, u32[]{:S(2)}) collective-permute-start(bf16[128,1024]{1,0:T(8,128)(2,1)S(1)} %get-tuple-element.29), channel_id=1, source_target_pairs={{0,2},{1,3},{2,0},{3,1},{4,6},{5,7},{6,4},{7,5},{8,10},{9,11},{10,... | collective-permute-start | bytes 786440 | tf_op jit(solution)/shard_map/ppermute | solution.py:24
  32.7 27.5 %collective-permute-start.2 = (bf16[128,1024]{1,0:T(8,128)(2,1)S(1)}, bf16[128,1024]{1,0:T(8,128)(2,1)S(1)}, u32[]{:S(2)}, u32[]{:S(2)}) collective-permute-start(bf16[128,1024]{1,0:T(8,128)(2,1)S(1)} %get-tuple-element.30), channel_id=1, source_target_pairs={{0,1},{1,0},{2,3},{3,2},{4,5},{5,4},{6,7},{7,6},{8,9},{9,8},{10,11... | collective-permute-start | bytes 786440 | tf_op jit(solution)/shard_map/ppermute | solution.py:24
  42.4 23.0 %copy-start.4 = (bf16[128,1024]{1,0:T(8,128)(2,1)}, bf16[128,1024]{1,0:T(8,128)(2,1)S(1)}, u32[]{:S(2)}) copy-start(bf16[128,1024]{1,0:T(8,128)(2,1)S(1)} %collective-permute-done.4) | copy-start | bytes 786436
  42.4 35.9 %collective-permute-start.8 = (bf16[128,2048]{1,0:T(8,128)(2,1)}, bf16[128,2048]{1,0:T(8,128)(2,1)S(1)}, u32[]{:S(2)}, u32[]{:S(2)}) collective-permute-start(bf16[128,2048]{1,0:T(8,128)(2,1)} %shard_map.68), channel_id=1, source_target_pairs={{0,1},{1,0},{2,3},{3,2},{4,5},{5,4},{6,7},{7,6},{8,9},{9,8},{10,11... | collective-permute-start | bytes 1572872 | tf_op jit(solution)/shard_map/ppermute | solution.py:24
  60.2 5.2 %copy-start.6 = (bf16[128,1024]{1,0:T(8,128)(2,1)}, bf16[128,1024]{1,0:T(8,128)(2,1)S(1)}, u32[]{:S(2)}) copy-start(bf16[128,1024]{1,0:T(8,128)(2,1)S(1)} %collective-permute-done.3) | copy-start | bytes 786436
  60.2 49.4 %collective-permute-start.9 = (bf16[128,2048]{1,0:T(8,128)(2,1)}, bf16[128,2048]{1,0:T(8,128)(2,1)S(1)}, u32[]{:S(2)}, u32[]{:S(2)}) collective-permute-start(bf16[128,2048]{1,0:T(8,128)(2,1)} %shard_map.69), channel_id=1, source_target_pairs={{0,2},{1,3},{2,0},{3,1},{4,6},{5,7},{6,4},{7,5},{8,10},{9,11},{10,... | collective-permute-start | bytes 1572872 | tf_op jit(solution)/shard_map/ppermute | solution.py:24
  60.2 5.2 %copy-start.8 = (bf16[128,1024]{1,0:T(8,128)(2,1)}, bf16[128,1024]{1,0:T(8,128)(2,1)S(1)}, u32[]{:S(2)}) copy-start(bf16[128,1024]{1,0:T(8,128)(2,1)S(1)} %collective-permute-done.2) | copy-start | bytes 786436
  60.2 49.4 %collective-permute-start.10 = (bf16[128,2048]{1,0:T(8,128)(2,1)S(1)}, bf16[128,2048]{1,0:T(8,128)(2,1)S(1)}, u32[]{:S(2)}, u32[]{:S(2)}) collective-permute-start(bf16[128,2048]{1,0:T(8,128)(2,1)S(1)} %copy-done.2), channel_id=1, source_target_pairs={{0,3},{1,2},{2,1},{3,0},{4,7},{5,6},{6,5},{7,4},{8,11},{9,10},{10,... | collective-permute-start | bytes 1572872 | tf_op jit(solution)/shard_map/ppermute | solution.py:24
  66.1 1.8 copy-start.13
  68.4 0.9 copy-start.12
  69.3 0.8 copy-start.3
  74.2 1.8 copy-start.5
  74.2 1.8 copy-start.7
  74.2 1.8 copy-start.9
  76.0 33.6 %copy-start = (bf16[128,16384]{1,0:T(8,128)(2,1)S(1)}, bf16[128,16384]{1,0:T(8,128)(2,1)}, u32[]{:S(2)}) copy-start(bf16[128,16384]{1,0:T(8,128)(2,1)} %refs_0_.3) | copy-start | bytes 12582916
  77.0 1.4 copy-start.1
  78.3 59.0 %collective-permute-start.7 = (bf16[128,2048]{1,0:T(8,128)(2,1)S(1)}, bf16[128,2048]{1,0:T(8,128)(2,1)S(1)}, u32[]{:S(2)}, u32[]{:S(2)}) collective-permute-start(bf16[128,2048]{1,0:T(8,128)(2,1)S(1)} %copy-done.1), channel_id=1, source_target_pairs={{0,3},{1,2},{2,1},{3,0},{4,7},{5,6},{6,5},{7,4},{8,11},{9,10},{10,... | collective-permute-start | bytes 1572872 | tf_op jit(solution)/shard_map/ppermute | solution.py:24
  112.8 47.9 %collective-permute-start.16 = (bf16[128,2048]{1,0:T(8,128)(2,1)S(1)}, bf16[128,2048]{1,0:T(8,128)(2,1)S(1)}, u32[]{:S(2)}, u32[]{:S(2)}) collective-permute-start(bf16[128,2048]{1,0:T(8,128)(2,1)S(1)} %get-tuple-element.23), channel_id=1, source_target_pairs={{0,3},{1,2},{2,1},{3,0},{4,7},{5,6},{6,5},{7,4},{8,11},{9,10},{10,... | collective-permute-start | bytes 1572872 | tf_op jit(solution)/shard_map/ppermute | solution.py:24
  114.7 84.8 %collective-permute-start.14 = (bf16[128,2048]{1,0:T(8,128)(2,1)S(1)}, bf16[128,2048]{1,0:T(8,128)(2,1)S(1)}, u32[]{:S(2)}, u32[]{:S(2)}) collective-permute-start(bf16[128,2048]{1,0:T(8,128)(2,1)S(1)} %get-tuple-element.21), channel_id=1, source_target_pairs={{0,2},{1,3},{2,0},{3,1},{4,6},{5,7},{6,4},{7,5},{8,10},{9,11},{10,... | collective-permute-start | bytes 1572872 | tf_op jit(solution)/shard_map/ppermute | solution.py:24
  137.3 41.8 %collective-permute-start.15 = (bf16[128,2048]{1,0:T(8,128)(2,1)S(1)}, bf16[128,2048]{1,0:T(8,128)(2,1)S(1)}, u32[]{:S(2)}, u32[]{:S(2)}) collective-permute-start(bf16[128,2048]{1,0:T(8,128)(2,1)S(1)} %get-tuple-element.22), channel_id=1, source_target_pairs={{0,1},{1,0},{2,3},{3,2},{4,5},{5,4},{6,7},{7,6},{8,9},{9,8},{10,11... | collective-permute-start | bytes 1572872 | tf_op jit(solution)/shard_map/ppermute | solution.py:24
  140.5 59.8 %collective-permute-start.13 = (bf16[128,2048]{1,0:T(8,128)(2,1)S(1)}, bf16[128,2048]{1,0:T(8,128)(2,1)S(1)}, u32[]{:S(2)}, u32[]{:S(2)}) collective-permute-start(bf16[128,2048]{1,0:T(8,128)(2,1)S(1)} %get-tuple-element.20), channel_id=1, source_target_pairs={{0,3},{1,2},{2,1},{3,0},{4,7},{5,6},{6,5},{7,4},{8,11},{9,10},{10,... | collective-permute-start | bytes 1572872 | tf_op jit(solution)/shard_map/ppermute | solution.py:24
  142.4 58.7 %collective-permute-start.12 = (bf16[128,2048]{1,0:T(8,128)(2,1)S(1)}, bf16[128,2048]{1,0:T(8,128)(2,1)S(1)}, u32[]{:S(2)}, u32[]{:S(2)}) collective-permute-start(bf16[128,2048]{1,0:T(8,128)(2,1)S(1)} %get-tuple-element.19), channel_id=1, source_target_pairs={{0,1},{1,0},{2,3},{3,2},{4,5},{5,4},{6,7},{7,6},{8,9},{9,8},{10,11... | collective-permute-start | bytes 1572872 | tf_op jit(solution)/shard_map/ppermute | solution.py:24
  160.7 59.2 %collective-permute-start.11 = (bf16[128,2048]{1,0:T(8,128)(2,1)S(1)}, bf16[128,2048]{1,0:T(8,128)(2,1)S(1)}, u32[]{:S(2)}, u32[]{:S(2)}) collective-permute-start(bf16[128,2048]{1,0:T(8,128)(2,1)S(1)} %get-tuple-element.18), channel_id=1, source_target_pairs={{0,2},{1,3},{2,0},{3,1},{4,6},{5,7},{6,4},{7,5},{8,10},{9,11},{10,... | collective-permute-start | bytes 1572872 | tf_op jit(solution)/shard_map/ppermute | solution.py:24

commit v2 on v0

--- a/solution.py
+++ b/solution.py
@@ -24,30 +24,11 @@
     return lax.ppermute(block, "member", partners(lax.axis_size("member"), step))
 
 
-def cut_kernel(first, pos_ref, state_ref, out_ref, sem):
-    width = out_ref.shape[1]
-    start = pl.multiple_of(first(pos_ref[0]) * width, LANES)
-    copy = pltpu.make_async_copy(state_ref.at[:, pl.ds(start, width)], out_ref, sem)
-    copy.start()
-    copy.wait()
-
-
 def cut(position, state, step, chunk, count):
     rows, total = state.shape
     width = total // (count * CHUNKS)
-    return pl.pallas_call(
-        functools.partial(cut_kernel, lambda pos: (pos ^ step) * CHUNKS + chunk),
-        in_specs=[
-            pl.BlockSpec(memory_space=pltpu.SMEM),
-            pl.BlockSpec(memory_space=pl.ANY),
-        ],
-        out_specs=pl.BlockSpec(memory_space=pltpu.VMEM),
-        scratch_shapes=[pltpu.SemaphoreType.DMA],
-        out_shape=jax.ShapeDtypeStruct((rows, width), state.dtype),
-        cost_estimate=pl.CostEstimate(
-            flops=0, transcendentals=0, bytes_accessed=2 * rows * width
-        ),
-    )(position, state)
+    start = ((position[0] ^ step) * CHUNKS + chunk) * width
+    return lax.dynamic_slice(state, (0, start), (rows, width))
 
 
 def pick_kernel(pos_ref, start_ref, index_ref, own_ref, low_ref, high_ref, out_ref, pair_ref, pool):
@@ -241,10 +222,19 @@
     position = lax.axis_index("member").astype(jnp.int32).reshape(1)
     steps = send_order(count)
 
-    def send_chunk(chunk):
-        return {step: swap(cut(position, state, step, chunk, count), step) for step in steps}
-
-    arrived = [send_chunk(0)]
+    source = state
+
+    def send_chunk(chunk, order):
+        nonlocal source
+        sent = {}
+        for step in order:
+            piece = cut(position, source, step, chunk, count)
+            source, piece = lax.optimization_barrier((source, piece))
+            sent[step] = swap(piece, step)
+        return sent
+
+    arrived = [send_chunk(0, steps[:1])]
+    arrived[0] |= send_chunk(0, steps[1:])
 
     pad = jnp.zeros((14, hx.shape[1]), hx.dtype)
     stacked = jnp.concatenate([hx, obs_value[None], obs_rinv[None], pad], axis=0)
@@ -257,17 +247,19 @@
     obs_block = jnp.concatenate([picked[0]] + [others[s] for s in range(1, count)], axis=0)
 
     for chunk in range(1, CHUNKS):
-        arrived.append(send_chunk(chunk))
+        arrived.append(send_chunk(chunk, steps))
 
     transform = analysis(obs_block, obs_pair, loc_weight[0])
 
     buffer, returned = None, []
+    back = steps[:0:-1] + steps[:1]
     for chunk in range(CHUNKS):
         received = [arrived[chunk][step] for step in range(1, count)]
         buffer, *others = update_state(position, transform, state, received, chunk, buffer)
-        returned.append({step: swap(others[step - 1], step) for step in steps})
+        returned.append({step: swap(others[step - 1], step) for step in back[:-1]})
+        returned[-1][back[-1]] = swap(others[back[-1] - 1], back[-1])
     for chunk in range(CHUNKS):
-        for step in steps:
+        for step in back:
             buffer = place(position, buffer, returned[chunk][step], step, chunk)
     return buffer
 

time: 221 us -> 224 us (1.014)
  the two profiles are of different devices: /device:TPU:0 before, /device:TPU:21 now
where the time goes in v2:
time: 224 us; the launch traced here: 223 us
  waiting for transfers between devices  155 us (69%)
  Pallas kernels  19.8 us (9%)
  starting transfers between devices  19.1 us (9%)
  local copies, waits for them, and re-layouts  13.9 us (6%)
  matrix products  12.5 us (6%)
    ppermute x15, waiting for transfers between devices, swap(): lax.ppermute(block, 'member', partners(lax.axis_size('member'), step))  155 us
    ppermute x15, starting transfers between devices, swap(): lax.ppermute(block, 'member', partners(lax.axis_size('member'), step))  17.2 us
    dynamic_slice x6, local copies, waits for them, and re-layouts, cut(): return lax.dynamic_slice(state, (0, start), (rows, width))  11.4 us
    dot_general x8, matrix products, product(): lax.dot_general(left, right, (dims, ((), ())), preferred_element_type=jnp...  10.2 us
    pallas_call x1, Pallas kernels, pick(): pl.pallas_call(pick_kernel, grid_spec=pltpu.PrefetchScalarGridSpec(num_sc...  8.61 us
    pallas_call x2, Pallas kernels, update_state(): pl.pallas_call(functools.partial(update_kernel, count, aliased), grid_spe...  6.33 us
    pallas_call x6, Pallas kernels, place(): pl.pallas_call(functools.partial(place_kernel, lambda pos: (pos ^ step) *...  4.82 us
  transfers between devices with their start and end apart: 17, of which 9 were waited for; matrix products, arithmetic and copies ran while one was open for 11% of the time, Pallas kernels for 8%

profile of v2, /device:TPU:21, one launch (start us, length us, event | category | flops | bytes accessed | tf_op | source)
XLA Modules:
  0.0 223.3 jit_solution(14037649422676872238)
XLA Ops:
  0.0 0.7 broadcast_in_dim.12
  0.7 0.7 broadcast_in_dim.13
  1.4 0.1 pad.7.clone
  1.5 1.5 maximum_maximum_fusion.own_ref
  3.1 0.7 collective-permute-start.1
  3.8 1.2 collective-permute-start
  5.0 1.9 constant_dynamic-slice_fusion.5
  6.9 1.9 constant_dynamic-slice_fusion.4
  8.8 1.9 constant_dynamic-slice_fusion.3
  10.7 1.9 constant_dynamic-slice_fusion.2
  12.6 1.9 constant_dynamic-slice_fusion.1
  14.5 1.9 constant_dynamic-slice_fusion
  16.3 0.1 collective-permute-start.6
  16.4 1.3 collective-permute-start.5
  17.7 0.1 reduce_min.9
  17.9 0.0 collective-permute-done.low_ref
  17.9 8.6 %shard_map.64 = (bf16[4,128,1024]{2,1,0:T(8,128)(2,1)S(1)}, bf16[16,1024]{1,0:T(8,128)(2,1)S(1)}) custom-call(s32[1]{0:T(128)} %bitcast.pos_ref, s32[4]{0:T(128)S(1)} %multiply_minimum_fusion.start_ref, s32[4,1,1024]{2,1,0:T(1,128)S(1)} %reshape.16.index_ref, bf16[144,4096]{1,0:T(8,128)(2,1)S(1)} %maximum_maximum_fusion.own_ref, ...), custom_call_target="tpu_custom_call" | custom-call | flops 2566914048 | bytes 2359296 | tf_op jit(solution)/shard_map/pallas_call | solution.py:66
  26.5 0.0 copy-start.10
  26.5 0.1 slice_bitcast_fusion.3
  26.6 1.4 collective-permute-start.4
  27.9 1.1 collective-permute-start.3
  29.0 1.1 collective-permute-start.2
  30.2 29.3 %collective-permute-done.4 = bf16[128,1024]{1,0:T(8,128)(2,1)S(1)} collective-permute-done((bf16[128,1024]{1,0:T(8,128)(2,1)S(1)}, bf16[128,1024]{1,0:T(8,128)(2,1)S(1)}, u32[]{:S(2)}, u32[]{:S(2)}) %collective-permute-start.4) | collective-permute-done | bytes 262176 | tf_op jit(solution)/shard_map/ppermute | solution.py:24
  59.5 0.0 collective-permute-start.9
  59.5 13.6 %collective-permute-done.3 = bf16[128,1024]{1,0:T(8,128)(2,1)S(1)} collective-permute-done((bf16[128,1024]{1,0:T(8,128)(2,1)S(1)}, bf16[128,1024]{1,0:T(8,128)(2,1)S(1)}, u32[]{:S(2)}, u32[]{:S(2)}) %collective-permute-start.3) | collective-permute-done | bytes 262176 | tf_op jit(solution)/shard_map/ppermute | solution.py:24
  73.2 4.4 %collective-permute-start.8 = (bf16[128,2048]{1,0:T(8,128)(2,1)}, bf16[128,2048]{1,0:T(8,128)(2,1)S(1)}, u32[]{:S(2)}, u32[]{:S(2)}) collective-permute-start(bf16[128,2048]{1,0:T(8,128)(2,1)} %constant_dynamic-slice_fusion.4), channel_id=1, source_target_pairs={{0,1},{1,0},{2,3},{3,2},{4,5},{5,4},{6,7},{7,6},{8,9},{9,8},{10,11... | collective-permute-start | bytes 1572872 | tf_op jit(solution)/shard_map/ppermute | solution.py:24
  77.6 0.2 convert_reduce_fusion
  77.8 2.4 %multiply_reduce_fusion = (f32[]{:T(128)}, f32[512,512]{1,0:T(8,128)}) fusion(f32[1024]{0:T(1024)S(1)} %bitcast.38, f32[1024]{0:T(1024)S(1)} %get-tuple-element.54, bf16[128,1024]{1,0:T(8,128)(2,1)S(1)} %collective-permute-done.4, bf16[128,1024]{1,0:T(8,128)(2,1)S(1)} %collective-permute-done.3, bf16[128,1024]{1,0:T(8,128)(2,1)S(1)} %collective-permute-done.2, ...), kind=kOutput, calls=%fused_computation.25 | convolution fusion | flops 543948800 | bytes 2105348 | tf_op jit(solution)/shard_map/dot_general | solution.py:177
  80.9 0.0 copy-start.12
  80.9 1.8 fusion.2
  82.7 0.4 convolution_convert_fusion.2
  83.1 0.0 copy-start.11
  83.1 0.4 convolution_convert_fusion.3
  83.5 0.4 fusion.3
  84.0 0.8 copy-done.1
  84.8 0.4 convolution_convert_fusion.1
  85.2 2.8 %fusion.4 = bf16[512,512]{1,0:T(8,128)(2,1)} fusion(bf16[512,512]{1,0:T(8,128)(2,1)S(1)} %convolution_convert_fusion.1, bf16[512,512]{1,0:T(8,128)(2,1)} %copy-done.11, bf16[512,512]{1,0:T(8,128)(2,1)} %copy-done.1), kind=kOutput, calls=%fused_computation.18 | convolution fusion | flops 538443776 | bytes 2097152 | tf_op jit(solution)/shard_map/dot_general | solution.py:177
  88.0 1.6 convolution_divide_fusion
  89.6 0.0 copy-start
  89.7 0.9 convolution_bitcast_fusion.1
  90.6 0.7 convolution_bitcast_fusion
  91.2 0.7 fusion.9
  91.9 0.1 copy-done.2
  92.0 1.5 collective-permute-start.7
  93.4 0.1 fusion.7.transform_ref
  93.6 26.8 %collective-permute-done.8.refs_1_ = bf16[128,2048]{1,0:T(8,128)(2,1)S(1)} collective-permute-done((bf16[128,2048]{1,0:T(8,128)(2,1)}, bf16[128,2048]{1,0:T(8,128)(2,1)S(1)}, u32[]{:S(2)}, u32[]{:S(2)}) %collective-permute-start.8) | collective-permute-done | bytes 524320 | tf_op jit(solution)/shard_map/ppermute | solution.py:24
  120.3 1.0 collective-permute-done.10.refs_3_
  121.3 3.2 %shard_map.65 = (bf16[128,16384]{1,0:T(8,128)(2,1)}, bf16[128,2048]{1,0:T(8,128)(2,1)S(1)}, bf16[128,2048]{1,0:T(8,128)(2,1)S(1)}, bf16[128,2048]{1,0:T(8,128)(2,1)S(1)}) custom-call(s32[1]{0:T(128)} %bitcast.pos_ref, bf16[512,512]{1,0:T(8,128)(2,1)S(1)} %fusion.7.transform_ref, bf16[128,16384]{1,0:T(8,128)(2,1)S(1)} %copy-done, ...), custom_call_target="tpu_custom_call" | custom-call | flops 1073741824 | bytes 4718592 | tf_op jit(solution)/shard_map/pallas_call | solution.py:125
  124.5 2.3 %collective-permute-start.14 = (bf16[128,2048]{1,0:T(8,128)(2,1)S(1)}, bf16[128,2048]{1,0:T(8,128)(2,1)S(1)}, u32[]{:S(2)}, u32[]{:S(2)}) collective-permute-start(bf16[128,2048]{1,0:T(8,128)(2,1)S(1)} %get-tuple-element.43), channel_id=1, source_target_pairs={{0,3},{1,2},{2,1},{3,0},{4,7},{5,6},{6,5},{7,4},{8,11},{9,10},{10,... | collective-permute-start | bytes 1572872 | tf_op jit(solution)/shard_map/ppermute | solution.py:24
  126.8 1.3 collective-permute-start.15
  128.1 27.0 %collective-permute-done.7.refs_3_ = bf16[128,2048]{1,0:T(8,128)(2,1)S(1)} collective-permute-done((bf16[128,2048]{1,0:T(8,128)(2,1)S(1)}, bf16[128,2048]{1,0:T(8,128)(2,1)S(1)}, u32[]{:S(2)}, u32[]{:S(2)}) %collective-permute-start.7) | collective-permute-done | bytes 524320 | tf_op jit(solution)/shard_map/ppermute | solution.py:24
  155.0 3.2 %shard_map.66 = (bf16[128,16384]{1,0:T(8,128)(2,1)}, bf16[128,2048]{1,0:T(8,128)(2,1)S(1)}, bf16[128,2048]{1,0:T(8,128)(2,1)S(1)}, bf16[128,2048]{1,0:T(8,128)(2,1)S(1)}) custom-call(s32[1]{0:T(128)} %bitcast.pos_ref, bf16[512,512]{1,0:T(8,128)(2,1)S(1)} %fusion.7.transform_ref, bf16[128,16384]{1,0:T(8,128)(2,1)S(1)} %copy-done, ...), custom_call_target="tpu_custom_call", output_to_operand_aliasing={{0}: (6, {})} | custom-call | flops 1073741824 | bytes 4718592 | tf_op jit(solution)/shard_map/pallas_call | solution.py:125
  158.2 0.4 collective-permute-start.12
  158.7 15.7 %collective-permute-done.16.piece_ref = bf16[128,2048]{1,0:T(8,128)(2,1)S(1)} collective-permute-done((bf16[128,2048]{1,0:T(8,128)(2,1)S(1)}, bf16[128,2048]{1,0:T(8,128)(2,1)S(1)}, u32[]{:S(2)}, u32[]{:S(2)}) %collective-permute-start.16) | collective-permute-done | bytes 524320 | tf_op jit(solution)/shard_map/ppermute | solution.py:24
  174.4 2.4 %collective-permute-start.11 = (bf16[128,2048]{1,0:T(8,128)(2,1)S(1)}, bf16[128,2048]{1,0:T(8,128)(2,1)S(1)}, u32[]{:S(2)}, u32[]{:S(2)}) collective-permute-start(bf16[128,2048]{1,0:T(8,128)(2,1)S(1)} %get-tuple-element.40), channel_id=1, source_target_pairs={{0,3},{1,2},{2,1},{3,0},{4,7},{5,6},{6,5},{7,4},{8,11},{9,10},{10,... | collective-permute-start | bytes 1572872 | tf_op jit(solution)/shard_map/ppermute | solution.py:24
  176.8 0.8 shard_map.67.buffer_ref
  177.6 0.8 shard_map.68.buffer_ref
  178.4 21.6 %collective-permute-done.14.piece_ref = bf16[128,2048]{1,0:T(8,128)(2,1)S(1)} collective-permute-done((bf16[128,2048]{1,0:T(8,128)(2,1)S(1)}, bf16[128,2048]{1,0:T(8,128)(2,1)S(1)}, u32[]{:S(2)}, u32[]{:S(2)}) %collective-permute-start.14) | collective-permute-done | bytes 524320 | tf_op jit(solution)/shard_map/ppermute | solution.py:24
  200.0 0.8 shard_map.69.buffer_ref
  200.8 7.3 %collective-permute-done.13.piece_ref = bf16[128,2048]{1,0:T(8,128)(2,1)S(1)} collective-permute-done((bf16[128,2048]{1,0:T(8,128)(2,1)S(1)}, bf16[128,2048]{1,0:T(8,128)(2,1)S(1)}, u32[]{:S(2)}, u32[]{:S(2)}) %collective-permute-start.13) | collective-permute-done | bytes 524320 | tf_op jit(solution)/shard_map/ppermute | solution.py:24
  208.1 0.8 shard_map.70.buffer_ref
  208.9 0.8 shard_map.71.buffer_ref
  209.7 12.8 %collective-permute-done.11.piece_ref = bf16[128,2048]{1,0:T(8,128)(2,1)S(1)} collective-permute-done((bf16[128,2048]{1,0:T(8,128)(2,1)S(1)}, bf16[128,2048]{1,0:T(8,128)(2,1)S(1)}, u32[]{:S(2)}, u32[]{:S(2)}) %collective-permute-start.11) | collective-permute-done | bytes 524320 | tf_op jit(solution)/shard_map/ppermute | solution.py:24
  222.5 0.8 shard_map.72
  (37 shorter events, 0.2 us)
Async XLA Ops:
  3.1 14.8 %collective-permute-start.1 = (bf16[144,1024]{1,0:T(8,128)(2,1)S(1)}, bf16[144,1024]{1,0:T(8,128)(2,1)S(1)}, u32[]{:S(2)}, u32[]{:S(2)}) collective-permute-start(bf16[144,1024]{1,0:T(8,128)(2,1)S(1)} %get-tuple-element.47), channel_id=1, source_target_pairs={{0,28},{4,0},{8,4},{12,8},{16,12},{20,16},{24,20},{28,24},{1,29},{... | collective-permute-start | bytes 884744 | tf_op jit(solution)/shard_map/ppermute | solution.py:212
  3.8 14.0 %collective-permute-start = (bf16[144,1024]{1,0:T(8,128)(2,1)S(1)}, bf16[144,1024]{1,0:T(8,128)(2,1)S(1)}, u32[]{:S(2)}, u32[]{:S(2)}) collective-permute-start(bf16[144,1024]{1,0:T(8,128)(2,1)S(1)} %get-tuple-element.48), channel_id=1, source_target_pairs={{0,4},{4,8},{8,12},{12,16},{16,20},{20,24},{24,28},{28,0},{1,5},{5... | collective-permute-start | bytes 884744 | tf_op jit(solution)/shard_map/ppermute | solution.py:212
  8.7 8.9 %copy-start.9 = (s32[4,1024]{1,0:T(4,128)S(1)}, s32[4,1024]{1,0:T(4,128)}, u32[]{:S(2)}) copy-start(s32[4,1024]{1,0:T(4,128)} %param.9) | copy-start | bytes 49156
  16.3 110.4 %collective-permute-start.6 = (bf16[128,2048]{1,0:T(8,128)(2,1)}, bf16[128,2048]{1,0:T(8,128)(2,1)S(1)}, u32[]{:S(2)}, u32[]{:S(2)}) collective-permute-start(bf16[128,2048]{1,0:T(8,128)(2,1)} %constant_dynamic-slice_fusion), channel_id=1, source_target_pairs={{0,2},{1,3},{2,0},{3,1},{4,6},{5,7},{6,4},{7,5},{8,10},{9,11},{10,... | collective-permute-start | bytes 1572872 | tf_op jit(solution)/shard_map/ppermute | solution.py:24
  16.4 111.7 %collective-permute-start.5 = (bf16[128,2048]{1,0:T(8,128)(2,1)}, bf16[128,2048]{1,0:T(8,128)(2,1)S(1)}, u32[]{:S(2)}, u32[]{:S(2)}) collective-permute-start(bf16[128,2048]{1,0:T(8,128)(2,1)} %constant_dynamic-slice_fusion.1), channel_id=1, source_target_pairs={{0,1},{1,0},{2,3},{3,2},{4,5},{5,4},{6,7},{7,6},{8,9},{9,8},{10,11... | collective-permute-start | bytes 1572872 | tf_op jit(solution)/shard_map/ppermute | solution.py:24
  26.5 3.7 %copy-start.10 = (f32[1,1024]{1,0:T(1,128)S(1)}, f32[1,1024]{1,0:T(1,128)}, u32[]{:S(2)}) copy-start(f32[1,1024]{1,0:T(1,128)} %param.10) | copy-start | bytes 12292
  26.6 32.9 %collective-permute-start.4 = (bf16[128,1024]{1,0:T(8,128)(2,1)S(1)}, bf16[128,1024]{1,0:T(8,128)(2,1)S(1)}, u32[]{:S(2)}, u32[]{:S(2)}) collective-permute-start(bf16[128,1024]{1,0:T(8,128)(2,1)S(1)} %get-tuple-element.50), channel_id=1, source_target_pairs={{0,3},{1,2},{2,1},{3,0},{4,7},{5,6},{6,5},{7,4},{8,11},{9,10},{10,... | collective-permute-start | bytes 786440 | tf_op jit(solution)/shard_map/ppermute | solution.py:24
  27.9 45.2 %collective-permute-start.3 = (bf16[128,1024]{1,0:T(8,128)(2,1)S(1)}, bf16[128,1024]{1,0:T(8,128)(2,1)S(1)}, u32[]{:S(2)}, u32[]{:S(2)}) collective-permute-start(bf16[128,1024]{1,0:T(8,128)(2,1)S(1)} %get-tuple-element.51), channel_id=1, source_target_pairs={{0,2},{1,3},{2,0},{3,1},{4,6},{5,7},{6,4},{7,5},{8,10},{9,11},{10,... | collective-permute-start | bytes 786440 | tf_op jit(solution)/shard_map/ppermute | solution.py:24
  29.0 48.5 %collective-permute-start.2 = (bf16[128,1024]{1,0:T(8,128)(2,1)S(1)}, bf16[128,1024]{1,0:T(8,128)(2,1)S(1)}, u32[]{:S(2)}, u32[]{:S(2)}) collective-permute-start(bf16[128,1024]{1,0:T(8,128)(2,1)S(1)} %get-tuple-element.52), channel_id=1, source_target_pairs={{0,1},{1,0},{2,3},{3,2},{4,5},{5,4},{6,7},{7,6},{8,9},{9,8},{10,11... | collective-permute-start | bytes 786440 | tf_op jit(solution)/shard_map/ppermute | solution.py:24
  59.5 20.6 %copy-start.3 = (bf16[128,1024]{1,0:T(8,128)(2,1)}, bf16[128,1024]{1,0:T(8,128)(2,1)S(1)}, u32[]{:S(2)}) copy-start(bf16[128,1024]{1,0:T(8,128)(2,1)S(1)} %collective-permute-done.4) | copy-start | bytes 786436
  59.5 32.4 %collective-permute-start.9 = (bf16[128,2048]{1,0:T(8,128)(2,1)}, bf16[128,2048]{1,0:T(8,128)(2,1)S(1)}, u32[]{:S(2)}, u32[]{:S(2)}) collective-permute-start(bf16[128,2048]{1,0:T(8,128)(2,1)} %constant_dynamic-slice_fusion.3), channel_id=1, source_target_pairs={{0,2},{1,3},{2,0},{3,1},{4,6},{5,7},{6,4},{7,5},{8,10},{9,11},{10,... | collective-permute-start | bytes 1572872 | tf_op jit(solution)/shard_map/ppermute | solution.py:24
  73.2 7.0 %copy-start.5 = (bf16[128,1024]{1,0:T(8,128)(2,1)}, bf16[128,1024]{1,0:T(8,128)(2,1)S(1)}, u32[]{:S(2)}) copy-start(bf16[128,1024]{1,0:T(8,128)(2,1)S(1)} %collective-permute-done.3) | copy-start | bytes 786436
  73.2 47.2 %collective-permute-start.8 = (bf16[128,2048]{1,0:T(8,128)(2,1)}, bf16[128,2048]{1,0:T(8,128)(2,1)S(1)}, u32[]{:S(2)}, u32[]{:S(2)}) collective-permute-start(bf16[128,2048]{1,0:T(8,128)(2,1)} %constant_dynamic-slice_fusion.4), channel_id=1, source_target_pairs={{0,1},{1,0},{2,3},{3,2},{4,5},{5,4},{6,7},{7,6},{8,9},{9,8},{10,11... | collective-permute-start | bytes 1572872 | tf_op jit(solution)/shard_map/ppermute | solution.py:24
  77.5 2.6 %copy-start.7 = (bf16[128,1024]{1,0:T(8,128)(2,1)}, bf16[128,1024]{1,0:T(8,128)(2,1)S(1)}, u32[]{:S(2)}) copy-start(bf16[128,1024]{1,0:T(8,128)(2,1)S(1)} %collective-permute-done.2) | copy-start | bytes 786436
  77.5 43.8 %collective-permute-start.10 = (bf16[128,2048]{1,0:T(8,128)(2,1)}, bf16[128,2048]{1,0:T(8,128)(2,1)S(1)}, u32[]{:S(2)}, u32[]{:S(2)}) collective-permute-start(bf16[128,2048]{1,0:T(8,128)(2,1)} %constant_dynamic-slice_fusion.5), channel_id=1, source_target_pairs={{0,3},{1,2},{2,1},{3,0},{4,7},{5,6},{6,5},{7,4},{8,11},{9,10},{10,... | collective-permute-start | bytes 1572872 | tf_op jit(solution)/shard_map/ppermute | solution.py:24
  80.9 1.8 copy-start.12
  83.1 0.9 copy-start.11
  84.0 0.8 copy-start.1
  88.0 1.6 copy-start.4
  88.0 1.6 copy-start.6
  88.0 1.6 copy-start.8
  89.6 31.7 %copy-start = (bf16[128,16384]{1,0:T(8,128)(2,1)S(1)}, bf16[128,16384]{1,0:T(8,128)(2,1)}, u32[]{:S(2)}) copy-start(bf16[128,16384]{1,0:T(8,128)(2,1)} %refs_0_.3) | copy-start | bytes 12582916
  90.6 1.4 copy-start.2
  92.0 63.1 %collective-permute-start.7 = (bf16[128,2048]{1,0:T(8,128)(2,1)S(1)}, bf16[128,2048]{1,0:T(8,128)(2,1)S(1)}, u32[]{:S(2)}, u32[]{:S(2)}) collective-permute-start(bf16[128,2048]{1,0:T(8,128)(2,1)S(1)} %copy-done.2), channel_id=1, source_target_pairs={{0,3},{1,2},{2,1},{3,0},{4,7},{5,6},{6,5},{7,4},{8,11},{9,10},{10,... | collective-permute-start | bytes 1572872 | tf_op jit(solution)/shard_map/ppermute | solution.py:24
  124.5 49.9 %collective-permute-start.16 = (bf16[128,2048]{1,0:T(8,128)(2,1)S(1)}, bf16[128,2048]{1,0:T(8,128)(2,1)S(1)}, u32[]{:S(2)}, u32[]{:S(2)}) collective-permute-start(bf16[128,2048]{1,0:T(8,128)(2,1)S(1)} %get-tuple-element.45), channel_id=1, source_target_pairs={{0,2},{1,3},{2,0},{3,1},{4,6},{5,7},{6,4},{7,5},{8,10},{9,11},{10,... | collective-permute-start | bytes 1572872 | tf_op jit(solution)/shard_map/ppermute | solution.py:24
  124.5 75.5 %collective-permute-start.14 = (bf16[128,2048]{1,0:T(8,128)(2,1)S(1)}, bf16[128,2048]{1,0:T(8,128)(2,1)S(1)}, u32[]{:S(2)}, u32[]{:S(2)}) collective-permute-start(bf16[128,2048]{1,0:T(8,128)(2,1)S(1)} %get-tuple-element.43), channel_id=1, source_target_pairs={{0,3},{1,2},{2,1},{3,0},{4,7},{5,6},{6,5},{7,4},{8,11},{9,10},{10,... | collective-permute-start | bytes 1572872 | tf_op jit(solution)/shard_map/ppermute | solution.py:24
  126.8 50.8 %collective-permute-start.15 = (bf16[128,2048]{1,0:T(8,128)(2,1)S(1)}, bf16[128,2048]{1,0:T(8,128)(2,1)S(1)}, u32[]{:S(2)}, u32[]{:S(2)}) collective-permute-start(bf16[128,2048]{1,0:T(8,128)(2,1)S(1)} %get-tuple-element.44), channel_id=1, source_target_pairs={{0,1},{1,0},{2,3},{3,2},{4,5},{5,4},{6,7},{7,6},{8,9},{9,8},{10,11... | collective-permute-start | bytes 1572872 | tf_op jit(solution)/shard_map/ppermute | solution.py:24
  158.2 49.9 %collective-permute-start.13 = (bf16[128,2048]{1,0:T(8,128)(2,1)S(1)}, bf16[128,2048]{1,0:T(8,128)(2,1)S(1)}, u32[]{:S(2)}, u32[]{:S(2)}) collective-permute-start(bf16[128,2048]{1,0:T(8,128)(2,1)S(1)} %get-tuple-element.42), channel_id=1, source_target_pairs={{0,2},{1,3},{2,0},{3,1},{4,6},{5,7},{6,4},{7,5},{8,10},{9,11},{10,... | collective-permute-start | bytes 1572872 | tf_op jit(solution)/shard_map/ppermute | solution.py:24
  158.2 50.7 %collective-permute-start.12 = (bf16[128,2048]{1,0:T(8,128)(2,1)S(1)}, bf16[128,2048]{1,0:T(8,128)(2,1)S(1)}, u32[]{:S(2)}, u32[]{:S(2)}) collective-permute-start(bf16[128,2048]{1,0:T(8,128)(2,1)S(1)} %get-tuple-element.41), channel_id=1, source_target_pairs={{0,1},{1,0},{2,3},{3,2},{4,5},{5,4},{6,7},{7,6},{8,9},{9,8},{10,11... | collective-permute-start | bytes 1572872 | tf_op jit(solution)/shard_map/ppermute | solution.py:24
  174.4 48.1 %collective-permute-start.11 = (bf16[128,2048]{1,0:T(8,128)(2,1)S(1)}, bf16[128,2048]{1,0:T(8,128)(2,1)S(1)}, u32[]{:S(2)}, u32[]{:S(2)}) collective-permute-start(bf16[128,2048]{1,0:T(8,128)(2,1)S(1)} %get-tuple-element.40), channel_id=1, source_target_pairs={{0,3},{1,2},{2,1},{3,0},{4,7},{5,6},{6,5},{7,4},{8,11},{9,10},{10,... | collective-permute-start | bytes 1572872 | tf_op jit(solution)/shard_map/ppermute | solution.py:24

commit v3 on v2

--- a/solution.py
+++ b/solution.py
@@ -24,11 +24,12 @@
     return lax.ppermute(block, "member", partners(lax.axis_size("member"), step))
 
 
-def cut(position, state, step, chunk, count):
+def cut(position, state, step, chunk, count, part=(0, 1)):
     rows, total = state.shape
     width = total // (count * CHUNKS)
-    start = ((position[0] ^ step) * CHUNKS + chunk) * width
-    return lax.dynamic_slice(state, (0, start), (rows, width))
+    low, high = int(part[0] * width), int(part[1] * width)
+    start = ((position[0] ^ step) * CHUNKS + chunk) * width + low
+    return lax.dynamic_slice(state, (0, start), (rows, high - low))
 
 
 def pick_kernel(pos_ref, start_ref, index_ref, own_ref, low_ref, high_ref, out_ref, pair_ref, pool):
@@ -224,17 +225,19 @@
 
     source = state
 
+    def send(chunk, step, part=(0, 1)):
+        nonlocal source
+        piece = cut(position, source, step, chunk, count, part)
+        source, piece = lax.optimization_barrier((source, piece))
+        return swap(piece, step)
+
     def send_chunk(chunk, order):
-        nonlocal source
-        sent = {}
-        for step in order:
-            piece = cut(position, source, step, chunk, count)
-            source, piece = lax.optimization_barrier((source, piece))
-            sent[step] = swap(piece, step)
-        return sent
-
-    arrived = [send_chunk(0, steps[:1])]
-    arrived[0] |= send_chunk(0, steps[1:])
+        return {step: send(chunk, step) for step in order}
+
+    head = send(0, steps[0], (0, 0.25))
+    rest = send(0, steps[0], (0.25, 1))
+    arrived = [send_chunk(0, steps[1:])]
+    arrived[0][steps[0]] = jnp.concatenate([head, rest], axis=1)
 
     pad = jnp.zeros((14, hx.shape[1]), hx.dtype)
     stacked = jnp.concatenate([hx, obs_value[None], obs_rinv[None], pad], axis=0)

time: 224 us -> 218 us (0.973)
  the two profiles are of different devices: /device:TPU:21 before, /device:TPU:13 now
where the time goes in v3:
time: 218 us; the launch traced here: 217 us
  waiting for transfers between devices  144 us (66%)
  starting transfers between devices  23 us (11%)
  Pallas kernels  19.8 us (9%)
  local copies, waits for them, and re-layouts  13.9 us (6%)
  matrix products  13.6 us (6%)
    ppermute x16, waiting for transfers between devices, swap(): lax.ppermute(block, 'member', partners(lax.axis_size('member'), step))  144 us
    ppermute x16, starting transfers between devices, swap(): lax.ppermute(block, 'member', partners(lax.axis_size('member'), step))  20.6 us
    dynamic_slice x7, local copies, waits for them, and re-layouts, cut(): return lax.dynamic_slice(state, (0, start), (rows, high - low))  11.4 us
    dot_general x8, matrix products, product(): lax.dot_general(left, right, (dims, ((), ())), preferred_element_type=jnp...  11.4 us
    pallas_call x1, Pallas kernels, pick(): pl.pallas_call(pick_kernel, grid_spec=pltpu.PrefetchScalarGridSpec(num_sc...  8.61 us
    pallas_call x2, Pallas kernels, update_state(): pl.pallas_call(functools.partial(update_kernel, count, aliased), grid_spe...  6.33 us
    pallas_call x6, Pallas kernels, place(): pl.pallas_call(functools.partial(place_kernel, lambda pos: (pos ^ step) *...  4.82 us
  transfers between devices with their start and end apart: 18, of which 7 were waited for; matrix products, arithmetic and copies ran while one was open for 13% of the time, Pallas kernels for 9%

profile of v3, /device:TPU:13, one launch (start us, length us, event | category | flops | bytes accessed | tf_op | source)
XLA Modules:
  0.0 217.0 jit_solution(96385946732988579)
XLA Ops:
  0.0 0.9 constant_dynamic-slice_fusion.6
  0.9 1.4 collective-permute-start.10
  2.3 1.0 constant_dynamic-slice_fusion.5
  3.3 0.2 collective-permute-start.11
  3.5 0.7 broadcast_in_dim.12
  4.2 0.7 broadcast_in_dim.13
  5.0 0.1 pad.9.clone
  5.0 1.5 maximum_maximum_fusion.own_ref
  6.6 1.3 collective-permute-start.1
  7.9 1.2 collective-permute-start
  9.1 1.9 constant_dynamic-slice_fusion.4
  11.0 1.9 constant_dynamic-slice_fusion.3
  12.9 1.9 constant_dynamic-slice_fusion.2
  14.8 1.9 constant_dynamic-slice_fusion.1
  16.6 1.9 constant_dynamic-slice_fusion
  18.6 0.1 reduce_min.9
  18.7 8.6 %shard_map.64 = (bf16[4,128,1024]{2,1,0:T(8,128)(2,1)S(1)}, bf16[16,1024]{1,0:T(8,128)(2,1)S(1)}) custom-call(s32[1]{0:T(128)} %bitcast.pos_ref, s32[4]{0:T(128)S(1)} %multiply_minimum_fusion.start_ref, s32[4,1,1024]{2,1,0:T(1,128)S(1)} %reshape.16.index_ref, bf16[144,4096]{1,0:T(8,128)(2,1)S(1)} %maximum_maximum_fusion.own_ref, ...), custom_call_target="tpu_custom_call" | custom-call | flops 2566914048 | bytes 2359296 | tf_op jit(solution)/shard_map/pallas_call | solution.py:67
  27.3 0.0 copy-start.9
  27.3 0.1 slice_bitcast_fusion.3
  27.4 1.4 collective-permute-start.4
  28.8 2.9 %collective-permute-start.3 = (bf16[128,1024]{1,0:T(8,128)(2,1)S(1)}, bf16[128,1024]{1,0:T(8,128)(2,1)S(1)}, u32[]{:S(2)}, u32[]{:S(2)}) collective-permute-start(bf16[128,1024]{1,0:T(8,128)(2,1)S(1)} %get-tuple-element.55), channel_id=1, source_target_pairs={{0,2},{1,3},{2,0},{3,1},{4,6},{5,7},{6,4},{7,5},{8,10},{9,11},{10,... | collective-permute-start | bytes 786440 | tf_op jit(solution)/shard_map/ppermute | solution.py:24
  31.7 1.1 collective-permute-start.2
  32.8 0.0 collective-permute-done.10
  32.8 2.4 %collective-permute-start.6 = (bf16[128,2048]{1,0:T(8,128)(2,1)}, bf16[128,2048]{1,0:T(8,128)(2,1)S(1)}, u32[]{:S(2)}, u32[]{:S(2)}) collective-permute-start(bf16[128,2048]{1,0:T(8,128)(2,1)} %constant_dynamic-slice_fusion), channel_id=1, source_target_pairs={{0,2},{1,3},{2,0},{3,1},{4,6},{5,7},{6,4},{7,5},{8,10},{9,11},{10,... | collective-permute-start | bytes 1572872 | tf_op jit(solution)/shard_map/ppermute | solution.py:24
  35.3 0.0 collective-permute-start.5
  35.3 11.7 %collective-permute-done.4 = bf16[128,1024]{1,0:T(8,128)(2,1)S(1)} collective-permute-done((bf16[128,1024]{1,0:T(8,128)(2,1)S(1)}, bf16[128,1024]{1,0:T(8,128)(2,1)S(1)}, u32[]{:S(2)}, u32[]{:S(2)}) %collective-permute-start.4) | collective-permute-done | bytes 262176 | tf_op jit(solution)/shard_map/ppermute | solution.py:24
  47.0 1.3 collective-permute-start.7
  48.3 14.7 %collective-permute-done.3 = bf16[128,1024]{1,0:T(8,128)(2,1)S(1)} collective-permute-done((bf16[128,1024]{1,0:T(8,128)(2,1)S(1)}, bf16[128,1024]{1,0:T(8,128)(2,1)S(1)}, u32[]{:S(2)}, u32[]{:S(2)}) %collective-permute-start.3) | collective-permute-done | bytes 262176 | tf_op jit(solution)/shard_map/ppermute | solution.py:24
  63.0 3.1 %collective-permute-start.9 = (bf16[128,2048]{1,0:T(8,128)(2,1)}, bf16[128,2048]{1,0:T(8,128)(2,1)S(1)}, u32[]{:S(2)}, u32[]{:S(2)}) collective-permute-start(bf16[128,2048]{1,0:T(8,128)(2,1)} %constant_dynamic-slice_fusion.3), channel_id=1, source_target_pairs={{0,2},{1,3},{2,0},{3,1},{4,6},{5,7},{6,4},{7,5},{8,10},{9,11},{10,... | collective-permute-start | bytes 1572872 | tf_op jit(solution)/shard_map/ppermute | solution.py:24
  66.2 0.2 convert_reduce_fusion
  66.4 2.4 %multiply_reduce_fusion = (f32[]{:T(128)}, f32[512,512]{1,0:T(8,128)}) fusion(f32[1024]{0:T(1024)S(1)} %bitcast.38, f32[1024]{0:T(1024)S(1)} %get-tuple-element.58, bf16[128,1024]{1,0:T(8,128)(2,1)S(1)} %collective-permute-done.4, bf16[128,1024]{1,0:T(8,128)(2,1)S(1)} %collective-permute-done.3, bf16[128,1024]{1,0:T(8,128)(2,1)S(1)} %collective-permute-done.2, ...), kind=kOutput, calls=%fused_computation.25 | convolution fusion | flops 543948800 | bytes 2105348 | tf_op jit(solution)/shard_map/dot_general | solution.py:178
  69.5 0.0 copy-start.11
  69.5 1.8 fusion.2
  71.3 0.4 convolution_convert_fusion.2
  71.8 0.4 convolution_convert_fusion.3
  72.2 0.4 fusion.3
  72.7 0.8 copy-done.1
  73.5 1.2 convolution_convert_fusion.1
  74.7 2.9 %fusion.4 = bf16[512,512]{1,0:T(8,128)(2,1)} fusion(bf16[512,512]{1,0:T(8,128)(2,1)} %convolution_convert_fusion.1, bf16[512,512]{1,0:T(8,128)(2,1)} %copy-done.10, bf16[512,512]{1,0:T(8,128)(2,1)} %copy-done.1), kind=kOutput, calls=%fused_computation.18 | convolution fusion | flops 538443776 | bytes 2097152 | tf_op jit(solution)/shard_map/dot_general | solution.py:178
  77.6 1.8 convolution_divide_fusion
  79.4 0.0 copy-start
  79.4 0.9 convolution_bitcast_fusion.1
  80.3 0.7 convolution_bitcast_fusion
  81.0 0.7 fusion.9
  81.7 0.1 fusion.7.transform_ref
  81.8 37.4 %collective-permute-done.9.refs_2_ = bf16[128,2048]{1,0:T(8,128)(2,1)S(1)} collective-permute-done((bf16[128,2048]{1,0:T(8,128)(2,1)}, bf16[128,2048]{1,0:T(8,128)(2,1)S(1)}, u32[]{:S(2)}, u32[]{:S(2)}) %collective-permute-start.9) | collective-permute-done | bytes 524320 | tf_op jit(solution)/shard_map/ppermute | solution.py:24
  119.2 3.2 %shard_map.65 = (bf16[128,16384]{1,0:T(8,128)(2,1)}, bf16[128,2048]{1,0:T(8,128)(2,1)S(1)}, bf16[128,2048]{1,0:T(8,128)(2,1)S(1)}, bf16[128,2048]{1,0:T(8,128)(2,1)S(1)}) custom-call(s32[1]{0:T(128)} %bitcast.pos_ref, bf16[512,512]{1,0:T(8,128)(2,1)S(1)} %fusion.7.transform_ref, bf16[128,16384]{1,0:T(8,128)(2,1)S(1)} %copy-done, ...), custom_call_target="tpu_custom_call" | custom-call | flops 1073741824 | bytes 4718592 | tf_op jit(solution)/shard_map/pallas_call | solution.py:126
  122.3 2.8 %collective-permute-start.17 = (bf16[128,2048]{1,0:T(8,128)(2,1)S(1)}, bf16[128,2048]{1,0:T(8,128)(2,1)S(1)}, u32[]{:S(2)}, u32[]{:S(2)}) collective-permute-start(bf16[128,2048]{1,0:T(8,128)(2,1)S(1)} %get-tuple-element.49), channel_id=1, source_target_pairs={{0,2},{1,3},{2,0},{3,1},{4,6},{5,7},{6,4},{7,5},{8,10},{9,11},{10,... | collective-permute-start | bytes 1572872 | tf_op jit(solution)/shard_map/ppermute | solution.py:24
  125.1 0.2 collective-permute-start.15
  125.3 1.0 collective-permute-start.16
  126.3 3.2 %shard_map.66 = (bf16[128,16384]{1,0:T(8,128)(2,1)}, bf16[128,2048]{1,0:T(8,128)(2,1)S(1)}, bf16[128,2048]{1,0:T(8,128)(2,1)S(1)}, bf16[128,2048]{1,0:T(8,128)(2,1)S(1)}) custom-call(s32[1]{0:T(128)} %bitcast.pos_ref, bf16[512,512]{1,0:T(8,128)(2,1)S(1)} %fusion.7.transform_ref, bf16[128,16384]{1,0:T(8,128)(2,1)S(1)} %copy-done, ...), custom_call_target="tpu_custom_call", output_to_operand_aliasing={{0}: (6, {})} | custom-call | flops 1073741824 | bytes 4718592 | tf_op jit(solution)/shard_map/pallas_call | solution.py:126
  129.5 1.5 collective-permute-start.14
  131.0 0.0 collective-permute-start.13
  131.0 27.0 %collective-permute-done.17.piece_ref = bf16[128,2048]{1,0:T(8,128)(2,1)S(1)} collective-permute-done((bf16[128,2048]{1,0:T(8,128)(2,1)S(1)}, bf16[128,2048]{1,0:T(8,128)(2,1)S(1)}, u32[]{:S(2)}, u32[]{:S(2)}) %collective-permute-start.17) | collective-permute-done | bytes 524320 | tf_op jit(solution)/shard_map/ppermute | solution.py:24
  158.0 1.3 collective-permute-start.12
  159.3 0.8 shard_map.67.buffer_ref
  160.1 0.8 shard_map.68.buffer_ref
  160.9 22.0 %collective-permute-done.15.piece_ref = bf16[128,2048]{1,0:T(8,128)(2,1)S(1)} collective-permute-done((bf16[128,2048]{1,0:T(8,128)(2,1)S(1)}, bf16[128,2048]{1,0:T(8,128)(2,1)S(1)}, u32[]{:S(2)}, u32[]{:S(2)}) %collective-permute-start.15) | collective-permute-done | bytes 524320 | tf_op jit(solution)/shard_map/ppermute | solution.py:24
  182.9 0.8 shard_map.69.buffer_ref
  183.7 19.2 %collective-permute-done.14.piece_ref = bf16[128,2048]{1,0:T(8,128)(2,1)S(1)} collective-permute-done((bf16[128,2048]{1,0:T(8,128)(2,1)S(1)}, bf16[128,2048]{1,0:T(8,128)(2,1)S(1)}, u32[]{:S(2)}, u32[]{:S(2)}) %collective-permute-start.14) | collective-permute-done | bytes 524320 | tf_op jit(solution)/shard_map/ppermute | solution.py:24
  203.0 0.8 shard_map.70.buffer_ref
  203.8 0.8 shard_map.71.buffer_ref
  204.6 11.6 %collective-permute-done.12.piece_ref = bf16[128,2048]{1,0:T(8,128)(2,1)S(1)} collective-permute-done((bf16[128,2048]{1,0:T(8,128)(2,1)S(1)}, bf16[128,2048]{1,0:T(8,128)(2,1)S(1)}, u32[]{:S(2)}, u32[]{:S(2)}) %collective-permute-start.12) | collective-permute-done | bytes 524320 | tf_op jit(solution)/shard_map/ppermute | solution.py:24
  216.2 0.8 shard_map.72
  (39 shorter events, 0.2 us)
Async XLA Ops:
  0.9 31.9 %collective-permute-start.10 = (bf16[128,512]{1,0:T(8,128)(2,1)S(1)}, bf16[128,512]{1,0:T(8,128)(2,1)S(1)}, u32[]{:S(2)}, u32[]{:S(2)}) collective-permute-start(bf16[128,512]{1,0:T(8,128)(2,1)S(1)} %constant_dynamic-slice_fusion.6), channel_id=1, source_target_pairs={{0,3},{1,2},{2,1},{3,0},{4,7},{5,6},{6,5},{7,4},{8,11},{9,10},{10,... | collective-permute-start | bytes 393224 | tf_op jit(solution)/shard_map/ppermute | solution.py:24
  3.3 32.0 %collective-permute-start.11 = (bf16[128,1536]{1,0:T(8,128)(2,1)S(1)}, bf16[128,1536]{1,0:T(8,128)(2,1)S(1)}, u32[]{:S(2)}, u32[]{:S(2)}) collective-permute-start(bf16[128,1536]{1,0:T(8,128)(2,1)S(1)} %constant_dynamic-slice_fusion.5), channel_id=1, source_target_pairs={{0,3},{1,2},{2,1},{3,0},{4,7},{5,6},{6,5},{7,4},{8,11},{9,10},{10,... | collective-permute-start | bytes 1179656 | tf_op jit(solution)/shard_map/ppermute | solution.py:24
  6.6 12.1 %collective-permute-start.1 = (bf16[144,1024]{1,0:T(8,128)(2,1)S(1)}, bf16[144,1024]{1,0:T(8,128)(2,1)S(1)}, u32[]{:S(2)}, u32[]{:S(2)}) collective-permute-start(bf16[144,1024]{1,0:T(8,128)(2,1)S(1)} %get-tuple-element.51), channel_id=1, source_target_pairs={{0,28},{4,0},{8,4},{12,8},{16,12},{20,16},{24,20},{28,24},{1,29},{... | collective-permute-start | bytes 884744 | tf_op jit(solution)/shard_map/ppermute | solution.py:213
  7.9 10.8 %collective-permute-start = (bf16[144,1024]{1,0:T(8,128)(2,1)S(1)}, bf16[144,1024]{1,0:T(8,128)(2,1)S(1)}, u32[]{:S(2)}, u32[]{:S(2)}) collective-permute-start(bf16[144,1024]{1,0:T(8,128)(2,1)S(1)} %get-tuple-element.52), channel_id=1, source_target_pairs={{0,4},{4,8},{8,12},{12,16},{16,20},{20,24},{24,28},{28,0},{1,5},{5... | collective-permute-start | bytes 884744 | tf_op jit(solution)/shard_map/ppermute | solution.py:213
  11.0 7.6 %copy-start.8 = (s32[4,1024]{1,0:T(4,128)S(1)}, s32[4,1024]{1,0:T(4,128)}, u32[]{:S(2)}) copy-start(s32[4,1024]{1,0:T(4,128)} %param.9) | copy-start | bytes 49156
  27.3 5.5 %copy-start.9 = (f32[1,1024]{1,0:T(1,128)S(1)}, f32[1,1024]{1,0:T(1,128)}, u32[]{:S(2)}) copy-start(f32[1,1024]{1,0:T(1,128)} %param.10) | copy-start | bytes 12292
  27.4 19.6 %collective-permute-start.4 = (bf16[128,1024]{1,0:T(8,128)(2,1)S(1)}, bf16[128,1024]{1,0:T(8,128)(2,1)S(1)}, u32[]{:S(2)}, u32[]{:S(2)}) collective-permute-start(bf16[128,1024]{1,0:T(8,128)(2,1)S(1)} %get-tuple-element.54), channel_id=1, source_target_pairs={{0,3},{1,2},{2,1},{3,0},{4,7},{5,6},{6,5},{7,4},{8,11},{9,10},{10,... | collective-permute-start | bytes 786440 | tf_op jit(solution)/shard_map/ppermute | solution.py:24
  28.8 34.3 %collective-permute-start.3 = (bf16[128,1024]{1,0:T(8,128)(2,1)S(1)}, bf16[128,1024]{1,0:T(8,128)(2,1)S(1)}, u32[]{:S(2)}, u32[]{:S(2)}) collective-permute-start(bf16[128,1024]{1,0:T(8,128)(2,1)S(1)} %get-tuple-element.55), channel_id=1, source_target_pairs={{0,2},{1,3},{2,0},{3,1},{4,6},{5,7},{6,4},{7,5},{8,10},{9,11},{10,... | collective-permute-start | bytes 786440 | tf_op jit(solution)/shard_map/ppermute | solution.py:24
  31.7 34.5 %collective-permute-start.2 = (bf16[128,1024]{1,0:T(8,128)(2,1)S(1)}, bf16[128,1024]{1,0:T(8,128)(2,1)S(1)}, u32[]{:S(2)}, u32[]{:S(2)}) collective-permute-start(bf16[128,1024]{1,0:T(8,128)(2,1)S(1)} %get-tuple-element.56), channel_id=1, source_target_pairs={{0,1},{1,0},{2,3},{3,2},{4,5},{5,4},{6,7},{7,6},{8,9},{9,8},{10,11... | collective-permute-start | bytes 786440 | tf_op jit(solution)/shard_map/ppermute | solution.py:24
  32.8 92.5 %collective-permute-start.6 = (bf16[128,2048]{1,0:T(8,128)(2,1)}, bf16[128,2048]{1,0:T(8,128)(2,1)S(1)}, u32[]{:S(2)}, u32[]{:S(2)}) collective-permute-start(bf16[128,2048]{1,0:T(8,128)(2,1)} %constant_dynamic-slice_fusion), channel_id=1, source_target_pairs={{0,2},{1,3},{2,0},{3,1},{4,6},{5,7},{6,4},{7,5},{8,10},{9,11},{10,... | collective-permute-start | bytes 1572872 | tf_op jit(solution)/shard_map/ppermute | solution.py:24
  35.3 91.1 %collective-permute-start.5 = (bf16[128,2048]{1,0:T(8,128)(2,1)}, bf16[128,2048]{1,0:T(8,128)(2,1)S(1)}, u32[]{:S(2)}, u32[]{:S(2)}) collective-permute-start(bf16[128,2048]{1,0:T(8,128)(2,1)} %constant_dynamic-slice_fusion.1), channel_id=1, source_target_pairs={{0,1},{1,0},{2,3},{3,2},{4,5},{5,4},{6,7},{7,6},{8,9},{9,8},{10,11... | collective-permute-start | bytes 1572872 | tf_op jit(solution)/shard_map/ppermute | solution.py:24
  47.0 21.7 %copy-start.2 = (bf16[128,1024]{1,0:T(8,128)(2,1)}, bf16[128,1024]{1,0:T(8,128)(2,1)S(1)}, u32[]{:S(2)}) copy-start(bf16[128,1024]{1,0:T(8,128)(2,1)S(1)} %collective-permute-done.4) | copy-start | bytes 786436
  47.0 79.3 %collective-permute-start.7 = (bf16[128,2048]{1,0:T(8,128)(2,1)}, bf16[128,2048]{1,0:T(8,128)(2,1)S(1)}, u32[]{:S(2)}, u32[]{:S(2)}) collective-permute-start(bf16[128,2048]{1,0:T(8,128)(2,1)} %constant_dynamic-slice_fusion.2), channel_id=1, source_target_pairs={{0,3},{1,2},{2,1},{3,0},{4,7},{5,6},{6,5},{7,4},{8,11},{9,10},{10,... | collective-permute-start | bytes 1572872 | tf_op jit(solution)/shard_map/ppermute | solution.py:24
  63.0 5.7 %copy-start.4 = (bf16[128,1024]{1,0:T(8,128)(2,1)}, bf16[128,1024]{1,0:T(8,128)(2,1)S(1)}, u32[]{:S(2)}) copy-start(bf16[128,1024]{1,0:T(8,128)(2,1)S(1)} %collective-permute-done.3) | copy-start | bytes 786436
  63.0 56.1 %collective-permute-start.9 = (bf16[128,2048]{1,0:T(8,128)(2,1)}, bf16[128,2048]{1,0:T(8,128)(2,1)S(1)}, u32[]{:S(2)}, u32[]{:S(2)}) collective-permute-start(bf16[128,2048]{1,0:T(8,128)(2,1)} %constant_dynamic-slice_fusion.3), channel_id=1, source_target_pairs={{0,2},{1,3},{2,0},{3,1},{4,6},{5,7},{6,4},{7,5},{8,10},{9,11},{10,... | collective-permute-start | bytes 1572872 | tf_op jit(solution)/shard_map/ppermute | solution.py:24
  66.1 2.6 %copy-start.6 = (bf16[128,1024]{1,0:T(8,128)(2,1)}, bf16[128,1024]{1,0:T(8,128)(2,1)S(1)}, u32[]{:S(2)}) copy-start(bf16[128,1024]{1,0:T(8,128)(2,1)S(1)} %collective-permute-done.2) | copy-start | bytes 786436
  66.1 53.0 %collective-permute-start.8 = (bf16[128,2048]{1,0:T(8,128)(2,1)}, bf16[128,2048]{1,0:T(8,128)(2,1)S(1)}, u32[]{:S(2)}, u32[]{:S(2)}) collective-permute-start(bf16[128,2048]{1,0:T(8,128)(2,1)} %constant_dynamic-slice_fusion.4), channel_id=1, source_target_pairs={{0,1},{1,0},{2,3},{3,2},{4,5},{5,4},{6,7},{7,6},{8,9},{9,8},{10,11... | collective-permute-start | bytes 1572872 | tf_op jit(solution)/shard_map/ppermute | solution.py:24
  69.5 1.8 copy-start.11
  71.8 0.9 copy-start.10
  72.6 0.8 copy-start.1
  77.6 1.8 copy-start.3
  77.6 1.8 copy-start.5
  77.6 1.8 copy-start.7
  79.4 39.8 %copy-start = (bf16[128,16384]{1,0:T(8,128)(2,1)S(1)}, bf16[128,16384]{1,0:T(8,128)(2,1)}, u32[]{:S(2)}) copy-start(bf16[128,16384]{1,0:T(8,128)(2,1)} %refs_0_.3) | copy-start | bytes 12582916
  122.3 35.6 %collective-permute-start.17 = (bf16[128,2048]{1,0:T(8,128)(2,1)S(1)}, bf16[128,2048]{1,0:T(8,128)(2,1)S(1)}, u32[]{:S(2)}, u32[]{:S(2)}) collective-permute-start(bf16[128,2048]{1,0:T(8,128)(2,1)S(1)} %get-tuple-element.49), channel_id=1, source_target_pairs={{0,2},{1,3},{2,0},{3,1},{4,6},{5,7},{6,4},{7,5},{8,10},{9,11},{10,... | collective-permute-start | bytes 1572872 | tf_op jit(solution)/shard_map/ppermute | solution.py:24
  125.1 57.8 %collective-permute-start.15 = (bf16[128,2048]{1,0:T(8,128)(2,1)S(1)}, bf16[128,2048]{1,0:T(8,128)(2,1)S(1)}, u32[]{:S(2)}, u32[]{:S(2)}) collective-permute-start(bf16[128,2048]{1,0:T(8,128)(2,1)S(1)} %get-tuple-element.47), channel_id=1, source_target_pairs={{0,3},{1,2},{2,1},{3,0},{4,7},{5,6},{6,5},{7,4},{8,11},{9,10},{10,... | collective-permute-start | bytes 1572872 | tf_op jit(solution)/shard_map/ppermute | solution.py:24
  125.3 34.8 %collective-permute-start.16 = (bf16[128,2048]{1,0:T(8,128)(2,1)S(1)}, bf16[128,2048]{1,0:T(8,128)(2,1)S(1)}, u32[]{:S(2)}, u32[]{:S(2)}) collective-permute-start(bf16[128,2048]{1,0:T(8,128)(2,1)S(1)} %get-tuple-element.48), channel_id=1, source_target_pairs={{0,1},{1,0},{2,3},{3,2},{4,5},{5,4},{6,7},{7,6},{8,9},{9,8},{10,11... | collective-permute-start | bytes 1572872 | tf_op jit(solution)/shard_map/ppermute | solution.py:24
  129.5 73.5 %collective-permute-start.14 = (bf16[128,2048]{1,0:T(8,128)(2,1)S(1)}, bf16[128,2048]{1,0:T(8,128)(2,1)S(1)}, u32[]{:S(2)}, u32[]{:S(2)}) collective-permute-start(bf16[128,2048]{1,0:T(8,128)(2,1)S(1)} %get-tuple-element.46), channel_id=1, source_target_pairs={{0,2},{1,3},{2,0},{3,1},{4,6},{5,7},{6,4},{7,5},{8,10},{9,11},{10,... | collective-permute-start | bytes 1572872 | tf_op jit(solution)/shard_map/ppermute | solution.py:24
  131.0 72.8 %collective-permute-start.13 = (bf16[128,2048]{1,0:T(8,128)(2,1)S(1)}, bf16[128,2048]{1,0:T(8,128)(2,1)S(1)}, u32[]{:S(2)}, u32[]{:S(2)}) collective-permute-start(bf16[128,2048]{1,0:T(8,128)(2,1)S(1)} %get-tuple-element.45), channel_id=1, source_target_pairs={{0,1},{1,0},{2,3},{3,2},{4,5},{5,4},{6,7},{7,6},{8,9},{9,8},{10,11... | collective-permute-start | bytes 1572872 | tf_op jit(solution)/shard_map/ppermute | solution.py:24
  158.0 58.2 %collective-permute-start.12 = (bf16[128,2048]{1,0:T(8,128)(2,1)S(1)}, bf16[128,2048]{1,0:T(8,128)(2,1)S(1)}, u32[]{:S(2)}, u32[]{:S(2)}) collective-permute-start(bf16[128,2048]{1,0:T(8,128)(2,1)S(1)} %get-tuple-element.44), channel_id=1, source_target_pairs={{0,3},{1,2},{2,1},{3,0},{4,7},{5,6},{6,5},{7,4},{8,11},{9,10},{10,... | collective-permute-start | bytes 1572872 | tf_op jit(solution)/shard_map/ppermute | solution.py:24

commit v4 on v3

--- a/solution.py
+++ b/solution.py
@@ -30,6 +30,31 @@
     low, high = int(part[0] * width), int(part[1] * width)
     start = ((position[0] ^ step) * CHUNKS + chunk) * width + low
     return lax.dynamic_slice(state, (0, start), (rows, high - low))
+
+
+def lead_kernel(first, pos_ref, state_ref, out_ref, sem):
+    start = pl.multiple_of(first(pos_ref[0]), LANES)
+    copy = pltpu.make_async_copy(state_ref.at[:, pl.ds(start, out_ref.shape[1])], out_ref, sem)
+    copy.start()
+    copy.wait()
+
+
+def lead_piece(position, state, step, width):
+    rows, total = state.shape
+    patch = total // lax.axis_size("member")
+    return pl.pallas_call(
+        functools.partial(lead_kernel, lambda pos: (pos ^ step) * patch),
+        in_specs=[
+            pl.BlockSpec(memory_space=pltpu.SMEM),
+            pl.BlockSpec(memory_space=pl.ANY),
+        ],
+        out_specs=pl.BlockSpec(memory_space=pltpu.VMEM),
+        scratch_shapes=[pltpu.SemaphoreType.DMA],
+        out_shape=pltpu.VMEM((rows, width), state.dtype),
+        cost_estimate=pl.CostEstimate(
+            flops=0, transcendentals=0, bytes_accessed=2 * rows * width
+        ),
+    )(position, state)
 
 
 def pick_kernel(pos_ref, start_ref, index_ref, own_ref, low_ref, high_ref, out_ref, pair_ref, pool):
@@ -148,16 +173,17 @@
 
 def place_kernel(first, pos_ref, piece_ref, buffer_ref, out_ref, sem):
     width = piece_ref.shape[1]
-    start = pl.multiple_of(first(pos_ref[0]) * width, LANES)
+    start = pl.multiple_of(first(pos_ref[0]), LANES)
     copy = pltpu.make_async_copy(piece_ref, out_ref.at[:, pl.ds(start, width)], sem)
     copy.start()
     copy.wait()
 
 
-def place(position, buffer, piece, step, chunk):
+def place(position, buffer, piece, step, offset):
     rows, width = piece.shape
+    patch = buffer.shape[1] // lax.axis_size("member")
     return pl.pallas_call(
-        functools.partial(place_kernel, lambda pos: (pos ^ step) * CHUNKS + chunk),
+        functools.partial(place_kernel, lambda pos: (pos ^ step) * patch + offset),
         in_specs=[
             pl.BlockSpec(memory_space=pltpu.SMEM),
             pl.BlockSpec(memory_space=pl.ANY),
@@ -234,7 +260,9 @@
     def send_chunk(chunk, order):
         return {step: send(chunk, step) for step in order}
 
-    head = send(0, steps[0], (0, 0.25))
+    piece = lead_piece(position, source, steps[0], state.shape[1] // (4 * count * CHUNKS))
+    source, piece = lax.optimization_barrier((source, piece))
+    head = swap(piece, steps[0])
     rest = send(0, steps[0], (0.25, 1))
     arrived = [send_chunk(0, steps[1:])]
     arrived[0][steps[0]] = jnp.concatenate([head, rest], axis=1)
@@ -256,14 +284,21 @@
 
     buffer, returned = None, []
     back = steps[:0:-1] + steps[:1]
+    width = state.shape[1] // (count * CHUNKS)
     for chunk in range(CHUNKS):
         received = [arrived[chunk][step] for step in range(1, count)]
         buffer, *others = update_state(position, transform, state, received, chunk, buffer)
-        returned.append({step: swap(others[step - 1], step) for step in back[:-1]})
-        returned[-1][back[-1]] = swap(others[back[-1] - 1], back[-1])
-    for chunk in range(CHUNKS):
-        for step in back:
-            buffer = place(position, buffer, returned[chunk][step], step, chunk)
+        last = chunk == CHUNKS - 1
+        for step in back[:-1]:
+            returned.append((swap(others[step - 1], step), step, chunk * width))
+        step, cuts = back[-1], [0, width]
+        if last:
+            cuts = [0, width * 3 // 4, width]
+        for low, high in zip(cuts, cuts[1:]):
+            piece = swap(others[step - 1][:, low:high], step)
+            returned.append((piece, step, chunk * width + low))
+    for piece, step, offset in returned:
+        buffer = place(position, buffer, piece, step, offset)
     return buffer
 
 

time: 218 us -> 215 us (0.986)
  the two profiles are of different devices: /device:TPU:13 before, /device:TPU:12 now
where the time goes in v4:
time: 215 us
  waiting for transfers between devices  139 us (65%)
  starting transfers between devices  25.5 us (12%)
  Pallas kernels  21.4 us (10%)
  matrix products  13.6 us (6%)
  local copies, waits for them, and re-layouts  12 us (6%)
    ppermute x17, waiting for transfers between devices, swap(): lax.ppermute(block, 'member', partners(lax.axis_size('member'), step))  139 us
    ppermute x17, starting transfers between devices, swap(): lax.ppermute(block, 'member', partners(lax.axis_size('member'), step))  25 us
    dot_general x8, matrix products, product(): lax.dot_general(left, right, (dims, ((), ())), preferred_element_type=jnp...  11.3 us
    dynamic_slice x6, local copies, waits for them, and re-layouts, cut(): return lax.dynamic_slice(state, (0, start), (rows, high - low))  10.5 us
    pallas_call x1, Pallas kernels, pick(): pl.pallas_call(pick_kernel, grid_spec=pltpu.PrefetchScalarGridSpec(num_sc...  8.61 us
    pallas_call x2, Pallas kernels, update_state(): pl.pallas_call(functools.partial(update_kernel, count, aliased), grid_spe...  6.33 us
    pallas_call x7, Pallas kernels, place(): pl.pallas_call(functools.partial(place_kernel, lambda pos: (pos ^ step) *...  5.43 us
  transfers between devices with their start and end apart: 19, of which 9 were waited for; matrix products, arithmetic and copies ran while one was open for 12% of the time, Pallas kernels for 9%

profile of v4, /device:TPU:12, one launch (start us, length us, event | category | flops | bytes accessed | tf_op | source)
XLA Modules:
  0.0 214.6 jit_solution(6734807887822197534)
XLA Ops:
  0.0 1.0 shard_map.65
  1.0 1.6 collective-permute-start.10
  2.7 1.0 constant_dynamic-slice_fusion.5
  3.7 0.5 collective-permute-start.11
  4.3 0.1 pad.9.clone
  4.3 0.3 maximum_maximum_fusion.own_ref
  4.7 0.4 collective-permute-start.1
  5.1 0.2 collective-permute-start
  5.3 1.9 constant_dynamic-slice_fusion.4
  7.2 1.9 constant_dynamic-slice_fusion.3
  9.1 1.9 constant_dynamic-slice_fusion.2
  11.0 1.9 constant_dynamic-slice_fusion.1
  12.9 1.9 constant_dynamic-slice_fusion
  14.8 0.1 reduce_min.9
  14.9 8.6 %shard_map.64 = (bf16[4,128,1024]{2,1,0:T(8,128)(2,1)S(1)}, bf16[16,1024]{1,0:T(8,128)(2,1)S(1)}) custom-call(s32[1]{0:T(128)} %bitcast.pos_ref, s32[4]{0:T(128)S(1)} %multiply_minimum_fusion.start_ref, s32[4,1,1024]{2,1,0:T(1,128)S(1)} %reshape.16.index_ref, bf16[144,4096]{1,0:T(8,128)(2,1)S(1)} %maximum_maximum_fusion.own_ref, ...), custom_call_target="tpu_custom_call" | custom-call | flops 2566914048 | bytes 2359296 | tf_op jit(solution)/shard_map/pallas_call | solution.py:92
  23.5 0.0 copy-start.12
  23.6 0.1 slice_bitcast_fusion.3
  23.6 1.6 collective-permute-start.4
  25.3 3.0 %collective-permute-start.3 = (bf16[128,1024]{1,0:T(8,128)(2,1)S(1)}, bf16[128,1024]{1,0:T(8,128)(2,1)S(1)}, u32[]{:S(2)}, u32[]{:S(2)}) collective-permute-start(bf16[128,1024]{1,0:T(8,128)(2,1)S(1)} %get-tuple-element.55), channel_id=1, source_target_pairs={{0,2},{1,3},{2,0},{3,1},{4,6},{5,7},{6,4},{7,5},{8,10},{9,11},{10,... | collective-permute-start | bytes 786440 | tf_op jit(solution)/shard_map/ppermute | solution.py:24
  28.3 1.2 collective-permute-start.2
  29.6 3.0 %collective-permute-start.6 = (bf16[128,2048]{1,0:T(8,128)(2,1)}, bf16[128,2048]{1,0:T(8,128)(2,1)S(1)}, u32[]{:S(2)}, u32[]{:S(2)}) collective-permute-start(bf16[128,2048]{1,0:T(8,128)(2,1)} %constant_dynamic-slice_fusion), channel_id=1, source_target_pairs={{0,2},{1,3},{2,0},{3,1},{4,6},{5,7},{6,4},{7,5},{8,10},{9,11},{10,... | collective-permute-start | bytes 1572872 | tf_op jit(solution)/shard_map/ppermute | solution.py:24
  32.6 0.9 pad_maximum_fusion.1.refs_3_
  33.6 10.4 %collective-permute-done.4 = bf16[128,1024]{1,0:T(8,128)(2,1)S(1)} collective-permute-done((bf16[128,1024]{1,0:T(8,128)(2,1)S(1)}, bf16[128,1024]{1,0:T(8,128)(2,1)S(1)}, u32[]{:S(2)}, u32[]{:S(2)}) %collective-permute-start.4) | collective-permute-done | bytes 262176 | tf_op jit(solution)/shard_map/ppermute | solution.py:24
  43.9 1.6 collective-permute-start.7
  45.5 14.4 %collective-permute-done.3 = bf16[128,1024]{1,0:T(8,128)(2,1)S(1)} collective-permute-done((bf16[128,1024]{1,0:T(8,128)(2,1)S(1)}, bf16[128,1024]{1,0:T(8,128)(2,1)S(1)}, u32[]{:S(2)}, u32[]{:S(2)}) %collective-permute-start.3) | collective-permute-done | bytes 262176 | tf_op jit(solution)/shard_map/ppermute | solution.py:24
  59.9 3.4 %collective-permute-start.9 = (bf16[128,2048]{1,0:T(8,128)(2,1)}, bf16[128,2048]{1,0:T(8,128)(2,1)S(1)}, u32[]{:S(2)}, u32[]{:S(2)}) collective-permute-start(bf16[128,2048]{1,0:T(8,128)(2,1)} %constant_dynamic-slice_fusion.3), channel_id=1, source_target_pairs={{0,2},{1,3},{2,0},{3,1},{4,6},{5,7},{6,4},{7,5},{8,10},{9,11},{10,... | collective-permute-start | bytes 1572872 | tf_op jit(solution)/shard_map/ppermute | solution.py:24
  63.3 0.2 convert_reduce_fusion
  63.5 2.3 %multiply_reduce_fusion = (f32[]{:T(128)}, f32[512,512]{1,0:T(8,128)}) fusion(f32[1024]{0:T(1024)S(1)} %bitcast.38, f32[1024]{0:T(1024)S(1)} %get-tuple-element.58, bf16[128,1024]{1,0:T(8,128)(2,1)S(1)} %collective-permute-done.4, bf16[128,1024]{1,0:T(8,128)(2,1)S(1)} %collective-permute-done.3, bf16[128,1024]{1,0:T(8,128)(2,1)S(1)} %collective-permute-done.2, ...), kind=kOutput, calls=%fused_computation.25 | convolution fusion | flops 543948800 | bytes 2105348 | tf_op jit(solution)/shard_map/dot_general | solution.py:204
  66.6 0.0 copy-start.14
  66.6 1.8 fusion.2
  68.4 0.4 convolution_convert_fusion.2
  68.8 0.4 convolution_convert_fusion.3
  69.2 0.4 copy-done.13
  69.6 0.4 fusion.3
  70.0 0.8 copy-done.2
  70.8 1.2 convolution_convert_fusion.1
  72.1 2.9 %fusion.4 = bf16[512,512]{1,0:T(8,128)(2,1)} fusion(bf16[512,512]{1,0:T(8,128)(2,1)} %convolution_convert_fusion.1, bf16[512,512]{1,0:T(8,128)(2,1)} %copy-done.13, bf16[512,512]{1,0:T(8,128)(2,1)} %copy-done.2), kind=kOutput, calls=%fused_computation.18 | convolution fusion | flops 538443776 | bytes 2097152 | tf_op jit(solution)/shard_map/dot_general | solution.py:204
  75.0 1.8 convolution_divide_fusion
  76.8 0.9 convolution_bitcast_fusion.1
  77.7 0.7 convolution_bitcast_fusion
  78.4 0.7 fusion.9
  79.1 0.1 fusion.7.transform_ref
  79.2 37.0 %collective-permute-done.9.refs_2_ = bf16[128,2048]{1,0:T(8,128)(2,1)S(1)} collective-permute-done((bf16[128,2048]{1,0:T(8,128)(2,1)}, bf16[128,2048]{1,0:T(8,128)(2,1)S(1)}, u32[]{:S(2)}, u32[]{:S(2)}) %collective-permute-start.9) | collective-permute-done | bytes 524320 | tf_op jit(solution)/shard_map/ppermute | solution.py:24
  116.2 3.2 %shard_map.66 = (bf16[128,16384]{1,0:T(8,128)(2,1)}, bf16[128,2048]{1,0:T(8,128)(2,1)S(1)}, bf16[128,2048]{1,0:T(8,128)(2,1)S(1)}, bf16[128,2048]{1,0:T(8,128)(2,1)S(1)}) custom-call(s32[1]{0:T(128)} %bitcast.pos_ref, bf16[512,512]{1,0:T(8,128)(2,1)S(1)} %fusion.7.transform_ref, bf16[128,16384]{1,0:T(8,128)(2,1)S(1)} %copy-done, ...), custom_call_target="tpu_custom_call" | custom-call | flops 1073741824 | bytes 4718592 | tf_op jit(solution)/shard_map/pallas_call | solution.py:151
  119.4 2.3 %collective-permute-start.17 = (bf16[128,2048]{1,0:T(8,128)(2,1)S(1)}, bf16[128,2048]{1,0:T(8,128)(2,1)S(1)}, u32[]{:S(2)}, u32[]{:S(2)}) collective-permute-start(bf16[128,2048]{1,0:T(8,128)(2,1)S(1)} %get-tuple-element.48), channel_id=1, source_target_pairs={{0,1},{1,0},{2,3},{3,2},{4,5},{5,4},{6,7},{7,6},{8,9},{9,8},{10,11... | collective-permute-start | bytes 1572872 | tf_op jit(solution)/shard_map/ppermute | solution.py:24
  121.7 1.0 collective-permute-start.18
  122.7 0.6 collective-permute-start.16
  123.3 3.2 %shard_map.67 = (bf16[128,16384]{1,0:T(8,128)(2,1)}, bf16[128,2048]{1,0:T(8,128)(2,1)S(1)}, bf16[128,2048]{1,0:T(8,128)(2,1)S(1)}, bf16[128,2048]{1,0:T(8,128)(2,1)S(1)}) custom-call(s32[1]{0:T(128)} %bitcast.pos_ref, bf16[512,512]{1,0:T(8,128)(2,1)S(1)} %fusion.7.transform_ref, bf16[128,16384]{1,0:T(8,128)(2,1)S(1)} %copy-done, ...), custom_call_target="tpu_custom_call", output_to_operand_aliasing={{0}: (6, {})} | custom-call | flops 1073741824 | bytes 4718592 | tf_op jit(solution)/shard_map/pallas_call | solution.py:151
  126.4 3.8 %collective-permute-start.15 = (bf16[128,2048]{1,0:T(8,128)(2,1)S(1)}, bf16[128,2048]{1,0:T(8,128)(2,1)S(1)}, u32[]{:S(2)}, u32[]{:S(2)}) collective-permute-start(bf16[128,2048]{1,0:T(8,128)(2,1)S(1)} %get-tuple-element.46), channel_id=1, source_target_pairs={{0,2},{1,3},{2,0},{3,1},{4,6},{5,7},{6,4},{7,5},{8,10},{9,11},{10,... | collective-permute-start | bytes 1572872 | tf_op jit(solution)/shard_map/ppermute | solution.py:24
  130.3 14.4 %collective-permute-done.17.piece_ref = bf16[128,2048]{1,0:T(8,128)(2,1)S(1)} collective-permute-done((bf16[128,2048]{1,0:T(8,128)(2,1)S(1)}, bf16[128,2048]{1,0:T(8,128)(2,1)S(1)}, u32[]{:S(2)}, u32[]{:S(2)}) %collective-permute-start.17) | collective-permute-done | bytes 524320 | tf_op jit(solution)/shard_map/ppermute | solution.py:24
  144.7 0.9 collective-permute-start.13
  145.6 23.2 %collective-permute-done.18.piece_ref = bf16[128,2048]{1,0:T(8,128)(2,1)S(1)} collective-permute-done((bf16[128,2048]{1,0:T(8,128)(2,1)S(1)}, bf16[128,2048]{1,0:T(8,128)(2,1)S(1)}, u32[]{:S(2)}, u32[]{:S(2)}) %collective-permute-start.18) | collective-permute-done | bytes 524320 | tf_op jit(solution)/shard_map/ppermute | solution.py:24
  168.8 0.4 collective-permute-start.12
  169.2 0.8 shard_map.68.buffer_ref
  170.0 0.8 shard_map.69.buffer_ref
  170.8 21.4 %collective-permute-done.16.piece_ref = bf16[128,2048]{1,0:T(8,128)(2,1)S(1)} collective-permute-done((bf16[128,2048]{1,0:T(8,128)(2,1)S(1)}, bf16[128,2048]{1,0:T(8,128)(2,1)S(1)}, u32[]{:S(2)}, u32[]{:S(2)}) %collective-permute-start.16) | collective-permute-done | bytes 524320 | tf_op jit(solution)/shard_map/ppermute | solution.py:24
  192.3 0.8 shard_map.70.buffer_ref
  193.1 9.4 %collective-permute-done.15.piece_ref = bf16[128,2048]{1,0:T(8,128)(2,1)S(1)} collective-permute-done((bf16[128,2048]{1,0:T(8,128)(2,1)S(1)}, bf16[128,2048]{1,0:T(8,128)(2,1)S(1)}, u32[]{:S(2)}, u32[]{:S(2)}) %collective-permute-start.15) | collective-permute-done | bytes 524320 | tf_op jit(solution)/shard_map/ppermute | solution.py:24
  202.5 0.8 shard_map.71.buffer_ref
  203.3 0.8 shard_map.72.buffer_ref
  204.1 7.8 %collective-permute-done.13.piece_ref = bf16[128,1536]{1,0:T(8,128)(2,1)S(1)} collective-permute-done((bf16[128,1536]{1,0:T(8,128)(2,1)S(1)}, bf16[128,1536]{1,0:T(8,128)(2,1)S(1)}, u32[]{:S(2)}, u32[]{:S(2)}) %collective-permute-start.13) | collective-permute-done | bytes 393248 | tf_op jit(solution)/shard_map/ppermute | solution.py:24
  211.9 0.8 shard_map.73.buffer_ref
  212.7 1.2 collective-permute-done.12.piece_ref
  213.9 0.7 shard_map.74
  (50 shorter events, 0.2 us)
Async XLA Ops:
  0.0 4.2 %copy-start.10 = (bf16[4096]{0:T(1024)(128)(2,1)S(1)}, bf16[4096]{0:T(1024)(128)(2,1)}, u32[]{:S(2)}) copy-start(bf16[4096]{0:T(1024)(128)(2,1)} %param.7) | copy-start | bytes 24580
  0.0 4.2 %copy-start.11 = (bf16[4096]{0:T(1024)(128)(2,1)S(1)}, bf16[4096]{0:T(1024)(128)(2,1)}, u32[]{:S(2)}) copy-start(bf16[4096]{0:T(1024)(128)(2,1)} %param.8) | copy-start | bytes 24580
  0.0 4.3 %copy-start.1 = (bf16[128,4096]{1,0:T(8,128)(2,1)S(1)}, bf16[128,4096]{1,0:T(8,128)(2,1)}, u32[]{:S(2)}) copy-start(bf16[128,4096]{1,0:T(8,128)(2,1)} %param.6) | copy-start | bytes 3145732
  1.0 28.6 %collective-permute-start.10 = (bf16[128,512]{1,0:T(8,128)(2,1)S(1)}, bf16[128,512]{1,0:T(8,128)(2,1)}, u32[]{:S(2)}, u32[]{:S(2)}) collective-permute-start(bf16[128,512]{1,0:T(8,128)(2,1)S(1)} %shard_map.65), channel_id=1, source_target_pairs={{0,3},{1,2},{2,1},{3,0},{4,7},{5,6},{6,5},{7,4},{8,11},{9,10},{10,... | collective-permute-start | bytes 393224 | tf_op jit(solution)/shard_map/ppermute | solution.py:24
  3.7 28.9 %collective-permute-start.11 = (bf16[128,1536]{1,0:T(8,128)(2,1)S(1)}, bf16[128,1536]{1,0:T(8,128)(2,1)S(1)}, u32[]{:S(2)}, u32[]{:S(2)}) collective-permute-start(bf16[128,1536]{1,0:T(8,128)(2,1)S(1)} %constant_dynamic-slice_fusion.5), channel_id=1, source_target_pairs={{0,3},{1,2},{2,1},{3,0},{4,7},{5,6},{6,5},{7,4},{8,11},{9,10},{10,... | collective-permute-start | bytes 1179656 | tf_op jit(solution)/shard_map/ppermute | solution.py:24
  4.7 10.2 %collective-permute-start.1 = (bf16[144,1024]{1,0:T(8,128)(2,1)S(1)}, bf16[144,1024]{1,0:T(8,128)(2,1)S(1)}, u32[]{:S(2)}, u32[]{:S(2)}) collective-permute-start(bf16[144,1024]{1,0:T(8,128)(2,1)S(1)} %get-tuple-element.51), channel_id=1, source_target_pairs={{0,28},{4,0},{8,4},{12,8},{16,12},{20,16},{24,20},{28,24},{1,29},{... | collective-permute-start | bytes 884744 | tf_op jit(solution)/shard_map/ppermute | solution.py:239
  5.1 9.9 %collective-permute-start = (bf16[144,1024]{1,0:T(8,128)(2,1)S(1)}, bf16[144,1024]{1,0:T(8,128)(2,1)S(1)}, u32[]{:S(2)}, u32[]{:S(2)}) collective-permute-start(bf16[144,1024]{1,0:T(8,128)(2,1)S(1)} %get-tuple-element.52), channel_id=1, source_target_pairs={{0,4},{4,8},{8,12},{12,16},{16,20},{20,24},{24,28},{28,0},{1,5},{5... | collective-permute-start | bytes 884744 | tf_op jit(solution)/shard_map/ppermute | solution.py:239
  7.2 7.6 %copy-start.9 = (s32[4,1024]{1,0:T(4,128)S(1)}, s32[4,1024]{1,0:T(4,128)}, u32[]{:S(2)}) copy-start(s32[4,1024]{1,0:T(4,128)} %param.9) | copy-start | bytes 49156
  23.5 6.0 %copy-start.12 = (f32[1,1024]{1,0:T(1,128)S(1)}, f32[1,1024]{1,0:T(1,128)}, u32[]{:S(2)}) copy-start(f32[1,1024]{1,0:T(1,128)} %param.10) | copy-start | bytes 12292
  23.6 20.3 %collective-permute-start.4 = (bf16[128,1024]{1,0:T(8,128)(2,1)S(1)}, bf16[128,1024]{1,0:T(8,128)(2,1)S(1)}, u32[]{:S(2)}, u32[]{:S(2)}) collective-permute-start(bf16[128,1024]{1,0:T(8,128)(2,1)S(1)} %get-tuple-element.54), channel_id=1, source_target_pairs={{0,3},{1,2},{2,1},{3,0},{4,7},{5,6},{6,5},{7,4},{8,11},{9,10},{10,... | collective-permute-start | bytes 786440 | tf_op jit(solution)/shard_map/ppermute | solution.py:24
  25.3 34.6 %collective-permute-start.3 = (bf16[128,1024]{1,0:T(8,128)(2,1)S(1)}, bf16[128,1024]{1,0:T(8,128)(2,1)S(1)}, u32[]{:S(2)}, u32[]{:S(2)}) collective-permute-start(bf16[128,1024]{1,0:T(8,128)(2,1)S(1)} %get-tuple-element.55), channel_id=1, source_target_pairs={{0,2},{1,3},{2,0},{3,1},{4,6},{5,7},{6,4},{7,5},{8,10},{9,11},{10,... | collective-permute-start | bytes 786440 | tf_op jit(solution)/shard_map/ppermute | solution.py:24
  28.3 35.0 %collective-permute-start.2 = (bf16[128,1024]{1,0:T(8,128)(2,1)S(1)}, bf16[128,1024]{1,0:T(8,128)(2,1)S(1)}, u32[]{:S(2)}, u32[]{:S(2)}) collective-permute-start(bf16[128,1024]{1,0:T(8,128)(2,1)S(1)} %get-tuple-element.56), channel_id=1, source_target_pairs={{0,1},{1,0},{2,3},{3,2},{4,5},{5,4},{6,7},{7,6},{8,9},{9,8},{10,11... | collective-permute-start | bytes 786440 | tf_op jit(solution)/shard_map/ppermute | solution.py:24
  29.6 93.1 %collective-permute-start.6 = (bf16[128,2048]{1,0:T(8,128)(2,1)}, bf16[128,2048]{1,0:T(8,128)(2,1)S(1)}, u32[]{:S(2)}, u32[]{:S(2)}) collective-permute-start(bf16[128,2048]{1,0:T(8,128)(2,1)} %constant_dynamic-slice_fusion), channel_id=1, source_target_pairs={{0,2},{1,3},{2,0},{3,1},{4,6},{5,7},{6,4},{7,5},{8,10},{9,11},{10,... | collective-permute-start | bytes 1572872 | tf_op jit(solution)/shard_map/ppermute | solution.py:24
  32.6 90.7 %collective-permute-start.5 = (bf16[128,2048]{1,0:T(8,128)(2,1)}, bf16[128,2048]{1,0:T(8,128)(2,1)S(1)}, u32[]{:S(2)}, u32[]{:S(2)}) collective-permute-start(bf16[128,2048]{1,0:T(8,128)(2,1)} %constant_dynamic-slice_fusion.1), channel_id=1, source_target_pairs={{0,1},{1,0},{2,3},{3,2},{4,5},{5,4},{6,7},{7,6},{8,9},{9,8},{10,11... | collective-permute-start | bytes 1572872 | tf_op jit(solution)/shard_map/ppermute | solution.py:24
  43.9 21.9 %copy-start.3 = (bf16[128,1024]{1,0:T(8,128)(2,1)}, bf16[128,1024]{1,0:T(8,128)(2,1)S(1)}, u32[]{:S(2)}) copy-start(bf16[128,1024]{1,0:T(8,128)(2,1)S(1)} %collective-permute-done.4) | copy-start | bytes 786436
  43.9 79.3 %collective-permute-start.7 = (bf16[128,2048]{1,0:T(8,128)(2,1)}, bf16[128,2048]{1,0:T(8,128)(2,1)S(1)}, u32[]{:S(2)}, u32[]{:S(2)}) collective-permute-start(bf16[128,2048]{1,0:T(8,128)(2,1)} %constant_dynamic-slice_fusion.2), channel_id=1, source_target_pairs={{0,3},{1,2},{2,1},{3,0},{4,7},{5,6},{6,5},{7,4},{8,11},{9,10},{10,... | collective-permute-start | bytes 1572872 | tf_op jit(solution)/shard_map/ppermute | solution.py:24
  59.9 5.9 %copy-start.5 = (bf16[128,1024]{1,0:T(8,128)(2,1)}, bf16[128,1024]{1,0:T(8,128)(2,1)S(1)}, u32[]{:S(2)}) copy-start(bf16[128,1024]{1,0:T(8,128)(2,1)S(1)} %collective-permute-done.3) | copy-start | bytes 786436
  59.9 56.3 %collective-permute-start.9 = (bf16[128,2048]{1,0:T(8,128)(2,1)}, bf16[128,2048]{1,0:T(8,128)(2,1)S(1)}, u32[]{:S(2)}, u32[]{:S(2)}) collective-permute-start(bf16[128,2048]{1,0:T(8,128)(2,1)} %constant_dynamic-slice_fusion.3), channel_id=1, source_target_pairs={{0,2},{1,3},{2,0},{3,1},{4,6},{5,7},{6,4},{7,5},{8,10},{9,11},{10,... | collective-permute-start | bytes 1572872 | tf_op jit(solution)/shard_map/ppermute | solution.py:24
  63.3 2.6 %copy-start.7 = (bf16[128,1024]{1,0:T(8,128)(2,1)}, bf16[128,1024]{1,0:T(8,128)(2,1)S(1)}, u32[]{:S(2)}) copy-start(bf16[128,1024]{1,0:T(8,128)(2,1)S(1)} %collective-permute-done.2) | copy-start | bytes 786436
  63.3 52.9 %collective-permute-start.8 = (bf16[128,2048]{1,0:T(8,128)(2,1)}, bf16[128,2048]{1,0:T(8,128)(2,1)S(1)}, u32[]{:S(2)}, u32[]{:S(2)}) collective-permute-start(bf16[128,2048]{1,0:T(8,128)(2,1)} %constant_dynamic-slice_fusion.4), channel_id=1, source_target_pairs={{0,1},{1,0},{2,3},{3,2},{4,5},{5,4},{6,7},{7,6},{8,9},{9,8},{10,11... | collective-permute-start | bytes 1572872 | tf_op jit(solution)/shard_map/ppermute | solution.py:24
  66.6 1.8 copy-start.14
  68.8 0.8 copy-start.13
  70.0 0.8 copy-start.2
  75.0 1.8 copy-start.4
  75.0 1.8 copy-start.6
  75.0 1.8 copy-start.8
  76.8 39.4 %copy-start = (bf16[128,16384]{1,0:T(8,128)(2,1)S(1)}, bf16[128,16384]{1,0:T(8,128)(2,1)}, u32[]{:S(2)}) copy-start(bf16[128,16384]{1,0:T(8,128)(2,1)} %refs_0_.3) | copy-start | bytes 12582916
  119.4 25.3 %collective-permute-start.17 = (bf16[128,2048]{1,0:T(8,128)(2,1)S(1)}, bf16[128,2048]{1,0:T(8,128)(2,1)S(1)}, u32[]{:S(2)}, u32[]{:S(2)}) collective-permute-start(bf16[128,2048]{1,0:T(8,128)(2,1)S(1)} %get-tuple-element.48), channel_id=1, source_target_pairs={{0,1},{1,0},{2,3},{3,2},{4,5},{5,4},{6,7},{7,6},{8,9},{9,8},{10,11... | collective-permute-start | bytes 1572872 | tf_op jit(solution)/shard_map/ppermute | solution.py:24
  121.7 47.1 %collective-permute-start.18 = (bf16[128,2048]{1,0:T(8,128)(2,1)S(1)}, bf16[128,2048]{1,0:T(8,128)(2,1)S(1)}, u32[]{:S(2)}, u32[]{:S(2)}) collective-permute-start(bf16[128,2048]{1,0:T(8,128)(2,1)S(1)} %get-tuple-element.49), channel_id=1, source_target_pairs={{0,2},{1,3},{2,0},{3,1},{4,6},{5,7},{6,4},{7,5},{8,10},{9,11},{10,... | collective-permute-start | bytes 1572872 | tf_op jit(solution)/shard_map/ppermute | solution.py:24
  122.7 69.6 %collective-permute-start.16 = (bf16[128,2048]{1,0:T(8,128)(2,1)S(1)}, bf16[128,2048]{1,0:T(8,128)(2,1)S(1)}, u32[]{:S(2)}, u32[]{:S(2)}) collective-permute-start(bf16[128,2048]{1,0:T(8,128)(2,1)S(1)} %get-tuple-element.47), channel_id=1, source_target_pairs={{0,3},{1,2},{2,1},{3,0},{4,7},{5,6},{6,5},{7,4},{8,11},{9,10},{10,... | collective-permute-start | bytes 1572872 | tf_op jit(solution)/shard_map/ppermute | solution.py:24
  126.4 76.1 %collective-permute-start.15 = (bf16[128,2048]{1,0:T(8,128)(2,1)S(1)}, bf16[128,2048]{1,0:T(8,128)(2,1)S(1)}, u32[]{:S(2)}, u32[]{:S(2)}) collective-permute-start(bf16[128,2048]{1,0:T(8,128)(2,1)S(1)} %get-tuple-element.46), channel_id=1, source_target_pairs={{0,2},{1,3},{2,0},{3,1},{4,6},{5,7},{6,4},{7,5},{8,10},{9,11},{10,... | collective-permute-start | bytes 1572872 | tf_op jit(solution)/shard_map/ppermute | solution.py:24
  130.2 73.1 %collective-permute-start.14 = (bf16[128,2048]{1,0:T(8,128)(2,1)S(1)}, bf16[128,2048]{1,0:T(8,128)(2,1)S(1)}, u32[]{:S(2)}, u32[]{:S(2)}) collective-permute-start(bf16[128,2048]{1,0:T(8,128)(2,1)S(1)} %get-tuple-element.45), channel_id=1, source_target_pairs={{0,1},{1,0},{2,3},{3,2},{4,5},{5,4},{6,7},{7,6},{8,9},{9,8},{10,11... | collective-permute-start | bytes 1572872 | tf_op jit(solution)/shard_map/ppermute | solution.py:24
  144.7 67.3 %collective-permute-start.13 = (bf16[128,1536]{1,0:T(8,128)(2,1)S(1)}, bf16[128,1536]{1,0:T(8,128)(2,1)S(1)}, u32[]{:S(2)}, u32[]{:S(2)}) collective-permute-start(bf16[128,1536]{1,0:T(8,128)(2,1)S(1)} %slice.39), channel_id=1, source_target_pairs={{0,3},{1,2},{2,1},{3,0},{4,7},{5,6},{6,5},{7,4},{8,11},{9,10},{10,... | collective-permute-start | bytes 1179656 | tf_op jit(solution)/shard_map/ppermute | solution.py:24
  168.8 45.1 %collective-permute-start.12 = (bf16[128,512]{1,0:T(8,128)(2,1)S(1)}, bf16[128,512]{1,0:T(8,128)(2,1)S(1)}, u32[]{:S(2)}, u32[]{:S(2)}) collective-permute-start(bf16[128,512]{1,0:T(8,128)(2,1)S(1)} %slice.38), channel_id=1, source_target_pairs={{0,3},{1,2},{2,1},{3,0},{4,7},{5,6},{6,5},{7,4},{8,11},{9,10},{10,... | collective-permute-start | bytes 393224 | tf_op jit(solution)/shard_map/ppermute | solution.py:24

commit v5 on v4

--- a/solution.py
+++ b/solution.py
@@ -32,29 +32,26 @@
     return lax.dynamic_slice(state, (0, start), (rows, high - low))
 
 
-def lead_kernel(first, pos_ref, state_ref, out_ref, sem):
-    start = pl.multiple_of(first(pos_ref[0]), LANES)
+def lead_kernel(first, state_ref, out_ref, sem):
+    start = pl.multiple_of(first(lax.axis_index("member")), LANES)
     copy = pltpu.make_async_copy(state_ref.at[:, pl.ds(start, out_ref.shape[1])], out_ref, sem)
     copy.start()
     copy.wait()
 
 
-def lead_piece(position, state, step, width):
+def lead_piece(state, step, width):
     rows, total = state.shape
     patch = total // lax.axis_size("member")
     return pl.pallas_call(
         functools.partial(lead_kernel, lambda pos: (pos ^ step) * patch),
-        in_specs=[
-            pl.BlockSpec(memory_space=pltpu.SMEM),
-            pl.BlockSpec(memory_space=pl.ANY),
-        ],
+        in_specs=[pl.BlockSpec(memory_space=pl.ANY)],
         out_specs=pl.BlockSpec(memory_space=pltpu.VMEM),
         scratch_shapes=[pltpu.SemaphoreType.DMA],
         out_shape=pltpu.VMEM((rows, width), state.dtype),
         cost_estimate=pl.CostEstimate(
             flops=0, transcendentals=0, bytes_accessed=2 * rows * width
         ),
-    )(position, state)
+    )(state)
 
 
 def pick_kernel(pos_ref, start_ref, index_ref, own_ref, low_ref, high_ref, out_ref, pair_ref, pool):
@@ -171,33 +168,29 @@
     )(position, transform, state, *received, *([] if buffer is None else [buffer]))
 
 
-def place_kernel(first, pos_ref, piece_ref, buffer_ref, out_ref, sem):
+def place_kernel(first, piece_ref, buffer_ref, out_ref, sem):
     width = piece_ref.shape[1]
-    start = pl.multiple_of(first(pos_ref[0]), LANES)
+    start = pl.multiple_of(first(lax.axis_index("member")), LANES)
     copy = pltpu.make_async_copy(piece_ref, out_ref.at[:, pl.ds(start, width)], sem)
     copy.start()
     copy.wait()
 
 
-def place(position, buffer, piece, step, offset):
+def place(buffer, piece, step, offset):
     rows, width = piece.shape
     patch = buffer.shape[1] // lax.axis_size("member")
     return pl.pallas_call(
         functools.partial(place_kernel, lambda pos: (pos ^ step) * patch + offset),
-        in_specs=[
-            pl.BlockSpec(memory_space=pltpu.SMEM),
-            pl.BlockSpec(memory_space=pl.ANY),
-            pl.BlockSpec(memory_space=pl.ANY),
-        ],
+        in_specs=[pl.BlockSpec(memory_space=pl.ANY)] * 2,
         out_specs=pl.BlockSpec(memory_space=pl.ANY),
         scratch_shapes=[pltpu.SemaphoreType.DMA],
         compiler_params=pltpu.CompilerParams(vmem_limit_bytes=1 << 20),
         out_shape=jax.ShapeDtypeStruct(buffer.shape, buffer.dtype),
-        input_output_aliases={2: 0},
+        input_output_aliases={1: 0},
         cost_estimate=pl.CostEstimate(
             flops=0, transcendentals=0, bytes_accessed=2 * rows * width
         ),
-    )(position, piece, buffer)
+    )(piece, buffer)
 
 
 def product(left, right, dims):
@@ -260,7 +253,7 @@
     def send_chunk(chunk, order):
         return {step: send(chunk, step) for step in order}
 
-    piece = lead_piece(position, source, steps[0], state.shape[1] // (4 * count * CHUNKS))
+    piece = lead_piece(source, steps[0], state.shape[1] // (4 * count * CHUNKS))
     source, piece = lax.optimization_barrier((source, piece))
     head = swap(piece, steps[0])
     rest = send(0, steps[0], (0.25, 1))
@@ -298,7 +291,7 @@
             piece = swap(others[step - 1][:, low:high], step)
             returned.append((piece, step, chunk * width + low))
     for piece, step, offset in returned:
-        buffer = place(position, buffer, piece, step, offset)
+        buffer = place(buffer, piece, step, offset)
     return buffer
 
 

time: 215 us -> 215 us (level)
  no operation moved by 1% of the time
where the time goes in v5:
time: 215 us
  waiting for transfers between devices  139 us (65%)
  starting transfers between devices  25.5 us (12%)
  Pallas kernels  21.4 us (10%)
  matrix products  13.5 us (6%)
  local copies, waits for them, and re-layouts  12 us (6%)
    ppermute x17, waiting for transfers between devices, swap(): lax.ppermute(block, 'member', partners(lax.axis_size('member'), step))  139 us
    ppermute x17, starting transfers between devices, swap(): lax.ppermute(block, 'member', partners(lax.axis_size('member'), step))  25 us
    dot_general x8, matrix products, product(): lax.dot_general(left, right, (dims, ((), ())), preferred_element_type=jnp...  11.3 us
    dynamic_slice x6, local copies, waits for them, and re-layouts, cut(): return lax.dynamic_slice(state, (0, start), (rows, high - low))  10.5 us
    pallas_call x1, Pallas kernels, pick(): pl.pallas_call(pick_kernel, grid_spec=pltpu.PrefetchScalarGridSpec(num_sc...  8.61 us
    pallas_call x2, Pallas kernels, update_state(): pl.pallas_call(functools.partial(update_kernel, count, aliased), grid_spe...  6.33 us
    pallas_call x7, Pallas kernels, place(): pl.pallas_call(functools.partial(place_kernel, lambda pos: (pos ^ step) *...  5.44 us
  transfers between devices with their start and end apart: 19, of which 9 were waited for; matrix products, arithmetic and copies ran while one was open for 12% of the time, Pallas kernels for 9%

profile of v5, /device:TPU:12, one launch (start us, length us, event | category | flops | bytes accessed | tf_op | source)
XLA Modules:
  0.0 214.6 jit_solution(9916031618050877131)
XLA Ops:
  0.0 1.0 shard_map.65
  1.0 1.6 collective-permute-start.10
  2.7 1.0 constant_dynamic-slice_fusion.5
  3.7 0.5 collective-permute-start.11
  4.3 0.1 pad.9.clone
  4.3 0.3 maximum_maximum_fusion.own_ref
  4.7 0.4 collective-permute-start.1
  5.1 0.2 collective-permute-start
  5.3 1.9 constant_dynamic-slice_fusion.4
  7.2 1.9 constant_dynamic-slice_fusion.3
  9.1 1.9 constant_dynamic-slice_fusion.2
  11.0 1.9 constant_dynamic-slice_fusion.1
  12.9 1.9 constant_dynamic-slice_fusion
  14.8 0.1 reduce_min.9
  14.9 8.6 %shard_map.64 = (bf16[4,128,1024]{2,1,0:T(8,128)(2,1)S(1)}, bf16[16,1024]{1,0:T(8,128)(2,1)S(1)}) custom-call(s32[1]{0:T(128)} %bitcast.pos_ref, s32[4]{0:T(128)S(1)} %multiply_minimum_fusion.start_ref, s32[4,1,1024]{2,1,0:T(1,128)S(1)} %reshape.16.index_ref, bf16[144,4096]{1,0:T(8,128)(2,1)S(1)} %maximum_maximum_fusion.own_ref, ...), custom_call_target="tpu_custom_call" | custom-call | flops 2566914048 | bytes 2359296 | tf_op jit(solution)/shard_map/pallas_call | solution.py:89
  23.6 0.1 slice_bitcast_fusion.3
  23.6 1.6 collective-permute-start.4
  25.3 3.0 %collective-permute-start.3 = (bf16[128,1024]{1,0:T(8,128)(2,1)S(1)}, bf16[128,1024]{1,0:T(8,128)(2,1)S(1)}, u32[]{:S(2)}, u32[]{:S(2)}) collective-permute-start(bf16[128,1024]{1,0:T(8,128)(2,1)S(1)} %get-tuple-element.55), channel_id=1, source_target_pairs={{0,2},{1,3},{2,0},{3,1},{4,6},{5,7},{6,4},{7,5},{8,10},{9,11},{10,... | collective-permute-start | bytes 786440 | tf_op jit(solution)/shard_map/ppermute | solution.py:24
  28.3 1.2 collective-permute-start.2
  29.6 3.0 %collective-permute-start.6 = (bf16[128,2048]{1,0:T(8,128)(2,1)}, bf16[128,2048]{1,0:T(8,128)(2,1)S(1)}, u32[]{:S(2)}, u32[]{:S(2)}) collective-permute-start(bf16[128,2048]{1,0:T(8,128)(2,1)} %constant_dynamic-slice_fusion), channel_id=1, source_target_pairs={{0,2},{1,3},{2,0},{3,1},{4,6},{5,7},{6,4},{7,5},{8,10},{9,11},{10,... | collective-permute-start | bytes 1572872 | tf_op jit(solution)/shard_map/ppermute | solution.py:24
  32.6 0.9 pad_maximum_fusion.1.refs_3_
  33.6 10.4 %collective-permute-done.4 = bf16[128,1024]{1,0:T(8,128)(2,1)S(1)} collective-permute-done((bf16[128,1024]{1,0:T(8,128)(2,1)S(1)}, bf16[128,1024]{1,0:T(8,128)(2,1)S(1)}, u32[]{:S(2)}, u32[]{:S(2)}) %collective-permute-start.4) | collective-permute-done | bytes 262176 | tf_op jit(solution)/shard_map/ppermute | solution.py:24
  43.9 1.6 collective-permute-start.7
  45.5 14.4 %collective-permute-done.3 = bf16[128,1024]{1,0:T(8,128)(2,1)S(1)} collective-permute-done((bf16[128,1024]{1,0:T(8,128)(2,1)S(1)}, bf16[128,1024]{1,0:T(8,128)(2,1)S(1)}, u32[]{:S(2)}, u32[]{:S(2)}) %collective-permute-start.3) | collective-permute-done | bytes 262176 | tf_op jit(solution)/shard_map/ppermute | solution.py:24
  59.9 3.4 %collective-permute-start.9 = (bf16[128,2048]{1,0:T(8,128)(2,1)}, bf16[128,2048]{1,0:T(8,128)(2,1)S(1)}, u32[]{:S(2)}, u32[]{:S(2)}) collective-permute-start(bf16[128,2048]{1,0:T(8,128)(2,1)} %constant_dynamic-slice_fusion.3), channel_id=1, source_target_pairs={{0,2},{1,3},{2,0},{3,1},{4,6},{5,7},{6,4},{7,5},{8,10},{9,11},{10,... | collective-permute-start | bytes 1572872 | tf_op jit(solution)/shard_map/ppermute | solution.py:24
  63.3 0.2 convert_reduce_fusion
  63.5 2.3 %multiply_reduce_fusion = (f32[]{:T(128)}, f32[512,512]{1,0:T(8,128)}) fusion(f32[1024]{0:T(1024)S(1)} %bitcast.38, f32[1024]{0:T(1024)S(1)} %get-tuple-element.58, bf16[128,1024]{1,0:T(8,128)(2,1)S(1)} %collective-permute-done.4, bf16[128,1024]{1,0:T(8,128)(2,1)S(1)} %collective-permute-done.3, bf16[128,1024]{1,0:T(8,128)(2,1)S(1)} %collective-permute-done.2, ...), kind=kOutput, calls=%fused_computation.25 | convolution fusion | flops 543948800 | bytes 2105348 | tf_op jit(solution)/shard_map/dot_general | solution.py:197
  66.6 0.0 copy-start.14
  66.6 1.8 fusion.2
  68.4 0.4 convolution_convert_fusion.2
  68.8 0.4 convolution_convert_fusion.3
  69.2 0.4 copy-done.13
  69.6 0.4 fusion.3
  70.0 0.8 copy-done.2
  70.8 1.2 convolution_convert_fusion.1
  72.1 2.9 %fusion.4 = bf16[512,512]{1,0:T(8,128)(2,1)} fusion(bf16[512,512]{1,0:T(8,128)(2,1)} %convolution_convert_fusion.1, bf16[512,512]{1,0:T(8,128)(2,1)} %copy-done.13, bf16[512,512]{1,0:T(8,128)(2,1)} %copy-done.2), kind=kOutput, calls=%fused_computation.18 | convolution fusion | flops 538443776 | bytes 2097152 | tf_op jit(solution)/shard_map/dot_general | solution.py:197
  75.0 1.8 convolution_divide_fusion
  76.8 0.0 copy-start
  76.8 0.9 convolution_bitcast_fusion.1
  77.7 0.7 convolution_bitcast_fusion
  78.4 0.7 fusion.9
  79.1 0.1 fusion.7.transform_ref
  79.2 37.0 %collective-permute-done.9.refs_2_ = bf16[128,2048]{1,0:T(8,128)(2,1)S(1)} collective-permute-done((bf16[128,2048]{1,0:T(8,128)(2,1)}, bf16[128,2048]{1,0:T(8,128)(2,1)S(1)}, u32[]{:S(2)}, u32[]{:S(2)}) %collective-permute-start.9) | collective-permute-done | bytes 524320 | tf_op jit(solution)/shard_map/ppermute | solution.py:24
  116.3 3.2 %shard_map.66 = (bf16[128,16384]{1,0:T(8,128)(2,1)}, bf16[128,2048]{1,0:T(8,128)(2,1)S(1)}, bf16[128,2048]{1,0:T(8,128)(2,1)S(1)}, bf16[128,2048]{1,0:T(8,128)(2,1)S(1)}) custom-call(s32[1]{0:T(128)} %bitcast.pos_ref, bf16[512,512]{1,0:T(8,128)(2,1)S(1)} %fusion.7.transform_ref, bf16[128,16384]{1,0:T(8,128)(2,1)S(1)} %copy-done, ...), custom_call_target="tpu_custom_call" | custom-call | flops 1073741824 | bytes 4718592 | tf_op jit(solution)/shard_map/pallas_call | solution.py:148
  119.4 2.3 %collective-permute-start.17 = (bf16[128,2048]{1,0:T(8,128)(2,1)S(1)}, bf16[128,2048]{1,0:T(8,128)(2,1)S(1)}, u32[]{:S(2)}, u32[]{:S(2)}) collective-permute-start(bf16[128,2048]{1,0:T(8,128)(2,1)S(1)} %get-tuple-element.48), channel_id=1, source_target_pairs={{0,1},{1,0},{2,3},{3,2},{4,5},{5,4},{6,7},{7,6},{8,9},{9,8},{10,11... | collective-permute-start | bytes 1572872 | tf_op jit(solution)/shard_map/ppermute | solution.py:24
  121.7 1.0 collective-permute-start.18
  122.7 0.6 collective-permute-start.16
  123.3 3.2 %shard_map.67 = (bf16[128,16384]{1,0:T(8,128)(2,1)}, bf16[128,2048]{1,0:T(8,128)(2,1)S(1)}, bf16[128,2048]{1,0:T(8,128)(2,1)S(1)}, bf16[128,2048]{1,0:T(8,128)(2,1)S(1)}) custom-call(s32[1]{0:T(128)} %bitcast.pos_ref, bf16[512,512]{1,0:T(8,128)(2,1)S(1)} %fusion.7.transform_ref, bf16[128,16384]{1,0:T(8,128)(2,1)S(1)} %copy-done, ...), custom_call_target="tpu_custom_call", output_to_operand_aliasing={{0}: (6, {})} | custom-call | flops 1073741824 | bytes 4718592 | tf_op jit(solution)/shard_map/pallas_call | solution.py:148
  126.4 3.8 %collective-permute-start.15 = (bf16[128,2048]{1,0:T(8,128)(2,1)S(1)}, bf16[128,2048]{1,0:T(8,128)(2,1)S(1)}, u32[]{:S(2)}, u32[]{:S(2)}) collective-permute-start(bf16[128,2048]{1,0:T(8,128)(2,1)S(1)} %get-tuple-element.46), channel_id=1, source_target_pairs={{0,2},{1,3},{2,0},{3,1},{4,6},{5,7},{6,4},{7,5},{8,10},{9,11},{10,... | collective-permute-start | bytes 1572872 | tf_op jit(solution)/shard_map/ppermute | solution.py:24
  130.3 14.4 %collective-permute-done.17.piece_ref = bf16[128,2048]{1,0:T(8,128)(2,1)S(1)} collective-permute-done((bf16[128,2048]{1,0:T(8,128)(2,1)S(1)}, bf16[128,2048]{1,0:T(8,128)(2,1)S(1)}, u32[]{:S(2)}, u32[]{:S(2)}) %collective-permute-start.17) | collective-permute-done | bytes 524320 | tf_op jit(solution)/shard_map/ppermute | solution.py:24
  144.7 0.9 collective-permute-start.13
  145.6 23.3 %collective-permute-done.18.piece_ref = bf16[128,2048]{1,0:T(8,128)(2,1)S(1)} collective-permute-done((bf16[128,2048]{1,0:T(8,128)(2,1)S(1)}, bf16[128,2048]{1,0:T(8,128)(2,1)S(1)}, u32[]{:S(2)}, u32[]{:S(2)}) %collective-permute-start.18) | collective-permute-done | bytes 524320 | tf_op jit(solution)/shard_map/ppermute | solution.py:24
  168.8 0.4 collective-permute-start.12
  169.2 0.8 shard_map.68.buffer_ref
  170.0 0.8 shard_map.69.buffer_ref
  170.9 21.4 %collective-permute-done.16.piece_ref = bf16[128,2048]{1,0:T(8,128)(2,1)S(1)} collective-permute-done((bf16[128,2048]{1,0:T(8,128)(2,1)S(1)}, bf16[128,2048]{1,0:T(8,128)(2,1)S(1)}, u32[]{:S(2)}, u32[]{:S(2)}) %collective-permute-start.16) | collective-permute-done | bytes 524320 | tf_op jit(solution)/shard_map/ppermute | solution.py:24
  192.3 0.8 shard_map.70.buffer_ref
  193.1 9.4 %collective-permute-done.15.piece_ref = bf16[128,2048]{1,0:T(8,128)(2,1)S(1)} collective-permute-done((bf16[128,2048]{1,0:T(8,128)(2,1)S(1)}, bf16[128,2048]{1,0:T(8,128)(2,1)S(1)}, u32[]{:S(2)}, u32[]{:S(2)}) %collective-permute-start.15) | collective-permute-done | bytes 524320 | tf_op jit(solution)/shard_map/ppermute | solution.py:24
  202.5 0.8 shard_map.71.buffer_ref
  203.3 0.8 shard_map.72.buffer_ref
  204.2 7.8 %collective-permute-done.13.piece_ref = bf16[128,1536]{1,0:T(8,128)(2,1)S(1)} collective-permute-done((bf16[128,1536]{1,0:T(8,128)(2,1)S(1)}, bf16[128,1536]{1,0:T(8,128)(2,1)S(1)}, u32[]{:S(2)}, u32[]{:S(2)}) %collective-permute-start.13) | collective-permute-done | bytes 393248 | tf_op jit(solution)/shard_map/ppermute | solution.py:24
  212.0 0.8 shard_map.73.buffer_ref
  212.7 1.2 collective-permute-done.12.piece_ref
  213.9 0.7 shard_map.74
  (50 shorter events, 0.2 us)
Async XLA Ops:
  0.0 4.2 %copy-start.10 = (bf16[4096]{0:T(1024)(128)(2,1)S(1)}, bf16[4096]{0:T(1024)(128)(2,1)}, u32[]{:S(2)}) copy-start(bf16[4096]{0:T(1024)(128)(2,1)} %param.7) | copy-start | bytes 24580
  0.0 4.2 %copy-start.11 = (bf16[4096]{0:T(1024)(128)(2,1)S(1)}, bf16[4096]{0:T(1024)(128)(2,1)}, u32[]{:S(2)}) copy-start(bf16[4096]{0:T(1024)(128)(2,1)} %param.8) | copy-start | bytes 24580
  0.0 4.3 %copy-start.1 = (bf16[128,4096]{1,0:T(8,128)(2,1)S(1)}, bf16[128,4096]{1,0:T(8,128)(2,1)}, u32[]{:S(2)}) copy-start(bf16[128,4096]{1,0:T(8,128)(2,1)} %param.6) | copy-start | bytes 3145732
  1.0 28.6 %collective-permute-start.10 = (bf16[128,512]{1,0:T(8,128)(2,1)S(1)}, bf16[128,512]{1,0:T(8,128)(2,1)}, u32[]{:S(2)}, u32[]{:S(2)}) collective-permute-start(bf16[128,512]{1,0:T(8,128)(2,1)S(1)} %shard_map.65), channel_id=1, source_target_pairs={{0,3},{1,2},{2,1},{3,0},{4,7},{5,6},{6,5},{7,4},{8,11},{9,10},{10,... | collective-permute-start | bytes 393224 | tf_op jit(solution)/shard_map/ppermute | solution.py:24
  3.7 28.9 %collective-permute-start.11 = (bf16[128,1536]{1,0:T(8,128)(2,1)S(1)}, bf16[128,1536]{1,0:T(8,128)(2,1)S(1)}, u32[]{:S(2)}, u32[]{:S(2)}) collective-permute-start(bf16[128,1536]{1,0:T(8,128)(2,1)S(1)} %constant_dynamic-slice_fusion.5), channel_id=1, source_target_pairs={{0,3},{1,2},{2,1},{3,0},{4,7},{5,6},{6,5},{7,4},{8,11},{9,10},{10,... | collective-permute-start | bytes 1179656 | tf_op jit(solution)/shard_map/ppermute | solution.py:24
  4.7 10.2 %collective-permute-start.1 = (bf16[144,1024]{1,0:T(8,128)(2,1)S(1)}, bf16[144,1024]{1,0:T(8,128)(2,1)S(1)}, u32[]{:S(2)}, u32[]{:S(2)}) collective-permute-start(bf16[144,1024]{1,0:T(8,128)(2,1)S(1)} %get-tuple-element.51), channel_id=1, source_target_pairs={{0,28},{4,0},{8,4},{12,8},{16,12},{20,16},{24,20},{28,24},{1,29},{... | collective-permute-start | bytes 884744 | tf_op jit(solution)/shard_map/ppermute | solution.py:232
  5.1 9.9 %collective-permute-start = (bf16[144,1024]{1,0:T(8,128)(2,1)S(1)}, bf16[144,1024]{1,0:T(8,128)(2,1)S(1)}, u32[]{:S(2)}, u32[]{:S(2)}) collective-permute-start(bf16[144,1024]{1,0:T(8,128)(2,1)S(1)} %get-tuple-element.52), channel_id=1, source_target_pairs={{0,4},{4,8},{8,12},{12,16},{16,20},{20,24},{24,28},{28,0},{1,5},{5... | collective-permute-start | bytes 884744 | tf_op jit(solution)/shard_map/ppermute | solution.py:232
  7.2 7.6 %copy-start.9 = (s32[4,1024]{1,0:T(4,128)S(1)}, s32[4,1024]{1,0:T(4,128)}, u32[]{:S(2)}) copy-start(s32[4,1024]{1,0:T(4,128)} %param.9) | copy-start | bytes 49156
  23.5 6.0 %copy-start.12 = (f32[1,1024]{1,0:T(1,128)S(1)}, f32[1,1024]{1,0:T(1,128)}, u32[]{:S(2)}) copy-start(f32[1,1024]{1,0:T(1,128)} %param.10) | copy-start | bytes 12292
  23.6 20.3 %collective-permute-start.4 = (bf16[128,1024]{1,0:T(8,128)(2,1)S(1)}, bf16[128,1024]{1,0:T(8,128)(2,1)S(1)}, u32[]{:S(2)}, u32[]{:S(2)}) collective-permute-start(bf16[128,1024]{1,0:T(8,128)(2,1)S(1)} %get-tuple-element.54), channel_id=1, source_target_pairs={{0,3},{1,2},{2,1},{3,0},{4,7},{5,6},{6,5},{7,4},{8,11},{9,10},{10,... | collective-permute-start | bytes 786440 | tf_op jit(solution)/shard_map/ppermute | solution.py:24
  25.3 34.6 %collective-permute-start.3 = (bf16[128,1024]{1,0:T(8,128)(2,1)S(1)}, bf16[128,1024]{1,0:T(8,128)(2,1)S(1)}, u32[]{:S(2)}, u32[]{:S(2)}) collective-permute-start(bf16[128,1024]{1,0:T(8,128)(2,1)S(1)} %get-tuple-element.55), channel_id=1, source_target_pairs={{0,2},{1,3},{2,0},{3,1},{4,6},{5,7},{6,4},{7,5},{8,10},{9,11},{10,... | collective-permute-start | bytes 786440 | tf_op jit(solution)/shard_map/ppermute | solution.py:24
  28.3 35.0 %collective-permute-start.2 = (bf16[128,1024]{1,0:T(8,128)(2,1)S(1)}, bf16[128,1024]{1,0:T(8,128)(2,1)S(1)}, u32[]{:S(2)}, u32[]{:S(2)}) collective-permute-start(bf16[128,1024]{1,0:T(8,128)(2,1)S(1)} %get-tuple-element.56), channel_id=1, source_target_pairs={{0,1},{1,0},{2,3},{3,2},{4,5},{5,4},{6,7},{7,6},{8,9},{9,8},{10,11... | collective-permute-start | bytes 786440 | tf_op jit(solution)/shard_map/ppermute | solution.py:24
  29.6 93.1 %collective-permute-start.6 = (bf16[128,2048]{1,0:T(8,128)(2,1)}, bf16[128,2048]{1,0:T(8,128)(2,1)S(1)}, u32[]{:S(2)}, u32[]{:S(2)}) collective-permute-start(bf16[128,2048]{1,0:T(8,128)(2,1)} %constant_dynamic-slice_fusion), channel_id=1, source_target_pairs={{0,2},{1,3},{2,0},{3,1},{4,6},{5,7},{6,4},{7,5},{8,10},{9,11},{10,... | collective-permute-start | bytes 1572872 | tf_op jit(solution)/shard_map/ppermute | solution.py:24
  32.6 90.7 %collective-permute-start.5 = (bf16[128,2048]{1,0:T(8,128)(2,1)}, bf16[128,2048]{1,0:T(8,128)(2,1)S(1)}, u32[]{:S(2)}, u32[]{:S(2)}) collective-permute-start(bf16[128,2048]{1,0:T(8,128)(2,1)} %constant_dynamic-slice_fusion.1), channel_id=1, source_target_pairs={{0,1},{1,0},{2,3},{3,2},{4,5},{5,4},{6,7},{7,6},{8,9},{9,8},{10,11... | collective-permute-start | bytes 1572872 | tf_op jit(solution)/shard_map/ppermute | solution.py:24
  43.9 21.9 %copy-start.3 = (bf16[128,1024]{1,0:T(8,128)(2,1)}, bf16[128,1024]{1,0:T(8,128)(2,1)S(1)}, u32[]{:S(2)}) copy-start(bf16[128,1024]{1,0:T(8,128)(2,1)S(1)} %collective-permute-done.4) | copy-start | bytes 786436
  43.9 79.3 %collective-permute-start.7 = (bf16[128,2048]{1,0:T(8,128)(2,1)}, bf16[128,2048]{1,0:T(8,128)(2,1)S(1)}, u32[]{:S(2)}, u32[]{:S(2)}) collective-permute-start(bf16[128,2048]{1,0:T(8,128)(2,1)} %constant_dynamic-slice_fusion.2), channel_id=1, source_target_pairs={{0,3},{1,2},{2,1},{3,0},{4,7},{5,6},{6,5},{7,4},{8,11},{9,10},{10,... | collective-permute-start | bytes 1572872 | tf_op jit(solution)/shard_map/ppermute | solution.py:24
  59.9 5.9 %copy-start.5 = (bf16[128,1024]{1,0:T(8,128)(2,1)}, bf16[128,1024]{1,0:T(8,128)(2,1)S(1)}, u32[]{:S(2)}) copy-start(bf16[128,1024]{1,0:T(8,128)(2,1)S(1)} %collective-permute-done.3) | copy-start | bytes 786436
  59.9 56.3 %collective-permute-start.9 = (bf16[128,2048]{1,0:T(8,128)(2,1)}, bf16[128,2048]{1,0:T(8,128)(2,1)S(1)}, u32[]{:S(2)}, u32[]{:S(2)}) collective-permute-start(bf16[128,2048]{1,0:T(8,128)(2,1)} %constant_dynamic-slice_fusion.3), channel_id=1, source_target_pairs={{0,2},{1,3},{2,0},{3,1},{4,6},{5,7},{6,4},{7,5},{8,10},{9,11},{10,... | collective-permute-start | bytes 1572872 | tf_op jit(solution)/shard_map/ppermute | solution.py:24
  63.3 2.5 %copy-start.7 = (bf16[128,1024]{1,0:T(8,128)(2,1)}, bf16[128,1024]{1,0:T(8,128)(2,1)S(1)}, u32[]{:S(2)}) copy-start(bf16[128,1024]{1,0:T(8,128)(2,1)S(1)} %collective-permute-done.2) | copy-start | bytes 786436
  63.3 52.9 %collective-permute-start.8 = (bf16[128,2048]{1,0:T(8,128)(2,1)}, bf16[128,2048]{1,0:T(8,128)(2,1)S(1)}, u32[]{:S(2)}, u32[]{:S(2)}) collective-permute-start(bf16[128,2048]{1,0:T(8,128)(2,1)} %constant_dynamic-slice_fusion.4), channel_id=1, source_target_pairs={{0,1},{1,0},{2,3},{3,2},{4,5},{5,4},{6,7},{7,6},{8,9},{9,8},{10,11... | collective-permute-start | bytes 1572872 | tf_op jit(solution)/shard_map/ppermute | solution.py:24
  66.6 1.8 copy-start.14
  68.8 0.8 copy-start.13
  70.0 0.8 copy-start.2
  75.0 1.8 copy-start.4
  75.0 1.8 copy-start.6
  75.0 1.8 copy-start.8
  76.8 39.4 %copy-start = (bf16[128,16384]{1,0:T(8,128)(2,1)S(1)}, bf16[128,16384]{1,0:T(8,128)(2,1)}, u32[]{:S(2)}) copy-start(bf16[128,16384]{1,0:T(8,128)(2,1)} %refs_0_.3) | copy-start | bytes 12582916
  119.4 25.3 %collective-permute-start.17 = (bf16[128,2048]{1,0:T(8,128)(2,1)S(1)}, bf16[128,2048]{1,0:T(8,128)(2,1)S(1)}, u32[]{:S(2)}, u32[]{:S(2)}) collective-permute-start(bf16[128,2048]{1,0:T(8,128)(2,1)S(1)} %get-tuple-element.48), channel_id=1, source_target_pairs={{0,1},{1,0},{2,3},{3,2},{4,5},{5,4},{6,7},{7,6},{8,9},{9,8},{10,11... | collective-permute-start | bytes 1572872 | tf_op jit(solution)/shard_map/ppermute | solution.py:24
  121.7 47.1 %collective-permute-start.18 = (bf16[128,2048]{1,0:T(8,128)(2,1)S(1)}, bf16[128,2048]{1,0:T(8,128)(2,1)S(1)}, u32[]{:S(2)}, u32[]{:S(2)}) collective-permute-start(bf16[128,2048]{1,0:T(8,128)(2,1)S(1)} %get-tuple-element.49), channel_id=1, source_target_pairs={{0,2},{1,3},{2,0},{3,1},{4,6},{5,7},{6,4},{7,5},{8,10},{9,11},{10,... | collective-permute-start | bytes 1572872 | tf_op jit(solution)/shard_map/ppermute | solution.py:24
  122.7 69.6 %collective-permute-start.16 = (bf16[128,2048]{1,0:T(8,128)(2,1)S(1)}, bf16[128,2048]{1,0:T(8,128)(2,1)S(1)}, u32[]{:S(2)}, u32[]{:S(2)}) collective-permute-start(bf16[128,2048]{1,0:T(8,128)(2,1)S(1)} %get-tuple-element.47), channel_id=1, source_target_pairs={{0,3},{1,2},{2,1},{3,0},{4,7},{5,6},{6,5},{7,4},{8,11},{9,10},{10,... | collective-permute-start | bytes 1572872 | tf_op jit(solution)/shard_map/ppermute | solution.py:24
  126.4 76.1 %collective-permute-start.15 = (bf16[128,2048]{1,0:T(8,128)(2,1)S(1)}, bf16[128,2048]{1,0:T(8,128)(2,1)S(1)}, u32[]{:S(2)}, u32[]{:S(2)}) collective-permute-start(bf16[128,2048]{1,0:T(8,128)(2,1)S(1)} %get-tuple-element.46), channel_id=1, source_target_pairs={{0,2},{1,3},{2,0},{3,1},{4,6},{5,7},{6,4},{7,5},{8,10},{9,11},{10,... | collective-permute-start | bytes 1572872 | tf_op jit(solution)/shard_map/ppermute | solution.py:24
  130.3 73.1 %collective-permute-start.14 = (bf16[128,2048]{1,0:T(8,128)(2,1)S(1)}, bf16[128,2048]{1,0:T(8,128)(2,1)S(1)}, u32[]{:S(2)}, u32[]{:S(2)}) collective-permute-start(bf16[128,2048]{1,0:T(8,128)(2,1)S(1)} %get-tuple-element.45), channel_id=1, source_target_pairs={{0,1},{1,0},{2,3},{3,2},{4,5},{5,4},{6,7},{7,6},{8,9},{9,8},{10,11... | collective-permute-start | bytes 1572872 | tf_op jit(solution)/shard_map/ppermute | solution.py:24
  144.7 67.3 %collective-permute-start.13 = (bf16[128,1536]{1,0:T(8,128)(2,1)S(1)}, bf16[128,1536]{1,0:T(8,128)(2,1)S(1)}, u32[]{:S(2)}, u32[]{:S(2)}) collective-permute-start(bf16[128,1536]{1,0:T(8,128)(2,1)S(1)} %slice.39), channel_id=1, source_target_pairs={{0,3},{1,2},{2,1},{3,0},{4,7},{5,6},{6,5},{7,4},{8,11},{9,10},{10,... | collective-permute-start | bytes 1179656 | tf_op jit(solution)/shard_map/ppermute | solution.py:24
  168.8 45.1 %collective-permute-start.12 = (bf16[128,512]{1,0:T(8,128)(2,1)S(1)}, bf16[128,512]{1,0:T(8,128)(2,1)S(1)}, u32[]{:S(2)}, u32[]{:S(2)}) collective-permute-start(bf16[128,512]{1,0:T(8,128)(2,1)S(1)} %slice.38), channel_id=1, source_target_pairs={{0,3},{1,2},{2,1},{3,0},{4,7},{5,6},{6,5},{7,4},{8,11},{9,10},{10,... | collective-permute-start | bytes 393224 | tf_op jit(solution)/shard_map/ppermute | solution.py:24

commit v6 on v3

--- a/solution.py
+++ b/solution.py
@@ -13,7 +13,7 @@
 LANES = 128
 WINDOW = 2 * LOC
 CHUNKS = 2
-BLOCK = 512
+BLOCK = 1024
 
 
 def partners(count, step):
@@ -148,16 +148,17 @@
 
 def place_kernel(first, pos_ref, piece_ref, buffer_ref, out_ref, sem):
     width = piece_ref.shape[1]
-    start = pl.multiple_of(first(pos_ref[0]) * width, LANES)
+    start = pl.multiple_of(first(pos_ref[0]), LANES)
     copy = pltpu.make_async_copy(piece_ref, out_ref.at[:, pl.ds(start, width)], sem)
     copy.start()
     copy.wait()
 
 
-def place(position, buffer, piece, step, chunk):
+def place(position, buffer, piece, step, offset):
     rows, width = piece.shape
+    patch = buffer.shape[1] // lax.axis_size("member")
     return pl.pallas_call(
-        functools.partial(place_kernel, lambda pos: (pos ^ step) * CHUNKS + chunk),
+        functools.partial(place_kernel, lambda pos: (pos ^ step) * patch + offset),
         in_specs=[
             pl.BlockSpec(memory_space=pltpu.SMEM),
             pl.BlockSpec(memory_space=pl.ANY),
@@ -256,14 +257,21 @@
 
     buffer, returned = None, []
     back = steps[:0:-1] + steps[:1]
+    width = state.shape[1] // (count * CHUNKS)
     for chunk in range(CHUNKS):
         received = [arrived[chunk][step] for step in range(1, count)]
         buffer, *others = update_state(position, transform, state, received, chunk, buffer)
-        returned.append({step: swap(others[step - 1], step) for step in back[:-1]})
-        returned[-1][back[-1]] = swap(others[back[-1] - 1], back[-1])
-    for chunk in range(CHUNKS):
-        for step in back:
-            buffer = place(position, buffer, returned[chunk][step], step, chunk)
+        last = chunk == CHUNKS - 1
+        for step in back[:-1]:
+            returned.append((swap(others[step - 1], step), step, chunk * width))
+        step, cuts = back[-1], [0, width]
+        if last:
+            cuts = [0, width * 3 // 4, width]
+        for low, high in zip(cuts, cuts[1:]):
+            piece = swap(others[step - 1][:, low:high], step)
+            returned.append((piece, step, chunk * width + low))
+    for piece, step, offset in returned:
+        buffer = place(position, buffer, piece, step, offset)
     return buffer
 
 

time: 218 us -> 217 us (level)
  the two profiles are of different devices: /device:TPU:13 before, /device:TPU:12 now
where the time goes in v6:
time: 217 us
  waiting for transfers between devices  141 us (65%)
  starting transfers between devices  25.5 us (12%)
  Pallas kernels  19.4 us (9%)
  local copies, waits for them, and re-layouts  13.9 us (6%)
  matrix products  13.6 us (6%)
    ppermute x17, waiting for transfers between devices, swap(): lax.ppermute(block, 'member', partners(lax.axis_size('member'), step))  141 us
    ppermute x17, starting transfers between devices, swap(): lax.ppermute(block, 'member', partners(lax.axis_size('member'), step))  25 us
    dynamic_slice x7, local copies, waits for them, and re-layouts, cut(): return lax.dynamic_slice(state, (0, start), (rows, high - low))  11.4 us
    dot_general x8, matrix products, product(): lax.dot_general(left, right, (dims, ((), ())), preferred_element_type=jnp...  11.4 us
    pallas_call x1, Pallas kernels, pick(): pl.pallas_call(pick_kernel, grid_spec=pltpu.PrefetchScalarGridSpec(num_sc...  8.61 us
    pallas_call x7, Pallas kernels, place(): pl.pallas_call(functools.partial(place_kernel, lambda pos: (pos ^ step) *...  5.43 us
    pallas_call x2, Pallas kernels, update_state(): pl.pallas_call(functools.partial(update_kernel, count, aliased), grid_spe...  5.35 us
  transfers between devices with their start and end apart: 19, of which 9 were waited for; matrix products, arithmetic and copies ran while one was open for 13% of the time, Pallas kernels for 9%

profile of v6, /device:TPU:12, one launch (start us, length us, event | category | flops | bytes accessed | tf_op | source)
XLA Modules:
  0.0 216.6 jit_solution(13937363661707282181)
XLA Ops:
  0.0 0.9 constant_dynamic-slice_fusion.6
  0.9 1.6 collective-permute-start.10
  2.6 1.0 constant_dynamic-slice_fusion.5
  3.6 0.5 collective-permute-start.11
  4.1 0.7 broadcast_in_dim.12
  4.8 0.7 broadcast_in_dim.13
  5.5 0.1 pad.9.clone
  5.6 1.5 maximum_maximum_fusion.own_ref
  7.2 0.4 collective-permute-start.1
  7.5 0.2 collective-permute-start
  7.7 1.9 constant_dynamic-slice_fusion.4
  9.6 1.9 constant_dynamic-slice_fusion.3
  11.5 1.9 constant_dynamic-slice_fusion.2
  13.4 1.9 constant_dynamic-slice_fusion.1
  15.3 1.9 constant_dynamic-slice_fusion
  17.2 0.1 reduce_min.9
  17.4 8.6 %shard_map.64 = (bf16[4,128,1024]{2,1,0:T(8,128)(2,1)S(1)}, bf16[16,1024]{1,0:T(8,128)(2,1)S(1)}) custom-call(s32[1]{0:T(128)} %bitcast.pos_ref, s32[4]{0:T(128)S(1)} %multiply_minimum_fusion.start_ref, s32[4,1,1024]{2,1,0:T(1,128)S(1)} %reshape.16.index_ref, bf16[144,4096]{1,0:T(8,128)(2,1)S(1)} %maximum_maximum_fusion.own_ref, ...), custom_call_target="tpu_custom_call" | custom-call | flops 2566914048 | bytes 2359296 | tf_op jit(solution)/shard_map/pallas_call | solution.py:67
  26.0 0.0 copy-start.9
  26.0 0.1 slice_bitcast_fusion.3
  26.1 1.6 collective-permute-start.4
  27.8 3.0 %collective-permute-start.3 = (bf16[128,1024]{1,0:T(8,128)(2,1)S(1)}, bf16[128,1024]{1,0:T(8,128)(2,1)S(1)}, u32[]{:S(2)}, u32[]{:S(2)}) collective-permute-start(bf16[128,1024]{1,0:T(8,128)(2,1)S(1)} %get-tuple-element.55), channel_id=1, source_target_pairs={{0,2},{1,3},{2,0},{3,1},{4,6},{5,7},{6,4},{7,5},{8,10},{9,11},{10,... | collective-permute-start | bytes 786440 | tf_op jit(solution)/shard_map/ppermute | solution.py:24
  30.8 1.2 collective-permute-start.2
  32.1 3.0 %collective-permute-start.6 = (bf16[128,2048]{1,0:T(8,128)(2,1)}, bf16[128,2048]{1,0:T(8,128)(2,1)S(1)}, u32[]{:S(2)}, u32[]{:S(2)}) collective-permute-start(bf16[128,2048]{1,0:T(8,128)(2,1)} %constant_dynamic-slice_fusion), channel_id=1, source_target_pairs={{0,2},{1,3},{2,0},{3,1},{4,6},{5,7},{6,4},{7,5},{8,10},{9,11},{10,... | collective-permute-start | bytes 1572872 | tf_op jit(solution)/shard_map/ppermute | solution.py:24
  35.1 11.3 %collective-permute-done.4 = bf16[128,1024]{1,0:T(8,128)(2,1)S(1)} collective-permute-done((bf16[128,1024]{1,0:T(8,128)(2,1)S(1)}, bf16[128,1024]{1,0:T(8,128)(2,1)S(1)}, u32[]{:S(2)}, u32[]{:S(2)}) %collective-permute-start.4) | collective-permute-done | bytes 262176 | tf_op jit(solution)/shard_map/ppermute | solution.py:24
  46.4 1.6 collective-permute-start.7
  48.0 14.4 %collective-permute-done.3 = bf16[128,1024]{1,0:T(8,128)(2,1)S(1)} collective-permute-done((bf16[128,1024]{1,0:T(8,128)(2,1)S(1)}, bf16[128,1024]{1,0:T(8,128)(2,1)S(1)}, u32[]{:S(2)}, u32[]{:S(2)}) %collective-permute-start.3) | collective-permute-done | bytes 262176 | tf_op jit(solution)/shard_map/ppermute | solution.py:24
  62.4 3.4 %collective-permute-start.9 = (bf16[128,2048]{1,0:T(8,128)(2,1)}, bf16[128,2048]{1,0:T(8,128)(2,1)S(1)}, u32[]{:S(2)}, u32[]{:S(2)}) collective-permute-start(bf16[128,2048]{1,0:T(8,128)(2,1)} %constant_dynamic-slice_fusion.3), channel_id=1, source_target_pairs={{0,2},{1,3},{2,0},{3,1},{4,6},{5,7},{6,4},{7,5},{8,10},{9,11},{10,... | collective-permute-start | bytes 1572872 | tf_op jit(solution)/shard_map/ppermute | solution.py:24
  65.8 0.2 convert_reduce_fusion
  66.0 2.4 %multiply_reduce_fusion = (f32[]{:T(128)}, f32[512,512]{1,0:T(8,128)}) fusion(f32[1024]{0:T(1024)S(1)} %bitcast.38, f32[1024]{0:T(1024)S(1)} %get-tuple-element.58, bf16[128,1024]{1,0:T(8,128)(2,1)S(1)} %collective-permute-done.4, bf16[128,1024]{1,0:T(8,128)(2,1)S(1)} %collective-permute-done.3, bf16[128,1024]{1,0:T(8,128)(2,1)S(1)} %collective-permute-done.2, ...), kind=kOutput, calls=%fused_computation.25 | convolution fusion | flops 543948800 | bytes 2105348 | tf_op jit(solution)/shard_map/dot_general | solution.py:179
  69.2 0.0 copy-start.11
  69.2 1.8 fusion.2
  71.0 0.4 convolution_convert_fusion.2
  71.4 0.4 convolution_convert_fusion.3
  71.8 0.4 fusion.3
  72.3 0.8 copy-done.1
  73.1 1.2 convolution_convert_fusion.1
  74.3 2.9 %fusion.4 = bf16[512,512]{1,0:T(8,128)(2,1)} fusion(bf16[512,512]{1,0:T(8,128)(2,1)} %convolution_convert_fusion.1, bf16[512,512]{1,0:T(8,128)(2,1)} %copy-done.10, bf16[512,512]{1,0:T(8,128)(2,1)} %copy-done.1), kind=kOutput, calls=%fused_computation.18 | convolution fusion | flops 538443776 | bytes 2097152 | tf_op jit(solution)/shard_map/dot_general | solution.py:179
  77.3 1.8 convolution_divide_fusion
  79.1 0.9 convolution_bitcast_fusion.1
  80.0 0.7 convolution_bitcast_fusion
  80.7 0.7 fusion.9
  81.3 0.1 fusion.7.transform_ref
  81.4 37.3 %collective-permute-done.9.refs_2_ = bf16[128,2048]{1,0:T(8,128)(2,1)S(1)} collective-permute-done((bf16[128,2048]{1,0:T(8,128)(2,1)}, bf16[128,2048]{1,0:T(8,128)(2,1)S(1)}, u32[]{:S(2)}, u32[]{:S(2)}) %collective-permute-start.9) | collective-permute-done | bytes 524320 | tf_op jit(solution)/shard_map/ppermute | solution.py:24
  118.7 2.7 %shard_map.65 = (bf16[128,16384]{1,0:T(8,128)(2,1)}, bf16[128,2048]{1,0:T(8,128)(2,1)S(1)}, bf16[128,2048]{1,0:T(8,128)(2,1)S(1)}, bf16[128,2048]{1,0:T(8,128)(2,1)S(1)}) custom-call(s32[1]{0:T(128)} %bitcast.pos_ref, bf16[512,512]{1,0:T(8,128)(2,1)S(1)} %fusion.7.transform_ref, bf16[128,16384]{1,0:T(8,128)(2,1)S(1)} %copy-done, ...), custom_call_target="tpu_custom_call" | custom-call | flops 1073741824 | bytes 4718592 | tf_op jit(solution)/shard_map/pallas_call | solution.py:126
  121.4 2.3 %collective-permute-start.17 = (bf16[128,2048]{1,0:T(8,128)(2,1)S(1)}, bf16[128,2048]{1,0:T(8,128)(2,1)S(1)}, u32[]{:S(2)}, u32[]{:S(2)}) collective-permute-start(bf16[128,2048]{1,0:T(8,128)(2,1)S(1)} %get-tuple-element.48), channel_id=1, source_target_pairs={{0,1},{1,0},{2,3},{3,2},{4,5},{5,4},{6,7},{7,6},{8,9},{9,8},{10,11... | collective-permute-start | bytes 1572872 | tf_op jit(solution)/shard_map/ppermute | solution.py:24
  123.7 1.0 collective-permute-start.18
  124.7 0.6 collective-permute-start.16
  125.3 2.7 %shard_map.66 = (bf16[128,16384]{1,0:T(8,128)(2,1)}, bf16[128,2048]{1,0:T(8,128)(2,1)S(1)}, bf16[128,2048]{1,0:T(8,128)(2,1)S(1)}, bf16[128,2048]{1,0:T(8,128)(2,1)S(1)}) custom-call(s32[1]{0:T(128)} %bitcast.pos_ref, bf16[512,512]{1,0:T(8,128)(2,1)S(1)} %fusion.7.transform_ref, bf16[128,16384]{1,0:T(8,128)(2,1)S(1)} %copy-done, ...), custom_call_target="tpu_custom_call", output_to_operand_aliasing={{0}: (6, {})} | custom-call | flops 1073741824 | bytes 4718592 | tf_op jit(solution)/shard_map/pallas_call | solution.py:126
  127.9 3.8 %collective-permute-start.15 = (bf16[128,2048]{1,0:T(8,128)(2,1)S(1)}, bf16[128,2048]{1,0:T(8,128)(2,1)S(1)}, u32[]{:S(2)}, u32[]{:S(2)}) collective-permute-start(bf16[128,2048]{1,0:T(8,128)(2,1)S(1)} %get-tuple-element.46), channel_id=1, source_target_pairs={{0,2},{1,3},{2,0},{3,1},{4,6},{5,7},{6,4},{7,5},{8,10},{9,11},{10,... | collective-permute-start | bytes 1572872 | tf_op jit(solution)/shard_map/ppermute | solution.py:24
  131.8 14.9 %collective-permute-done.17.piece_ref = bf16[128,2048]{1,0:T(8,128)(2,1)S(1)} collective-permute-done((bf16[128,2048]{1,0:T(8,128)(2,1)S(1)}, bf16[128,2048]{1,0:T(8,128)(2,1)S(1)}, u32[]{:S(2)}, u32[]{:S(2)}) %collective-permute-start.17) | collective-permute-done | bytes 524320 | tf_op jit(solution)/shard_map/ppermute | solution.py:24
  146.7 0.9 collective-permute-start.13
  147.5 23.3 %collective-permute-done.18.piece_ref = bf16[128,2048]{1,0:T(8,128)(2,1)S(1)} collective-permute-done((bf16[128,2048]{1,0:T(8,128)(2,1)S(1)}, bf16[128,2048]{1,0:T(8,128)(2,1)S(1)}, u32[]{:S(2)}, u32[]{:S(2)}) %collective-permute-start.18) | collective-permute-done | bytes 524320 | tf_op jit(solution)/shard_map/ppermute | solution.py:24
  170.8 0.4 collective-permute-start.12
  171.2 0.8 shard_map.67.buffer_ref
  172.0 0.8 shard_map.68.buffer_ref
  172.8 21.4 %collective-permute-done.16.piece_ref = bf16[128,2048]{1,0:T(8,128)(2,1)S(1)} collective-permute-done((bf16[128,2048]{1,0:T(8,128)(2,1)S(1)}, bf16[128,2048]{1,0:T(8,128)(2,1)S(1)}, u32[]{:S(2)}, u32[]{:S(2)}) %collective-permute-start.16) | collective-permute-done | bytes 524320 | tf_op jit(solution)/shard_map/ppermute | solution.py:24
  194.3 0.8 shard_map.69.buffer_ref
  195.1 9.4 %collective-permute-done.15.piece_ref = bf16[128,2048]{1,0:T(8,128)(2,1)S(1)} collective-permute-done((bf16[128,2048]{1,0:T(8,128)(2,1)S(1)}, bf16[128,2048]{1,0:T(8,128)(2,1)S(1)}, u32[]{:S(2)}, u32[]{:S(2)}) %collective-permute-start.15) | collective-permute-done | bytes 524320 | tf_op jit(solution)/shard_map/ppermute | solution.py:24
  204.5 0.8 shard_map.70.buffer_ref
  205.3 0.8 shard_map.71.buffer_ref
  206.1 7.8 %collective-permute-done.13.piece_ref = bf16[128,1536]{1,0:T(8,128)(2,1)S(1)} collective-permute-done((bf16[128,1536]{1,0:T(8,128)(2,1)S(1)}, bf16[128,1536]{1,0:T(8,128)(2,1)S(1)}, u32[]{:S(2)}, u32[]{:S(2)}) %collective-permute-start.13) | collective-permute-done | bytes 393248 | tf_op jit(solution)/shard_map/ppermute | solution.py:24
  213.9 0.8 shard_map.72.buffer_ref
  214.7 1.2 collective-permute-done.12.piece_ref
  215.9 0.7 shard_map.73
  (44 shorter events, 0.3 us)
Async XLA Ops:
  0.9 31.2 %collective-permute-start.10 = (bf16[128,512]{1,0:T(8,128)(2,1)S(1)}, bf16[128,512]{1,0:T(8,128)(2,1)S(1)}, u32[]{:S(2)}, u32[]{:S(2)}) collective-permute-start(bf16[128,512]{1,0:T(8,128)(2,1)S(1)} %constant_dynamic-slice_fusion.6), channel_id=1, source_target_pairs={{0,3},{1,2},{2,1},{3,0},{4,7},{5,6},{6,5},{7,4},{8,11},{9,10},{10,... | collective-permute-start | bytes 393224 | tf_op jit(solution)/shard_map/ppermute | solution.py:24
  3.6 31.5 %collective-permute-start.11 = (bf16[128,1536]{1,0:T(8,128)(2,1)S(1)}, bf16[128,1536]{1,0:T(8,128)(2,1)S(1)}, u32[]{:S(2)}, u32[]{:S(2)}) collective-permute-start(bf16[128,1536]{1,0:T(8,128)(2,1)S(1)} %constant_dynamic-slice_fusion.5), channel_id=1, source_target_pairs={{0,3},{1,2},{2,1},{3,0},{4,7},{5,6},{6,5},{7,4},{8,11},{9,10},{10,... | collective-permute-start | bytes 1179656 | tf_op jit(solution)/shard_map/ppermute | solution.py:24
  7.2 10.2 %collective-permute-start.1 = (bf16[144,1024]{1,0:T(8,128)(2,1)S(1)}, bf16[144,1024]{1,0:T(8,128)(2,1)S(1)}, u32[]{:S(2)}, u32[]{:S(2)}) collective-permute-start(bf16[144,1024]{1,0:T(8,128)(2,1)S(1)} %get-tuple-element.51), channel_id=1, source_target_pairs={{0,28},{4,0},{8,4},{12,8},{16,12},{20,16},{24,20},{28,24},{1,29},{... | collective-permute-start | bytes 884744 | tf_op jit(solution)/shard_map/ppermute | solution.py:214
  7.5 9.9 %collective-permute-start = (bf16[144,1024]{1,0:T(8,128)(2,1)S(1)}, bf16[144,1024]{1,0:T(8,128)(2,1)S(1)}, u32[]{:S(2)}, u32[]{:S(2)}) collective-permute-start(bf16[144,1024]{1,0:T(8,128)(2,1)S(1)} %get-tuple-element.52), channel_id=1, source_target_pairs={{0,4},{4,8},{8,12},{12,16},{16,20},{20,24},{24,28},{28,0},{1,5},{5... | collective-permute-start | bytes 884744 | tf_op jit(solution)/shard_map/ppermute | solution.py:214
  9.6 7.6 %copy-start.8 = (s32[4,1024]{1,0:T(4,128)S(1)}, s32[4,1024]{1,0:T(4,128)}, u32[]{:S(2)}) copy-start(s32[4,1024]{1,0:T(4,128)} %param.9) | copy-start | bytes 49156
  26.0 6.0 %copy-start.9 = (f32[1,1024]{1,0:T(1,128)S(1)}, f32[1,1024]{1,0:T(1,128)}, u32[]{:S(2)}) copy-start(f32[1,1024]{1,0:T(1,128)} %param.10) | copy-start | bytes 12292
  26.1 20.3 %collective-permute-start.4 = (bf16[128,1024]{1,0:T(8,128)(2,1)S(1)}, bf16[128,1024]{1,0:T(8,128)(2,1)S(1)}, u32[]{:S(2)}, u32[]{:S(2)}) collective-permute-start(bf16[128,1024]{1,0:T(8,128)(2,1)S(1)} %get-tuple-element.54), channel_id=1, source_target_pairs={{0,3},{1,2},{2,1},{3,0},{4,7},{5,6},{6,5},{7,4},{8,11},{9,10},{10,... | collective-permute-start | bytes 786440 | tf_op jit(solution)/shard_map/ppermute | solution.py:24
  27.8 34.6 %collective-permute-start.3 = (bf16[128,1024]{1,0:T(8,128)(2,1)S(1)}, bf16[128,1024]{1,0:T(8,128)(2,1)S(1)}, u32[]{:S(2)}, u32[]{:S(2)}) collective-permute-start(bf16[128,1024]{1,0:T(8,128)(2,1)S(1)} %get-tuple-element.55), channel_id=1, source_target_pairs={{0,2},{1,3},{2,0},{3,1},{4,6},{5,7},{6,4},{7,5},{8,10},{9,11},{10,... | collective-permute-start | bytes 786440 | tf_op jit(solution)/shard_map/ppermute | solution.py:24
  30.8 35.0 %collective-permute-start.2 = (bf16[128,1024]{1,0:T(8,128)(2,1)S(1)}, bf16[128,1024]{1,0:T(8,128)(2,1)S(1)}, u32[]{:S(2)}, u32[]{:S(2)}) collective-permute-start(bf16[128,1024]{1,0:T(8,128)(2,1)S(1)} %get-tuple-element.56), channel_id=1, source_target_pairs={{0,1},{1,0},{2,3},{3,2},{4,5},{5,4},{6,7},{7,6},{8,9},{9,8},{10,11... | collective-permute-start | bytes 786440 | tf_op jit(solution)/shard_map/ppermute | solution.py:24
  32.1 92.6 %collective-permute-start.6 = (bf16[128,2048]{1,0:T(8,128)(2,1)}, bf16[128,2048]{1,0:T(8,128)(2,1)S(1)}, u32[]{:S(2)}, u32[]{:S(2)}) collective-permute-start(bf16[128,2048]{1,0:T(8,128)(2,1)} %constant_dynamic-slice_fusion), channel_id=1, source_target_pairs={{0,2},{1,3},{2,0},{3,1},{4,6},{5,7},{6,4},{7,5},{8,10},{9,11},{10,... | collective-permute-start | bytes 1572872 | tf_op jit(solution)/shard_map/ppermute | solution.py:24
  35.1 90.2 %collective-permute-start.5 = (bf16[128,2048]{1,0:T(8,128)(2,1)}, bf16[128,2048]{1,0:T(8,128)(2,1)S(1)}, u32[]{:S(2)}, u32[]{:S(2)}) collective-permute-start(bf16[128,2048]{1,0:T(8,128)(2,1)} %constant_dynamic-slice_fusion.1), channel_id=1, source_target_pairs={{0,1},{1,0},{2,3},{3,2},{4,5},{5,4},{6,7},{7,6},{8,9},{9,8},{10,11... | collective-permute-start | bytes 1572872 | tf_op jit(solution)/shard_map/ppermute | solution.py:24
  46.4 22.0 %copy-start.2 = (bf16[128,1024]{1,0:T(8,128)(2,1)}, bf16[128,1024]{1,0:T(8,128)(2,1)S(1)}, u32[]{:S(2)}) copy-start(bf16[128,1024]{1,0:T(8,128)(2,1)S(1)} %collective-permute-done.4) | copy-start | bytes 786436
  46.4 78.8 %collective-permute-start.7 = (bf16[128,2048]{1,0:T(8,128)(2,1)}, bf16[128,2048]{1,0:T(8,128)(2,1)S(1)}, u32[]{:S(2)}, u32[]{:S(2)}) collective-permute-start(bf16[128,2048]{1,0:T(8,128)(2,1)} %constant_dynamic-slice_fusion.2), channel_id=1, source_target_pairs={{0,3},{1,2},{2,1},{3,0},{4,7},{5,6},{6,5},{7,4},{8,11},{9,10},{10,... | collective-permute-start | bytes 1572872 | tf_op jit(solution)/shard_map/ppermute | solution.py:24
  62.4 6.0 %copy-start.4 = (bf16[128,1024]{1,0:T(8,128)(2,1)}, bf16[128,1024]{1,0:T(8,128)(2,1)S(1)}, u32[]{:S(2)}) copy-start(bf16[128,1024]{1,0:T(8,128)(2,1)S(1)} %collective-permute-done.3) | copy-start | bytes 786436
  62.4 56.3 %collective-permute-start.9 = (bf16[128,2048]{1,0:T(8,128)(2,1)}, bf16[128,2048]{1,0:T(8,128)(2,1)S(1)}, u32[]{:S(2)}, u32[]{:S(2)}) collective-permute-start(bf16[128,2048]{1,0:T(8,128)(2,1)} %constant_dynamic-slice_fusion.3), channel_id=1, source_target_pairs={{0,2},{1,3},{2,0},{3,1},{4,6},{5,7},{6,4},{7,5},{8,10},{9,11},{10,... | collective-permute-start | bytes 1572872 | tf_op jit(solution)/shard_map/ppermute | solution.py:24
  65.8 2.6 %copy-start.6 = (bf16[128,1024]{1,0:T(8,128)(2,1)}, bf16[128,1024]{1,0:T(8,128)(2,1)S(1)}, u32[]{:S(2)}) copy-start(bf16[128,1024]{1,0:T(8,128)(2,1)S(1)} %collective-permute-done.2) | copy-start | bytes 786436
  65.8 52.9 %collective-permute-start.8 = (bf16[128,2048]{1,0:T(8,128)(2,1)}, bf16[128,2048]{1,0:T(8,128)(2,1)S(1)}, u32[]{:S(2)}, u32[]{:S(2)}) collective-permute-start(bf16[128,2048]{1,0:T(8,128)(2,1)} %constant_dynamic-slice_fusion.4), channel_id=1, source_target_pairs={{0,1},{1,0},{2,3},{3,2},{4,5},{5,4},{6,7},{7,6},{8,9},{9,8},{10,11... | collective-permute-start | bytes 1572872 | tf_op jit(solution)/shard_map/ppermute | solution.py:24
  69.2 1.8 copy-start.11
  71.4 0.9 copy-start.10
  72.3 0.8 copy-start.1
  77.3 1.8 copy-start.3
  77.3 1.8 copy-start.5
  77.3 1.8 copy-start.7
  79.1 39.7 %copy-start = (bf16[128,16384]{1,0:T(8,128)(2,1)S(1)}, bf16[128,16384]{1,0:T(8,128)(2,1)}, u32[]{:S(2)}) copy-start(bf16[128,16384]{1,0:T(8,128)(2,1)} %refs_0_.3) | copy-start | bytes 12582916
  121.4 25.3 %collective-permute-start.17 = (bf16[128,2048]{1,0:T(8,128)(2,1)S(1)}, bf16[128,2048]{1,0:T(8,128)(2,1)S(1)}, u32[]{:S(2)}, u32[]{:S(2)}) collective-permute-start(bf16[128,2048]{1,0:T(8,128)(2,1)S(1)} %get-tuple-element.48), channel_id=1, source_target_pairs={{0,1},{1,0},{2,3},{3,2},{4,5},{5,4},{6,7},{7,6},{8,9},{9,8},{10,11... | collective-permute-start | bytes 1572872 | tf_op jit(solution)/shard_map/ppermute | solution.py:24
  123.7 47.1 %collective-permute-start.18 = (bf16[128,2048]{1,0:T(8,128)(2,1)S(1)}, bf16[128,2048]{1,0:T(8,128)(2,1)S(1)}, u32[]{:S(2)}, u32[]{:S(2)}) collective-permute-start(bf16[128,2048]{1,0:T(8,128)(2,1)S(1)} %get-tuple-element.49), channel_id=1, source_target_pairs={{0,2},{1,3},{2,0},{3,1},{4,6},{5,7},{6,4},{7,5},{8,10},{9,11},{10,... | collective-permute-start | bytes 1572872 | tf_op jit(solution)/shard_map/ppermute | solution.py:24
  124.7 69.6 %collective-permute-start.16 = (bf16[128,2048]{1,0:T(8,128)(2,1)S(1)}, bf16[128,2048]{1,0:T(8,128)(2,1)S(1)}, u32[]{:S(2)}, u32[]{:S(2)}) collective-permute-start(bf16[128,2048]{1,0:T(8,128)(2,1)S(1)} %get-tuple-element.47), channel_id=1, source_target_pairs={{0,3},{1,2},{2,1},{3,0},{4,7},{5,6},{6,5},{7,4},{8,11},{9,10},{10,... | collective-permute-start | bytes 1572872 | tf_op jit(solution)/shard_map/ppermute | solution.py:24
  127.9 76.6 %collective-permute-start.15 = (bf16[128,2048]{1,0:T(8,128)(2,1)S(1)}, bf16[128,2048]{1,0:T(8,128)(2,1)S(1)}, u32[]{:S(2)}, u32[]{:S(2)}) collective-permute-start(bf16[128,2048]{1,0:T(8,128)(2,1)S(1)} %get-tuple-element.46), channel_id=1, source_target_pairs={{0,2},{1,3},{2,0},{3,1},{4,6},{5,7},{6,4},{7,5},{8,10},{9,11},{10,... | collective-permute-start | bytes 1572872 | tf_op jit(solution)/shard_map/ppermute | solution.py:24
  131.7 73.6 %collective-permute-start.14 = (bf16[128,2048]{1,0:T(8,128)(2,1)S(1)}, bf16[128,2048]{1,0:T(8,128)(2,1)S(1)}, u32[]{:S(2)}, u32[]{:S(2)}) collective-permute-start(bf16[128,2048]{1,0:T(8,128)(2,1)S(1)} %get-tuple-element.45), channel_id=1, source_target_pairs={{0,1},{1,0},{2,3},{3,2},{4,5},{5,4},{6,7},{7,6},{8,9},{9,8},{10,11... | collective-permute-start | bytes 1572872 | tf_op jit(solution)/shard_map/ppermute | solution.py:24
  146.7 67.3 %collective-permute-start.13 = (bf16[128,1536]{1,0:T(8,128)(2,1)S(1)}, bf16[128,1536]{1,0:T(8,128)(2,1)S(1)}, u32[]{:S(2)}, u32[]{:S(2)}) collective-permute-start(bf16[128,1536]{1,0:T(8,128)(2,1)S(1)} %slice.39), channel_id=1, source_target_pairs={{0,3},{1,2},{2,1},{3,0},{4,7},{5,6},{6,5},{7,4},{8,11},{9,10},{10,... | collective-permute-start | bytes 1179656 | tf_op jit(solution)/shard_map/ppermute | solution.py:24
  170.8 45.1 %collective-permute-start.12 = (bf16[128,512]{1,0:T(8,128)(2,1)S(1)}, bf16[128,512]{1,0:T(8,128)(2,1)S(1)}, u32[]{:S(2)}, u32[]{:S(2)}) collective-permute-start(bf16[128,512]{1,0:T(8,128)(2,1)S(1)} %slice.38), channel_id=1, source_target_pairs={{0,3},{1,2},{2,1},{3,0},{4,7},{5,6},{6,5},{7,4},{8,11},{9,10},{10,... | collective-permute-start | bytes 393224 | tf_op jit(solution)/shard_map/ppermute | solution.py:24
